TPU v7x, 256 devices: a whole 4x4x8 slice. The times are simulated.
256 devices in a mesh: seq: 16 (over y_lo, x, core), tp: 16 (over z, y_hi).
Axes of the slice: x: 4, y: 4 (y_hi: 2, y_lo: 2; y = y_hi * 2 + y_lo), z: 8, core: 2. Of those that a mesh axis runs over, the one named last changes fastest.
Arguments:
- tokens: bfloat16 [4096, 5376], P('seq', 'tp'), may hold values from -24 to 24
- w_query: bfloat16 [5376, 4096], P('seq', 'tp'), may hold values from -0.078125 to 0.078125
- w_key: bfloat16 [5376, 2048], P('seq', 'tp'), may hold values from -0.078125 to 0.078125
- w_value: bfloat16 [5376, 2048], P('seq', 'tp'), may hold values from -0.078125 to 0.078125
- w_out: bfloat16 [4096, 5376], P('tp', 'seq'), may hold values from -0.09375 to 0.09375
- cotangent: bfloat16 [4096, 5376], P('seq', 'tp'), may hold values from -6 to 6
- block_lists: int32 [32, 9], P('seq'), may hold values from -1 to 31, as said below
Outputs:
- grad_tokens: bfloat16 [4096, 5376], P('seq', 'tp')
- grad_query: bfloat16 [5376, 4096], P('seq', 'tp')
- grad_key: bfloat16 [5376, 2048], P('seq', 'tp')
- grad_value: bfloat16 [5376, 2048], P('seq', 'tp')
- grad_w_out: bfloat16 [4096, 5376], P('tp', 'seq')
Inputs may be any that keep to these rules, and one draw needn't show every extreme that they name: `block_lists`: entry k of query block b is b - 8 + k if that key block lies in the same document as block b, else -1. Documents are runs of whole blocks; the last entry of each row is b, and the valid entries of a row are its last ones.
All inputs are finite; a program needn't handle non-finite values.
Results may differ from a plain program's by a relative error of at most 0.025.
Values may be sent and summed in bfloat16 or wider, within the bound.
No kernel may reach another device: no remote copies, remote signals or barrier semaphores. Data moves between devices by JAX's collectives and lax.ppermute only.
A program may use at most 64 MiB of HBM per device.

v0:
```python
import jax
import jax.numpy as jnp
from jax import lax
from jax.sharding import PartitionSpec as P

HEADS = 32
KV_HEADS = 16
HD = 128
WIN = 1024
ATTN_SCALAR = 168


def from_behind(block, axis, distance):
    devices = range(lax.axis_size(axis))
    route = [(i - distance, i) for i in devices if i - distance in devices]
    return lax.ppermute(block, axis, route)


def window_view(blocks, n_blocks, span):
    return jnp.concatenate([blocks[offset : offset + n_blocks] for offset in range(span)], axis=1)


def fold_windows(windows, n_blocks, span, block_len):
    shaped = windows.reshape(n_blocks, span, block_len, windows.shape[2], windows.shape[3])
    summed = jnp.zeros(
        (n_blocks + span - 1, block_len, windows.shape[2], windows.shape[3]), jnp.float32
    )
    for offset in range(span):
        summed = summed.at[offset : offset + n_blocks].add(shaped[:, offset])
    return summed.reshape((n_blocks + span - 1) * block_len, windows.shape[2] * windows.shape[3])


def local_attention(query, keys, values, d_attn, block_lists, softmax_scale):
    tok_rows, kv_local, group_size, head_dim = query.shape
    n_blocks, span = block_lists.shape
    block_len = tok_rows // n_blocks
    width = span * block_len
    key_blocks = keys.reshape(n_blocks + span - 1, block_len, kv_local, head_dim)
    val_blocks = values.reshape(n_blocks + span - 1, block_len, kv_local, head_dim)
    key_win = window_view(key_blocks, n_blocks, span)
    val_win = window_view(val_blocks, n_blocks, span)
    q_blocks = query.reshape(n_blocks, block_len, kv_local, group_size, head_dim)
    grad_blocks = d_attn.reshape(n_blocks, block_len, kv_local, group_size, head_dim)
    scores = (
        jnp.einsum("btkgd,bwkd->bkgtw", q_blocks, key_win, preferred_element_type=jnp.float32)
        * softmax_scale
    )
    rows_at = jnp.arange(block_len)[:, None]
    cols_at = jnp.arange(width)[None, :]
    inside = (cols_at > rows_at) & (cols_at <= rows_at + (width - block_len))
    listed = jnp.repeat(block_lists >= 0, block_len, axis=1)
    allowed = inside[None, None, None] & listed[:, None, None, None, :]
    masked = jnp.where(allowed, scores, -1e30)
    highest = jnp.max(masked, axis=-1, keepdims=True)
    weights = jnp.where(allowed, jnp.exp(masked - highest), 0.0)
    probs = weights / jnp.sum(weights, axis=-1, keepdims=True)
    probs_half = probs.astype(jnp.bfloat16)
    attn = jnp.einsum(
        "bkgtw,bwkd->btkgd", probs_half, val_win, preferred_element_type=jnp.float32
    ).astype(jnp.bfloat16)
    delta = jnp.sum(grad_blocks.astype(jnp.float32) * attn.astype(jnp.float32), axis=-1)
    delta = jnp.transpose(delta, (0, 2, 3, 1))[..., None]
    grad_probs = jnp.einsum(
        "btkgd,bwkd->bkgtw", grad_blocks, val_win, preferred_element_type=jnp.float32
    )
    grad_scores = (probs * (grad_probs - delta)).astype(jnp.bfloat16)
    grad_q = (
        jnp.einsum("bkgtw,bwkd->btkgd", grad_scores, key_win, preferred_element_type=jnp.float32)
        * softmax_scale
    ).astype(jnp.bfloat16)
    grad_kwin = (
        jnp.einsum("bkgtw,btkgd->bwkd", grad_scores, q_blocks, preferred_element_type=jnp.float32)
        * softmax_scale
    )
    grad_vwin = jnp.einsum(
        "bkgtw,btkgd->bwkd", probs_half, grad_blocks, preferred_element_type=jnp.float32
    )
    grad_keys = fold_windows(grad_kwin, n_blocks, span, block_len)
    grad_values = fold_windows(grad_vwin, n_blocks, span, block_len)
    flat = kv_local * group_size * head_dim
    return (attn.reshape(tok_rows, flat), grad_q.reshape(tok_rows, flat), grad_keys, grad_values)


def contract_cols(left, right):
    return lax.dot_general(
        left, right, (((1,), (1,)), ((), ())), preferred_element_type=jnp.float32
    )


def term_maker(left, right):
    return lax.dot_general(
        left, right, (((0,), (0,)), ((), ())), preferred_element_type=jnp.float32
    )


def shards(tokens, w_query, w_key, w_value, w_out, cotangent, block_lists):
    softmax_scale = ATTN_SCALAR ** (-0.5)
    group_size = HEADS // KV_HEADS
    head_dim = HD
    tok_rows = tokens.shape[0]
    reach = WIN // tok_rows
    full_tokens, full_cot = (
        lax.all_gather(tokens, "tp", axis=1, tiled=True),
        lax.all_gather(cotangent, "tp", axis=1, tiled=True),
    )
    query_full, key_full, value_full = (
        lax.all_gather(w_query, "seq", axis=0, tiled=True),
        lax.all_gather(w_key, "seq", axis=0, tiled=True),
        lax.all_gather(w_value, "seq", axis=0, tiled=True),
    )
    d_attn = contract_cols(full_cot, lax.all_gather(w_out, "seq", axis=1, tiled=True)).astype(
        jnp.bfloat16
    )
    query = jnp.dot(full_tokens, query_full, preferred_element_type=jnp.float32).astype(
        jnp.bfloat16
    )
    keys = jnp.dot(full_tokens, key_full, preferred_element_type=jnp.float32).astype(jnp.bfloat16)
    values = jnp.dot(full_tokens, value_full, preferred_element_type=jnp.float32).astype(
        jnp.bfloat16
    )
    earlier = [from_behind((keys, values), "seq", distance) for distance in range(reach, 0, -1)]
    key_ext = jnp.concatenate([member[0] for member in earlier] + [keys], axis=0)
    value_ext = jnp.concatenate([member[1] for member in earlier] + [values], axis=0)
    kv_local = keys.shape[1] // head_dim
    attn, grad_q, grad_k_ext, grad_v_ext = local_attention(
        query.reshape(tok_rows, kv_local, group_size, head_dim),
        key_ext.reshape(-1, kv_local, head_dim),
        value_ext.reshape(-1, kv_local, head_dim),
        d_attn.reshape(tok_rows, kv_local, group_size, head_dim),
        block_lists,
        softmax_scale,
    )

    def segment(array, index):
        return array[index * tok_rows : (index + 1) * tok_rows]

    summed_k = segment(grad_k_ext, reach)
    summed_v = segment(grad_v_ext, reach)
    for distance in range(1, reach + 1):
        back_k, back_v = from_behind(
            (segment(grad_k_ext, reach - distance), segment(grad_v_ext, reach - distance)),
            "seq",
            -distance,
        )
        summed_k = summed_k + back_k
        summed_v = summed_v + back_v
    grad_k = summed_k.astype(jnp.bfloat16)
    grad_v = summed_v.astype(jnp.bfloat16)
    token_term = (
        contract_cols(grad_q, query_full)
        + contract_cols(grad_k, key_full)
        + contract_cols(grad_v, value_full)
    )
    grad_tokens = lax.psum_scatter(token_term, "tp", scatter_dimension=1, tiled=True).astype(
        jnp.bfloat16
    )
    operand_pairs = (
        (full_tokens, grad_q),
        (full_tokens, grad_k),
        (full_tokens, grad_v),
        (full_cot, attn),
    )

    def reduce_rows(left, right):
        return lax.psum_scatter(
            term_maker(left, right).astype(jnp.bfloat16), "seq", scatter_dimension=0, tiled=True
        ).astype(jnp.float32)

    results = [reduce_rows(left, right) for left, right in operand_pairs]
    grad_query = results[0].astype(jnp.bfloat16)
    grad_key = results[1].astype(jnp.bfloat16)
    grad_value = results[2].astype(jnp.bfloat16)
    grad_w_out = results[3].T.astype(jnp.bfloat16)
    return (grad_tokens, grad_query, grad_key, grad_value, grad_w_out)


def solution(mesh):
    in_specs = (
        P("seq", "tp"),
        P("seq", "tp"),
        P("seq", "tp"),
        P("seq", "tp"),
        P("tp", "seq"),
        P("seq", "tp"),
        P("seq", None),
    )
    out_specs = (P("seq", "tp"), P("seq", "tp"), P("seq", "tp"), P("seq", "tp"), P("tp", "seq"))
    return jax.shard_map(shards, mesh=mesh, in_specs=in_specs, out_specs=out_specs, check_vma=False)
```

profile of v0, /device:TPU:128, one launch (start us, length us, event | category | flops | bytes accessed | tf_op | source)
XLA Modules:
  0.0 932.2 jit_solution(3593583309488818795)
XLA Ops:
  12.6 33.9 %all-gather.9.cloned.1.call-done = bf16[5376,128]{1,0:T(8,128)(2,1)} async-done(((bf16[336,128]{1,0:T(8,128)(2,1)}), bf16[5376,128]{1,0:T(8,128)(2,1)}) %all-gather.9.cloned.1.call-update) | async-done | bytes 1376272 | tf_op jit(solution)/shard_map/all_gather | solution.py:108
  46.5 89.9 %all-gather.7.cloned.1.call-done = bf16[256,5376]{0,1:T(8,128)(2,1)} async-done(((bf16[256,336]{0,1:T(8,128)(2,1)}), bf16[256,5376]{0,1:T(8,128)(2,1)}) %all-gather.7.cloned.1.call-update) | async-done | bytes 2752528 | tf_op jit(solution)/shard_map/all_gather | solution.py:103
  136.4 3.2 convolution_convert_fusion.7
  139.6 5.5 collective-permute-start
  145.1 1.9 collective-permute-start.1
  147.0 3.1 collective-permute-start.2
  150.1 3.3 collective-permute-start.3
  153.3 21.7 %all-gather.11.cloned.1.call-done = bf16[5376,256]{1,0:T(8,128)(2,1)} async-done(((bf16[336,256]{1,0:T(8,128)(2,1)}), bf16[5376,256]{1,0:T(8,128)(2,1)}) %all-gather.11.cloned.1.call-update) | async-done | bytes 2752528 | tf_op jit(solution)/shard_map/all_gather | solution.py:107
  175.1 3.4 convolution_convert_fusion.5
  178.4 86.4 %all-gather.15.cloned.1.call-done = bf16[256,5376]{0,1:T(8,128)(2,1)} async-done(((bf16[256,336]{0,1:T(8,128)(2,1)}), bf16[256,5376]{0,1:T(8,128)(2,1)}) %all-gather.15.cloned.1.call-update) | async-done | bytes 2752528 | tf_op jit(solution)/shard_map/all_gather | solution.py:104
  264.9 38.5 %all-gather.17.cloned.1.call-done = bf16[256,5376]{0,1:T(8,128)(2,1)} async-done(((bf16[256,336]{0,1:T(8,128)(2,1)}), bf16[256,5376]{0,1:T(8,128)(2,1)}) %all-gather.17.cloned.1.call-update) | async-done | bytes 2752528 | tf_op jit(solution)/shard_map/all_gather | solution.py:111
  303.4 3.5 convolution_convert_fusion.4
  306.9 33.5 %all-gather.13.cloned.1.call-done = bf16[5376,128]{1,0:T(8,128)(2,1)} async-done(((bf16[336,128]{1,0:T(8,128)(2,1)}), bf16[5376,128]{1,0:T(8,128)(2,1)}) %all-gather.13.cloned.1.call-update) | async-done | bytes 1376272 | tf_op jit(solution)/shard_map/all_gather | solution.py:109
  340.5 2.3 convolution_convert_fusion.6
  343.4 1.0 reshape.830
  344.5 1.6 reshape.805
  346.1 1.7 copy.86
  347.7 1.7 copy.97
  349.4 4.0 collective-permute-start.4
  354.2 2.0 collective-permute-start.5
  357.1 3.5 collective-permute-start.6
  360.6 3.0 collective-permute-start.7
  367.1 1.4 fusion.79
  369.0 1.8 convolution_bitcast_fusion.1
  372.7 1.5 fusion.11
  374.6 2.7 copy.99
  379.2 0.9 fusion.53
  380.2 0.9 fusion.51
  381.1 0.9 fusion.49
  382.1 0.9 fusion.47
  384.9 1.7 fusion.41
  386.6 1.3 collective-permute-start.12
  387.9 2.7 copy.88
  394.4 0.9 fusion.62
  395.3 0.9 fusion.60
  398.2 1.7 fusion.54
  399.9 1.3 collective-permute-start.10
  401.2 1.3 collective-permute-start.11
  402.5 1.3 collective-permute-start.8
  403.8 1.5 collective-permute-start.9
  405.4 2.8 fusion.39
  408.3 1.3 collective-permute-start.13
  409.6 2.9 collective-permute-done.11
  412.5 1.3 collective-permute-start.14
  413.8 1.3 collective-permute-start.15
  415.1 1.1 fusion.74
  417.2 1.4 collective-permute-done.13
  418.5 1.4 collective-permute-done.14
  419.9 5.3 collective-permute-done.15
  425.3 3.3 convolution_add_fusion
  428.6 2.2 fusion.3
  430.8 2.5 copy.131
  433.4 2.2 fusion.2
  435.6 2.5 copy.129
  438.2 2.6 fusion
  440.7 4.5 copy.127
  445.5 2.8 fusion.1
  448.3 2.9 copy.133
  451.2 200.6 %reduce-scatter.14.cloned.1.call-done = f32[256,336]{0,1:T(8,128)} async-done(((f32[256,5376]{0,1:T(8,128)}), f32[256,336]{0,1:T(8,128)}) %reduce-scatter.14.cloned.1.call-update) | async-done | bytes 344080 | tf_op jit(solution)/shard_map/reduce_scatter | solution.py:154
  651.8 1.7 convert_element_type.114
  653.5 66.4 %reduce-scatter.20.cloned.1.call-done = bf16[336,128]{1,0:T(8,128)(2,1)} async-done(((bf16[5376,128]{1,0:T(8,128)(2,1)}), bf16[336,128]{1,0:T(8,128)(2,1)}) %reduce-scatter.20.cloned.1.call-update) | async-done | bytes 86032
  719.9 67.3 %reduce-scatter.18.cloned.1.call-done = bf16[336,128]{1,0:T(8,128)(2,1)} async-done(((bf16[5376,128]{1,0:T(8,128)(2,1)}), bf16[336,128]{1,0:T(8,128)(2,1)}) %reduce-scatter.18.cloned.1.call-update) | async-done | bytes 86032
  787.1 69.2 %reduce-scatter.16.cloned.1.call-done = bf16[336,256]{1,0:T(8,128)(2,1)} async-done(((bf16[5376,256]{1,0:T(8,128)(2,1)}), bf16[336,256]{1,0:T(8,128)(2,1)}) %reduce-scatter.16.cloned.1.call-update) | async-done | bytes 172048
  856.3 69.3 %reduce-scatter.22.cloned.1.call-done = bf16[336,256]{1,0:T(8,128)(2,1)} async-done(((bf16[5376,256]{1,0:T(8,128)(2,1)}), bf16[336,256]{1,0:T(8,128)(2,1)}) %reduce-scatter.22.cloned.1.call-update) | async-done | bytes 172048
  (102 shorter events, 24.8 us)
Async XLA Ops:
  7.2 39.3 %all-gather.9.cloned.1.call-start = ((), (), s32[]{:S(2)}) async-start(), calls=%async_computation.6 | async-start | bytes 1462272 | tf_op jit(solution)/shard_map/all_gather | solution.py:108
  7.9 128.5 %all-gather.7.cloned.1.call-start = ((), (), s32[]{:S(2)}) async-start(), calls=%async_computation.5 | async-start | bytes 2924544 | tf_op jit(solution)/shard_map/all_gather | solution.py:103
  8.6 166.4 %all-gather.11.cloned.1.call-start = ((), (), s32[]{:S(2)}) async-start(), calls=%async_computation.7 | async-start | bytes 2924544 | tf_op jit(solution)/shard_map/all_gather | solution.py:107
  9.4 255.5 %all-gather.15.cloned.1.call-start = ((), (), s32[]{:S(2)}) async-start(), calls=%async_computation.9 | async-start | bytes 2924544 | tf_op jit(solution)/shard_map/all_gather | solution.py:104
  10.0 293.4 %all-gather.17.cloned.1.call-start = ((), (), s32[]{:S(2)}) async-start(), calls=%async_computation.10 | async-start | bytes 2924544 | tf_op jit(solution)/shard_map/all_gather | solution.py:111
  10.5 329.9 %all-gather.13.cloned.1.call-start = ((), (), s32[]{:S(2)}) async-start(), calls=%async_computation.8 | async-start | bytes 1462272 | tf_op jit(solution)/shard_map/all_gather | solution.py:109
  11.1 640.7 %reduce-scatter.14.cloned.1.call-start = ((), (), s32[]{:S(2)}) async-start(), calls=%async_computation.11 | async-start | bytes 5849088 | tf_op jit(solution)/shard_map/reduce_scatter | solution.py:154
  136.4 38.7 %copy-start = (bf16[256,5376]{0,1:T(8,128)(2,1)S(1)}, bf16[256,5376]{0,1:T(8,128)(2,1)}, u32[]{:S(2)}) copy-start(bf16[256,5376]{0,1:T(8,128)(2,1)} %all-gather.7.cloned.1.call-done) | copy-start | bytes 8257540
  139.6 214.6 %collective-permute-start = (bf16[256,128]{1,0:T(8,128)(2,1)S(1)}, bf16[256,128]{1,0:T(8,128)(2,1)}, u32[]{:S(2)}, u32[]{:S(2)}) collective-permute-start(bf16[256,128]{1,0:T(8,128)(2,1)S(1)} %convolution_convert_fusion.7), channel_id=1, source_target_pairs={{0,64},{16,80},{32,96},{48,112},{64,128},{80,144},{96,160},{112,17... | collective-permute-start | bytes 196616 | tf_op jit(solution)/shard_map/ppermute | solution.py:16
  145.1 212.0 %collective-permute-start.1 = (bf16[256,128]{1,0:T(8,128)(2,1)S(1)}, bf16[256,128]{1,0:T(8,128)(2,1)}, u32[]{:S(2)}, u32[]{:S(2)}) collective-permute-start(bf16[256,128]{1,0:T(8,128)(2,1)S(1)} %convolution_convert_fusion.7), channel_id=1, source_target_pairs={{0,48},{16,64},{32,80},{48,96},{64,112},{80,128},{96,144},{112,160... | collective-permute-start | bytes 196616 | tf_op jit(solution)/shard_map/ppermute | solution.py:16
  147.0 213.5 %collective-permute-start.2 = (bf16[256,128]{1,0:T(8,128)(2,1)S(1)}, bf16[256,128]{1,0:T(8,128)(2,1)}, u32[]{:S(2)}, u32[]{:S(2)}) collective-permute-start(bf16[256,128]{1,0:T(8,128)(2,1)S(1)} %convolution_convert_fusion.7), channel_id=1, source_target_pairs={{0,32},{16,48},{32,64},{48,80},{64,96},{80,112},{96,128},{112,144}... | collective-permute-start | bytes 196616 | tf_op jit(solution)/shard_map/ppermute | solution.py:16
  150.1 213.5 %collective-permute-start.3 = (bf16[256,128]{1,0:T(8,128)(2,1)S(1)}, bf16[256,128]{1,0:T(8,128)(2,1)}, u32[]{:S(2)}, u32[]{:S(2)}) collective-permute-start(bf16[256,128]{1,0:T(8,128)(2,1)S(1)} %convolution_convert_fusion.7), channel_id=1, source_target_pairs={{0,16},{16,32},{32,48},{48,64},{64,80},{80,96},{96,112},{112,128},... | collective-permute-start | bytes 196616 | tf_op jit(solution)/shard_map/ppermute | solution.py:16
  306.9 35.8 %copy-start.4 = (bf16[256,256]{1,0:T(8,128)(2,1)}, bf16[256,256]{1,0:T(8,128)(2,1)S(1)}, u32[]{:S(2)}) copy-start(bf16[256,256]{1,0:T(8,128)(2,1)S(1)} %convolution_convert_fusion.4) | copy-start | bytes 393220
  349.4 21.4 %collective-permute-start.4 = (bf16[256,128]{1,0:T(8,128)(2,1)S(1)}, bf16[256,128]{1,0:T(8,128)(2,1)S(1)}, u32[]{:S(2)}, u32[]{:S(2)}) collective-permute-start(bf16[256,128]{1,0:T(8,128)(2,1)S(1)} %convolution_convert_fusion.6), channel_id=1, source_target_pairs={{0,64},{16,80},{32,96},{48,112},{64,128},{80,144},{96,160},{112,17... | collective-permute-start | bytes 196616 | tf_op jit(solution)/shard_map/ppermute | solution.py:16
  354.2 16.6 %collective-permute-start.5 = (bf16[256,128]{1,0:T(8,128)(2,1)S(1)}, bf16[256,128]{1,0:T(8,128)(2,1)S(1)}, u32[]{:S(2)}, u32[]{:S(2)}) collective-permute-start(bf16[256,128]{1,0:T(8,128)(2,1)S(1)} %convolution_convert_fusion.6), channel_id=1, source_target_pairs={{0,48},{16,64},{32,80},{48,96},{64,112},{80,128},{96,144},{112,160... | collective-permute-start | bytes 196616 | tf_op jit(solution)/shard_map/ppermute | solution.py:16
  357.1 13.8 %collective-permute-start.6 = (bf16[256,128]{1,0:T(8,128)(2,1)S(1)}, bf16[256,128]{1,0:T(8,128)(2,1)S(1)}, u32[]{:S(2)}, u32[]{:S(2)}) collective-permute-start(bf16[256,128]{1,0:T(8,128)(2,1)S(1)} %convolution_convert_fusion.6), channel_id=1, source_target_pairs={{0,32},{16,48},{32,64},{48,80},{64,96},{80,112},{96,128},{112,144}... | collective-permute-start | bytes 196616 | tf_op jit(solution)/shard_map/ppermute | solution.py:16
  360.6 10.3 %collective-permute-start.7 = (bf16[256,128]{1,0:T(8,128)(2,1)S(1)}, bf16[256,128]{1,0:T(8,128)(2,1)S(1)}, u32[]{:S(2)}, u32[]{:S(2)}) collective-permute-start(bf16[256,128]{1,0:T(8,128)(2,1)S(1)} %convolution_convert_fusion.6), channel_id=1, source_target_pairs={{0,16},{16,32},{32,48},{48,64},{64,80},{80,96},{96,112},{112,128},... | collective-permute-start | bytes 196616 | tf_op jit(solution)/shard_map/ppermute | solution.py:16
  367.1 1.9 copy-start.6
  369.0 2.0 copy-start.5
  371.8 0.9 copy-start.3
  386.6 30.5 %collective-permute-start.12 = (f32[256,128]{1,0:T(8,128)}, f32[256,128]{1,0:T(8,128)S(1)}, u32[]{:S(2)}, u32[]{:S(2)}) collective-permute-start(f32[256,128]{1,0:T(8,128)} %bitcast.73), channel_id=1, source_target_pairs={{16,0},{32,16},{48,32},{64,48},{80,64},{96,80},{112,96},{128,112},... | collective-permute-start | bytes 393224 | tf_op jit(solution)/shard_map/ppermute | solution.py:16
  399.9 8.4 collective-permute-start.10
  401.2 11.3 %collective-permute-start.11 = (f32[256,128]{1,0:T(8,128)}, f32[256,128]{1,0:T(8,128)}, u32[]{:S(2)}, u32[]{:S(2)}) collective-permute-start(f32[256,128]{1,0:T(8,128)} %bitcast.57), channel_id=1, source_target_pairs={{64,0},{80,16},{96,32},{112,48},{128,64},{144,80},{160,96},{176,11... | collective-permute-start | bytes 393224 | tf_op jit(solution)/shard_map/ppermute | solution.py:16
  402.5 11.3 %collective-permute-start.8 = (f32[256,128]{1,0:T(8,128)}, f32[256,128]{1,0:T(8,128)}, u32[]{:S(2)}, u32[]{:S(2)}) collective-permute-start(f32[256,128]{1,0:T(8,128)} %bitcast.54), channel_id=1, source_target_pairs={{16,0},{32,16},{48,32},{64,48},{80,64},{96,80},{112,96},{128,112},... | collective-permute-start | bytes 393224 | tf_op jit(solution)/shard_map/ppermute | solution.py:16
  403.8 11.3 %collective-permute-start.9 = (f32[256,128]{1,0:T(8,128)}, f32[256,128]{1,0:T(8,128)}, u32[]{:S(2)}, u32[]{:S(2)}) collective-permute-start(f32[256,128]{1,0:T(8,128)} %bitcast.55), channel_id=1, source_target_pairs={{32,0},{48,16},{64,32},{80,48},{96,64},{112,80},{128,96},{144,112}... | collective-permute-start | bytes 393224 | tf_op jit(solution)/shard_map/ppermute | solution.py:16
  405.4 2.9 copy-start.9
  405.4 7.1 copy-start.8
  405.4 8.4 copy-start.7
  405.4 10.8 %copy-start.1 = (bf16[5376,128]{1,0:T(8,128)(2,1)S(1)}, bf16[5376,128]{1,0:T(8,128)(2,1)}, u32[]{:S(2)}) copy-start(bf16[5376,128]{1,0:T(8,128)(2,1)} %all-gather.9.cloned.1.call-done) | copy-start | bytes 4128772
  408.3 10.2 %collective-permute-start.13 = (f32[256,128]{1,0:T(8,128)S(1)}, f32[256,128]{1,0:T(8,128)S(1)}, u32[]{:S(2)}, u32[]{:S(2)}) collective-permute-start(f32[256,128]{1,0:T(8,128)S(1)} %bitcast.356), channel_id=1, source_target_pairs={{32,0},{48,16},{64,32},{80,48},{96,64},{112,80},{128,96},{144,112}... | collective-permute-start | bytes 393224 | tf_op jit(solution)/shard_map/ppermute | solution.py:16
  412.5 7.4 collective-permute-start.14
  413.8 11.4 %collective-permute-start.15 = (f32[256,128]{1,0:T(8,128)S(1)}, f32[256,128]{1,0:T(8,128)S(1)}, u32[]{:S(2)}, u32[]{:S(2)}) collective-permute-start(f32[256,128]{1,0:T(8,128)S(1)} %bitcast.354), channel_id=1, source_target_pairs={{64,0},{80,16},{96,32},{112,48},{128,64},{144,80},{160,96},{176,11... | collective-permute-start | bytes 393224 | tf_op jit(solution)/shard_map/ppermute | solution.py:16
  416.3 9.0 copy-start.2
  428.6 291.3 %reduce-scatter.20.cloned.1.call-start = ((), (), s32[]{:S(2)}) async-start(), calls=%async_computation.14 | async-start | bytes 1462272
  433.4 353.8 %reduce-scatter.18.cloned.1.call-start = ((), (), s32[]{:S(2)}) async-start(), calls=%async_computation.13 | async-start | bytes 1462272
  438.1 418.2 %reduce-scatter.16.cloned.1.call-start = ((), (), s32[]{:S(2)}) async-start(), calls=%async_computation.12 | async-start | bytes 2924544
  445.3 480.4 %reduce-scatter.22.cloned.1.call-start = ((), (), s32[]{:S(2)}) async-start(), calls=%async_computation.15 | async-start | bytes 2924544
Sparse Core Ops, SparseCore 0:
  9.8 36.6 all-gather.8
  49.1 87.2 all-gather.6
  138.2 36.8 all-gather.10
  177.5 87.2 all-gather.14
  266.5 36.8 all-gather.16
  305.1 35.3 all-gather.12
  428.7 223.0 reduce-scatter.13
  654.9 64.8 reduce-scatter.19
  723.0 64.1 reduce-scatter.17
  790.1 66.1 reduce-scatter.15
  859.5 66.1 reduce-scatter.21
where the time goes:
time: 935 us; the launch traced here: 932 us
  waiting for transfers between devices  791 us (85%)
  starting transfers between devices  37.1 us (4%)
  matrix products  35.7 us (4%)
  local copies, waits for them, and re-layouts  31.4 us (3%)
  other arithmetic  22.1 us (2%)
  between operations  14.4 us (2%)
    unnamed x15, waiting for transfers between devices  276 us
    reduce_scatter x1, waiting for transfers between devices, shards(): lax.psum_scatter(token_term, 'tp', scatter_dimension=1, tiled=True)  201 us
    all_gather x1, waiting for transfers between devices, shards(): lax.all_gather(tokens, 'tp', axis=1, tiled=True)  89.9 us
    all_gather x1, waiting for transfers between devices, shards(): lax.all_gather(cotangent, 'tp', axis=1, tiled=True)  86.4 us
    all_gather x1, waiting for transfers between devices, shards(): lax.all_gather(w_out, 'seq', axis=1, tiled=True)  38.5 us
    ppermute x16, starting transfers between devices, from_behind(): return lax.ppermute(block, axis, route)  36.6 us
    all_gather x1, waiting for transfers between devices, shards(): lax.all_gather(w_key, 'seq', axis=0, tiled=True)  33.9 us
    all_gather x1, waiting for transfers between devices, shards(): lax.all_gather(w_value, 'seq', axis=0, tiled=True)  33.5 us
  transfers between devices with their start and end apart: 27, of which 15 were waited for; matrix products, arithmetic and copies ran while one was open for 8% of the time, Pallas kernels for 0%

commit v1 on v0

--- a/solution.py
+++ b/solution.py
@@ -1,6 +1,7 @@
 import jax
 import jax.numpy as jnp
 from jax import lax
+from jax.sharding import Mesh
 from jax.sharding import PartitionSpec as P
 
 HEADS = 32
@@ -9,9 +10,14 @@
 WIN = 1024
 ATTN_SCALAR = 168
 
+SEQ = ("ylo", "x", "core")
+TP = ("z", "yhi")
+SEQ_SPLIT = (2, 4, 2)
+TP_SPLIT = (8, 2)
+
 
 def from_behind(block, axis, distance):
-    devices = range(lax.axis_size(axis))
+    devices = range(lax.psum(1, axis))
     route = [(i - distance, i) for i in devices if i - distance in devices]
     return lax.ppermute(block, axis, route)
 
@@ -99,26 +105,24 @@
     head_dim = HD
     tok_rows = tokens.shape[0]
     reach = WIN // tok_rows
-    full_tokens, full_cot = (
-        lax.all_gather(tokens, "tp", axis=1, tiled=True),
-        lax.all_gather(cotangent, "tp", axis=1, tiled=True),
-    )
-    query_full, key_full, value_full = (
-        lax.all_gather(w_query, "seq", axis=0, tiled=True),
-        lax.all_gather(w_key, "seq", axis=0, tiled=True),
-        lax.all_gather(w_value, "seq", axis=0, tiled=True),
-    )
-    d_attn = contract_cols(full_cot, lax.all_gather(w_out, "seq", axis=1, tiled=True)).astype(
+    n_q = w_query.shape[1]
+    n_kv = w_key.shape[1]
+    n_proj = n_q + 2 * n_kv
+    pair = jnp.stack([tokens, cotangent])
+    pair = lax.all_gather(pair, "yhi", axis=2, tiled=True)
+    pair = lax.all_gather(pair, "z", axis=2, tiled=True)
+    full_tokens, full_cot = pair[0], pair[1]
+    w_cat = jnp.concatenate([w_query, w_key, w_value, w_out.T], axis=1)
+    w_full = lax.all_gather(w_cat, SEQ, axis=0, tiled=True)
+    proj_full = w_full[:, :n_proj]
+    d_attn = jnp.dot(full_cot, w_full[:, n_proj:], preferred_element_type=jnp.float32).astype(
         jnp.bfloat16
     )
-    query = jnp.dot(full_tokens, query_full, preferred_element_type=jnp.float32).astype(
-        jnp.bfloat16
-    )
-    keys = jnp.dot(full_tokens, key_full, preferred_element_type=jnp.float32).astype(jnp.bfloat16)
-    values = jnp.dot(full_tokens, value_full, preferred_element_type=jnp.float32).astype(
-        jnp.bfloat16
-    )
-    earlier = [from_behind((keys, values), "seq", distance) for distance in range(reach, 0, -1)]
+    qkv = jnp.dot(full_tokens, proj_full, preferred_element_type=jnp.float32).astype(jnp.bfloat16)
+    query = qkv[:, :n_q]
+    keys = qkv[:, n_q : n_q + n_kv]
+    values = qkv[:, n_q + n_kv :]
+    earlier = [from_behind((keys, values), SEQ, distance) for distance in range(reach, 0, -1)]
     key_ext = jnp.concatenate([member[0] for member in earlier] + [keys], axis=0)
     value_ext = jnp.concatenate([member[1] for member in earlier] + [values], axis=0)
     kv_local = keys.shape[1] // head_dim
@@ -139,50 +143,44 @@
     for distance in range(1, reach + 1):
         back_k, back_v = from_behind(
             (segment(grad_k_ext, reach - distance), segment(grad_v_ext, reach - distance)),
-            "seq",
+            SEQ,
             -distance,
         )
         summed_k = summed_k + back_k
         summed_v = summed_v + back_v
     grad_k = summed_k.astype(jnp.bfloat16)
     grad_v = summed_v.astype(jnp.bfloat16)
-    token_term = (
-        contract_cols(grad_q, query_full)
-        + contract_cols(grad_k, key_full)
-        + contract_cols(grad_v, value_full)
+    grad_act = jnp.concatenate([grad_q, grad_k, grad_v], axis=1)
+    token_term = contract_cols(grad_act, proj_full).astype(jnp.bfloat16)
+    n_tp = lax.psum(1, TP)
+    cols = token_term.shape[1] // n_tp
+    parts = lax.all_to_all(token_term.reshape(tok_rows, n_tp, cols), TP, 1, 1, tiled=True)
+    grad_tokens = parts.astype(jnp.float32).sum(axis=1).astype(jnp.bfloat16)
+    weight_terms = jnp.concatenate(
+        [
+            term_maker(full_tokens, grad_act).astype(jnp.bfloat16),
+            term_maker(full_cot, attn).astype(jnp.bfloat16),
+        ],
+        axis=1,
     )
-    grad_tokens = lax.psum_scatter(token_term, "tp", scatter_dimension=1, tiled=True).astype(
-        jnp.bfloat16
-    )
-    operand_pairs = (
-        (full_tokens, grad_q),
-        (full_tokens, grad_k),
-        (full_tokens, grad_v),
-        (full_cot, attn),
-    )
-
-    def reduce_rows(left, right):
-        return lax.psum_scatter(
-            term_maker(left, right).astype(jnp.bfloat16), "seq", scatter_dimension=0, tiled=True
-        ).astype(jnp.float32)
-
-    results = [reduce_rows(left, right) for left, right in operand_pairs]
-    grad_query = results[0].astype(jnp.bfloat16)
-    grad_key = results[1].astype(jnp.bfloat16)
-    grad_value = results[2].astype(jnp.bfloat16)
-    grad_w_out = results[3].T.astype(jnp.bfloat16)
+    summed = lax.psum_scatter(weight_terms, SEQ, scatter_dimension=0, tiled=True)
+    grad_query = summed[:, :n_q]
+    grad_key = summed[:, n_q : n_q + n_kv]
+    grad_value = summed[:, n_q + n_kv : n_proj]
+    grad_w_out = summed[:, n_proj:].T
     return (grad_tokens, grad_query, grad_key, grad_value, grad_w_out)
 
 
 def solution(mesh):
+    fine = Mesh(mesh.devices.reshape(SEQ_SPLIT + TP_SPLIT), SEQ + TP)
     in_specs = (
-        P("seq", "tp"),
-        P("seq", "tp"),
-        P("seq", "tp"),
-        P("seq", "tp"),
-        P("tp", "seq"),
-        P("seq", "tp"),
-        P("seq", None),
+        P(SEQ, TP),
+        P(SEQ, TP),
+        P(SEQ, TP),
+        P(SEQ, TP),
+        P(TP, SEQ),
+        P(SEQ, TP),
+        P(SEQ, None),
     )
-    out_specs = (P("seq", "tp"), P("seq", "tp"), P("seq", "tp"), P("seq", "tp"), P("tp", "seq"))
-    return jax.shard_map(shards, mesh=mesh, in_specs=in_specs, out_specs=out_specs, check_vma=False)
+    out_specs = (P(SEQ, TP), P(SEQ, TP), P(SEQ, TP), P(SEQ, TP), P(TP, SEQ))
+    return jax.shard_map(shards, mesh=fine, in_specs=in_specs, out_specs=out_specs, check_vma=False)

time: 935 us -> 347 us (0.37)
  waiting for transfers between devices: 791 us -> 147 us
  blocking collectives: 0 us -> 87.4 us
  matrix products: 35.7 us -> 25.4 us
    unnamed x15 -> x4, waiting for transfers between devices: 276 us -> 18.2 us
    reduce_scatter x1 -> x0, waiting for transfers between devices: 201 us -> none  [shards(): lax.psum_scatter(token_term, 'tp', scatter_dimension=1, tiled=True)]
    all_gather x6 -> x2, waiting for transfers between devices: 304 us -> 121 us  [the longest x1 64.2 us: shards(): pair = lax.all_gather(pair, 'z', axis=2, tiled=True)]
    all_to_all x0 -> x1, blocking collectives: none -> 75.3 us  [shards(): lax.all_to_all(token_term.reshape(tok_rows, n_tp, cols), TP, 1, 1, tiled=...]
    scatter-add x14, other arithmetic: 13.1 us -> 0.39 us  [fold_windows(): summed = summed.at[offset:offset + n_blocks].add(shaped[:, offset])]
    all_gather x0 -> x1, blocking collectives: none -> 12.1 us  [shards(): pair = lax.all_gather(pair, 'yhi', axis=2, tiled=True)]
  transfers between devices with their start and end apart: 27 -> 19, of which waited for: 15 -> 7; matrix products, arithmetic and copies ran while one was open for 8% -> 6% of each run, Pallas kernels for 0% -> 0%
where the time goes in v1:
time: 347 us; the launch traced here: 345 us
  waiting for transfers between devices  147 us (42%)
  blocking collectives  87.4 us (25%)
  starting transfers between devices  34.2 us (10%)
  matrix products  25.4 us (7%)
  local copies, waits for them, and re-layouts  22.1 us (6%)
  between operations  14.6 us (4%)
  other arithmetic  14.5 us (4%)
    all_to_all x1, blocking collectives, shards(): lax.all_to_all(token_term.reshape(tok_rows, n_tp, cols), TP, 1, 1, tiled=...  75.3 us
    all_gather x1, waiting for transfers between devices, shards(): pair = lax.all_gather(pair, 'z', axis=2, tiled=True)  64.2 us
    all_gather x1, waiting for transfers between devices, shards(): w_full = lax.all_gather(w_cat, SEQ, axis=0, tiled=True)  57.1 us
    ppermute x16, starting transfers between devices, from_behind(): return lax.ppermute(block, axis, route)  34.1 us
    unnamed x4, waiting for transfers between devices  18.2 us
    unnamed x56, local copies, waits for them, and re-layouts  12.9 us
    all_gather x1, blocking collectives, shards(): pair = lax.all_gather(pair, 'yhi', axis=2, tiled=True)  12.1 us
    dot_general x2, matrix products, term_maker(): lax.dot_general(left, right, (((0,), (0,)), ((), ())), preferred_element_...  8.72 us
  transfers between devices with their start and end apart: 19, of which 7 were waited for; matrix products, arithmetic and copies ran while one was open for 6% of the time, Pallas kernels for 0%

profile of v1, /device:TPU:128, one launch (start us, length us, event | category | flops | bytes accessed | tf_op | source)
XLA Modules:
  0.0 345.4 jit_solution(4111263255536026014)
XLA Ops:
  7.2 0.0 all-gather.3.cloned.1.call-start
  7.3 1.2 pad_maximum_fusion.2
  8.4 12.1 %all_gather.9 = bf16[2,256,672]{1,2,0:T(8,128)(2,1)} all-gather(bf16[2,256,336]{1,2,0:T(8,128)(2,1)S(1)} %pad_maximum_fusion.2), channel_id=1, replica_groups=mesh['ylo'=2,'x'=4,'core'=2,'z'=8,'yhi'=2] {'yhi'}, dimensions={2}, use_global_device_ids=true | all-gather | bytes 1032192 | tf_op jit(solution)/shard_map/all_gather | solution.py:112
  20.5 0.0 all-gather.5.cloned.1.call-start
  20.6 0.8 pad_maximum_fusion.1
  21.5 0.0 reduce-scatter.4.cloned.1.call-start
  21.6 0.1 broadcast_bitcast_fusion
  21.7 0.1 fusion.38
  21.8 0.5 broadcast_and_fusion
  22.3 64.2 %all-gather.3.cloned.1.call-done = bf16[2,256,5376]{1,2,0:T(8,128)(2,1)} async-done(((bf16[2,256,672]{1,2,0:T(8,128)(2,1)}), bf16[2,256,5376]{1,2,0:T(8,128)(2,1)}) %all-gather.3.cloned.1.call-update) | async-done | bytes 5505040 | tf_op jit(solution)/shard_map/all_gather | solution.py:113
  86.6 57.1 %all-gather.5.cloned.1.call-done = bf16[5376,768]{1,0:T(8,128)(2,1)} async-done(((bf16[336,768]{1,0:T(8,128)(2,1)}), bf16[5376,768]{1,0:T(8,128)(2,1)}) %all-gather.5.cloned.1.call-update) | async-done | bytes 8257552 | tf_op jit(solution)/shard_map/all_gather | solution.py:116
  143.7 5.1 %fusion.15 = bf16[256,512]{1,0:T(8,128)(2,1)S(1)} fusion(bf16[5376,768]{1,0:T(8,128)(2,1)} %all-gather.5.cloned.1.call-done, bf16[2,256,5376]{1,2,0:T(8,128)(2,1)} %all-gather.3.cloned.1.call-done), kind=kOutput, calls=%fused_computation.26 | convolution fusion | flops 1409417216 | bytes 8519680 | tf_op jit(solution)/shard_map/dot_general | solution.py:121
  148.9 4.5 %collective-permute-start = (bf16[256,128]{1,0:T(8,128)(2,1)S(1)}, bf16[256,128]{1,0:T(8,128)(2,1)S(1)}, u32[]{:S(2)}, u32[]{:S(2)}) collective-permute-start(bf16[256,128]{1,0:T(8,128)(2,1)S(1)} %get-tuple-element.251), channel_id=1, source_target_pairs={{0,64},{16,80},{32,96},{48,112},{64,128},{80,144},{96,160},{112,17... | collective-permute-start | bytes 196616 | tf_op jit(solution)/shard_map/ppermute | solution.py:22
  153.4 2.7 fusion.25
  156.1 0.1 reshape.834
  156.3 1.9 collective-permute-start.7
  158.2 2.9 collective-permute-start.6
  161.0 4.9 %collective-permute-start.4 = (bf16[256,128]{1,0:T(8,128)(2,1)S(1)}, bf16[256,128]{1,0:T(8,128)(2,1)S(1)}, u32[]{:S(2)}, u32[]{:S(2)}) collective-permute-start(bf16[256,128]{1,0:T(8,128)(2,1)S(1)} %get-tuple-element.250), channel_id=1, source_target_pairs={{0,64},{16,80},{32,96},{48,112},{64,128},{80,144},{96,160},{112,17... | collective-permute-start | bytes 196616 | tf_op jit(solution)/shard_map/ppermute | solution.py:22
  166.0 3.2 collective-permute-start.3
  169.2 0.8 copy.98
  170.0 0.1 copy.83
  170.2 0.1 copy.87
  170.3 1.8 collective-permute-start.2
  172.1 1.9 collective-permute-start.1
  174.1 2.4 collective-permute-start.5
  176.7 1.9 collective-permute-done.5
  178.8 0.5 fusion.85
  179.3 0.5 fusion.14
  179.8 0.8 multiply_reduce_fusion
  180.5 0.8 copy.110
  181.3 1.8 convolution_bitcast_fusion.1
  183.2 0.8 fusion.10
  184.0 1.0 copy-done.1
  185.0 0.5 fusion.12
  185.5 0.4 copy.89
  185.9 0.4 copy.100
  186.6 0.8 fusion.58
  187.4 1.3 collective-permute-start.11
  188.7 1.3 collective-permute-start.10
  190.0 1.3 collective-permute-start.9
  191.3 1.4 collective-permute-start.8
  193.0 0.8 fusion.45
  193.8 1.3 collective-permute-start.15
  195.1 2.8 convolution_convert_fusion.1
  198.0 0.4 fusion.31
  198.4 0.1 copy.86
  198.6 1.3 collective-permute-start.14
  199.9 1.3 collective-permute-start.13
  201.2 1.5 collective-permute-start.12
  202.7 1.0 fusion.78
  203.7 2.7 collective-permute-done.15
  206.4 1.1 collective-permute-done.14
  207.4 2.0 collective-permute-done.13
  209.4 0.9 fusion.74
  210.3 5.9 %convolution_convert_fusion = bf16[5376,512]{0,1:T(8,128)(2,1)} fusion(bf16[2,256,5376]{1,2,0:T(8,128)(2,1)} %all-gather.3.cloned.1.call-done, bf16[256,128]{1,0:T(8,128)(2,1)S(1)} %fusion.74, bf16[256,128]{1,0:T(8,128)(2,1)S(1)} %fusion.78, bf16[256,256]{1,0:T(8,128)(2,1)S(1)} %bitcast.326), kind=kOutput, calls=%fused_computation | convolution fusion | flops 1412825088 | bytes 8519680 | tf_op jit(solution)/shard_map/dot_general | solution.py:97
  216.2 6.3 %pad_maximum_fusion = bf16[5376,768]{0,1:T(8,128)(2,1)} fusion(bf16[5376,256]{0,1:T(8,128)(2,1)S(1)} %convolution_convert_fusion.1, bf16[5376,512]{0,1:T(8,128)(2,1)} %convolution_convert_fusion), kind=kLoop, calls=%fused_computation.1 | loop fusion | flops 16515072 | bytes 16515072 | tf_op jit(solution)/shard_map/concatenate | solution.py:159
  222.5 11.5 %copy.129 = bf16[5376,768]{1,0:T(8,128)(2,1)} copy(bf16[5376,768]{0,1:T(8,128)(2,1)} %pad_maximum_fusion) | data formatting | bytes 16515072
  234.0 4.2 %convolution_convert_fusion.2 = bf16[256,5376]{1,0:T(8,128)(2,1)S(1)} fusion(bf16[5376,768]{1,0:T(8,128)(2,1)} %all-gather.5.cloned.1.call-done, bf16[256,128]{1,0:T(8,128)(2,1)S(1)} %fusion.74, bf16[256,128]{1,0:T(8,128)(2,1)S(1)} %fusion.78, bf16[256,256]{1,0:T(8,128)(2,1)S(1)} %bitcast.327), kind=kOutput, calls=%fused_computation.3 | convolution fusion | flops 1411448832 | bytes 8519680 | tf_op jit(solution)/shard_map/dot_general | solution.py:91
  238.2 2.8 copy.109
  241.0 75.3 %all_to_all.5 = bf16[256,16,336]{0,2,1:T(8,128)(2,1)S(1)} all-to-all(bf16[256,16,336]{0,2,1:T(8,128)(2,1)} %bitcast.304), channel_id=1, replica_groups=mesh['ylo'=2,'x'=4,'core'=2,'z'=8,'yhi'=2] {'z','yhi'}, dimensions={1} | all-to-all | bytes 5505024 | tf_op jit(solution)/shard_map/all_to_all | solution.py:157
  316.3 1.1 reduce_sum.35
  317.4 18.2 %reduce-scatter.4.cloned.1.call-done = bf16[336,768]{1,0:T(8,128)(2,1)} async-done(((bf16[5376,768]{1,0:T(8,128)(2,1)}), bf16[336,768]{1,0:T(8,128)(2,1)}) %reduce-scatter.4.cloned.1.call-update) | async-done | bytes 516112
  335.5 1.6 fusion.83
  337.1 1.8 slice_bitcast_fusion.10
  (96 shorter events, 1.1 us)
Async XLA Ops:
  7.2 13.4 %copy-start.10 = (bf16[256,336]{0,1:T(8,128)(2,1)S(1)}, bf16[256,336]{0,1:T(8,128)(2,1)}, u32[]{:S(2)}) copy-start(bf16[256,336]{0,1:T(8,128)(2,1)} %param.47) | copy-start | bytes 516100
  7.2 13.4 %copy-start.13 = (bf16[336,128]{1,0:T(8,128)(2,1)S(1)}, bf16[336,128]{1,0:T(8,128)(2,1)}, u32[]{:S(2)}) copy-start(bf16[336,128]{1,0:T(8,128)(2,1)} %param.46) | copy-start | bytes 258052
  7.2 13.4 %copy-start.14 = (bf16[336,128]{1,0:T(8,128)(2,1)S(1)}, bf16[336,128]{1,0:T(8,128)(2,1)}, u32[]{:S(2)}) copy-start(bf16[336,128]{1,0:T(8,128)(2,1)} %param.45) | copy-start | bytes 258052
  7.2 13.4 %copy-start.11 = (bf16[336,256]{1,0:T(8,128)(2,1)S(1)}, bf16[336,256]{1,0:T(8,128)(2,1)}, u32[]{:S(2)}) copy-start(bf16[336,256]{1,0:T(8,128)(2,1)} %param.44) | copy-start | bytes 516100
  7.2 14.3 %copy-start.17 = (s32[2,9]{1,0:T(2,128)S(1)}, s32[2,9]{1,0:T(2,128)}, u32[]{:S(2)}) copy-start(s32[2,9]{1,0:T(2,128)} %param.49) | copy-start | bytes 220
  7.2 79.3 %all-gather.3.cloned.1.call-start = ((), (), s32[]{:S(2)}) async-start(), calls=%async_computation.2 | async-start | bytes 6193152 | tf_op jit(solution)/shard_map/all_gather | solution.py:113
  20.5 123.2 %all-gather.5.cloned.1.call-start = ((), (), s32[]{:S(2)}) async-start(), calls=%async_computation.3 | async-start | bytes 8773632 | tf_op jit(solution)/shard_map/all_gather | solution.py:116
  21.5 314.0 %reduce-scatter.4.cloned.1.call-start = ((), (), s32[]{:S(2)}) async-start(), calls=%async_computation.4 | async-start | bytes 8773632
  22.3 157.5 %copy-start.3 = (pred[2,128,1152]{1,2,0:T(8,128)(4,1)}, pred[2,128,1152]{1,2,0:T(8,128)(4,1)S(1)}, u32[]{:S(2)}) copy-start(pred[2,128,1152]{1,2,0:T(8,128)(4,1)S(1)} %broadcast_and_fusion) | copy-start | bytes 884740
  143.7 9.7 %copy-start = (bf16[2,256,5376]{1,2,0:T(8,128)(2,1)S(1)}, bf16[2,256,5376]{1,2,0:T(8,128)(2,1)}, u32[]{:S(2)}) copy-start(bf16[2,256,5376]{1,2,0:T(8,128)(2,1)} %all-gather.3.cloned.1.call-done) | copy-start | bytes 16515076
  148.9 21.4 %collective-permute-start = (bf16[256,128]{1,0:T(8,128)(2,1)S(1)}, bf16[256,128]{1,0:T(8,128)(2,1)S(1)}, u32[]{:S(2)}, u32[]{:S(2)}) collective-permute-start(bf16[256,128]{1,0:T(8,128)(2,1)S(1)} %get-tuple-element.251), channel_id=1, source_target_pairs={{0,64},{16,80},{32,96},{48,112},{64,128},{80,144},{96,160},{112,17... | collective-permute-start | bytes 196616 | tf_op jit(solution)/shard_map/ppermute | solution.py:22
  156.3 20.4 %collective-permute-start.7 = (bf16[256,128]{1,0:T(8,128)(2,1)S(1)}, bf16[256,128]{1,0:T(8,128)(2,1)S(1)}, u32[]{:S(2)}, u32[]{:S(2)}) collective-permute-start(bf16[256,128]{1,0:T(8,128)(2,1)S(1)} %get-tuple-element.250), channel_id=1, source_target_pairs={{0,16},{16,32},{32,48},{48,64},{64,80},{80,96},{96,112},{112,128},... | collective-permute-start | bytes 196616 | tf_op jit(solution)/shard_map/ppermute | solution.py:22
  158.2 18.5 %collective-permute-start.6 = (bf16[256,128]{1,0:T(8,128)(2,1)S(1)}, bf16[256,128]{1,0:T(8,128)(2,1)S(1)}, u32[]{:S(2)}, u32[]{:S(2)}) collective-permute-start(bf16[256,128]{1,0:T(8,128)(2,1)S(1)} %get-tuple-element.250), channel_id=1, source_target_pairs={{0,32},{16,48},{32,64},{48,80},{64,96},{80,112},{96,128},{112,144}... | collective-permute-start | bytes 196616 | tf_op jit(solution)/shard_map/ppermute | solution.py:22
  161.0 11.1 %collective-permute-start.4 = (bf16[256,128]{1,0:T(8,128)(2,1)S(1)}, bf16[256,128]{1,0:T(8,128)(2,1)S(1)}, u32[]{:S(2)}, u32[]{:S(2)}) collective-permute-start(bf16[256,128]{1,0:T(8,128)(2,1)S(1)} %get-tuple-element.250), channel_id=1, source_target_pairs={{0,64},{16,80},{32,96},{48,112},{64,128},{80,144},{96,160},{112,17... | collective-permute-start | bytes 196616 | tf_op jit(solution)/shard_map/ppermute | solution.py:22
  166.0 8.1 %collective-permute-start.3 = (bf16[256,128]{1,0:T(8,128)(2,1)S(1)}, bf16[256,128]{1,0:T(8,128)(2,1)S(1)}, u32[]{:S(2)}, u32[]{:S(2)}) collective-permute-start(bf16[256,128]{1,0:T(8,128)(2,1)S(1)} %get-tuple-element.251), channel_id=1, source_target_pairs={{0,16},{16,32},{32,48},{48,64},{64,80},{80,96},{96,112},{112,128},... | collective-permute-start | bytes 196616 | tf_op jit(solution)/shard_map/ppermute | solution.py:22
  170.3 9.0 %copy-start.8 = (bf16[2,128,2,128]{1,3,2,0:T(8,128)(2,1)}, bf16[2,128,2,128]{1,3,2,0:T(8,128)(2,1)S(1)}, u32[]{:S(2)}) copy-start(bf16[2,128,2,128]{1,3,2,0:T(8,128)(2,1)S(1)} %copy.87) | copy-start | bytes 393220
  170.3 6.2 %collective-permute-start.2 = (bf16[256,128]{1,0:T(8,128)(2,1)S(1)}, bf16[256,128]{1,0:T(8,128)(2,1)S(1)}, u32[]{:S(2)}, u32[]{:S(2)}) collective-permute-start(bf16[256,128]{1,0:T(8,128)(2,1)S(1)} %get-tuple-element.251), channel_id=1, source_target_pairs={{0,32},{16,48},{32,64},{48,80},{64,96},{80,112},{96,128},{112,144}... | collective-permute-start | bytes 196616 | tf_op jit(solution)/shard_map/ppermute | solution.py:22
  172.1 4.4 %collective-permute-start.1 = (bf16[256,128]{1,0:T(8,128)(2,1)S(1)}, bf16[256,128]{1,0:T(8,128)(2,1)S(1)}, u32[]{:S(2)}, u32[]{:S(2)}) collective-permute-start(bf16[256,128]{1,0:T(8,128)(2,1)S(1)} %get-tuple-element.251), channel_id=1, source_target_pairs={{0,48},{16,64},{32,80},{48,96},{64,112},{80,128},{96,144},{112,160... | collective-permute-start | bytes 196616 | tf_op jit(solution)/shard_map/ppermute | solution.py:22
  174.1 4.5 %collective-permute-start.5 = (bf16[256,128]{1,0:T(8,128)(2,1)S(1)}, bf16[256,128]{1,0:T(8,128)(2,1)S(1)}, u32[]{:S(2)}, u32[]{:S(2)}) collective-permute-start(bf16[256,128]{1,0:T(8,128)(2,1)S(1)} %get-tuple-element.250), channel_id=1, source_target_pairs={{0,48},{16,64},{32,80},{48,96},{64,112},{80,128},{96,144},{112,160... | collective-permute-start | bytes 196616 | tf_op jit(solution)/shard_map/ppermute | solution.py:22
  176.7 2.6 copy-start.5
  178.8 1.0 copy-start.15
  181.3 1.8 copy-start.4
  181.3 1.8 copy-start.12
  181.3 1.8 copy-start.16
  183.2 1.8 copy-start.9
  184.0 1.0 copy-start.1
  187.4 11.2 %collective-permute-start.11 = (f32[256,128]{1,0:T(8,128)}, f32[256,128]{1,0:T(8,128)S(1)}, u32[]{:S(2)}, u32[]{:S(2)}) collective-permute-start(f32[256,128]{1,0:T(8,128)} %bitcast.62), channel_id=1, source_target_pairs={{64,0},{80,16},{96,32},{112,48},{128,64},{144,80},{160,96},{176,11... | collective-permute-start | bytes 393224 | tf_op jit(solution)/shard_map/ppermute | solution.py:22
  188.7 11.2 %collective-permute-start.10 = (f32[256,128]{1,0:T(8,128)}, f32[256,128]{1,0:T(8,128)S(1)}, u32[]{:S(2)}, u32[]{:S(2)}) collective-permute-start(f32[256,128]{1,0:T(8,128)} %bitcast.61), channel_id=1, source_target_pairs={{48,0},{64,16},{80,32},{96,48},{112,64},{128,80},{144,96},{160,112... | collective-permute-start | bytes 393224 | tf_op jit(solution)/shard_map/ppermute | solution.py:22
  190.0 11.2 %collective-permute-start.9 = (f32[256,128]{1,0:T(8,128)}, f32[256,128]{1,0:T(8,128)}, u32[]{:S(2)}, u32[]{:S(2)}) collective-permute-start(f32[256,128]{1,0:T(8,128)} %bitcast.60), channel_id=1, source_target_pairs={{32,0},{48,16},{64,32},{80,48},{96,64},{112,80},{128,96},{144,112}... | collective-permute-start | bytes 393224 | tf_op jit(solution)/shard_map/ppermute | solution.py:22
  191.3 3.8 %copy-start.7 = (bf16[2,128,1,2,128]{4,3,1,0,2:T(2,128)(2,1)S(1)}, bf16[2,128,1,2,128]{4,3,1,0,2:T(2,128)(2,1)}, u32[]{:S(2)}) copy-start(bf16[2,128,1,2,128]{4,3,1,0,2:T(2,128)(2,1)} %copy.110) | copy-start | bytes 393220
  191.3 11.4 %collective-permute-start.8 = (f32[256,128]{1,0:T(8,128)}, f32[256,128]{1,0:T(8,128)}, u32[]{:S(2)}, u32[]{:S(2)}) collective-permute-start(f32[256,128]{1,0:T(8,128)} %bitcast.59), channel_id=1, source_target_pairs={{16,0},{32,16},{48,32},{64,48},{80,64},{96,80},{112,96},{128,112},... | collective-permute-start | bytes 393224 | tf_op jit(solution)/shard_map/ppermute | solution.py:22
  193.8 12.5 %collective-permute-start.15 = (f32[256,128]{1,0:T(8,128)}, f32[256,128]{1,0:T(8,128)}, u32[]{:S(2)}, u32[]{:S(2)}) collective-permute-start(f32[256,128]{1,0:T(8,128)} %bitcast.81), channel_id=1, source_target_pairs={{64,0},{80,16},{96,32},{112,48},{128,64},{144,80},{160,96},{176,11... | collective-permute-start | bytes 393224 | tf_op jit(solution)/shard_map/ppermute | solution.py:22
  195.1 2.9 copy-start.2
  195.1 2.9 copy-start.6
  198.6 8.9 %collective-permute-start.14 = (f32[256,128]{1,0:T(8,128)}, f32[256,128]{1,0:T(8,128)S(1)}, u32[]{:S(2)}, u32[]{:S(2)}) collective-permute-start(f32[256,128]{1,0:T(8,128)} %bitcast.350), channel_id=1, source_target_pairs={{48,0},{64,16},{80,32},{96,48},{112,64},{128,80},{144,96},{160,112... | collective-permute-start | bytes 393224 | tf_op jit(solution)/shard_map/ppermute | solution.py:22
  199.9 9.5 %collective-permute-start.13 = (f32[256,128]{1,0:T(8,128)}, f32[256,128]{1,0:T(8,128)S(1)}, u32[]{:S(2)}, u32[]{:S(2)}) collective-permute-start(f32[256,128]{1,0:T(8,128)} %bitcast.349), channel_id=1, source_target_pairs={{32,0},{48,16},{64,32},{80,48},{96,64},{112,80},{128,96},{144,112}... | collective-permute-start | bytes 393224 | tf_op jit(solution)/shard_map/ppermute | solution.py:22
  201.2 8.2 %collective-permute-start.12 = (f32[256,128]{1,0:T(8,128)}, f32[256,128]{1,0:T(8,128)S(1)}, u32[]{:S(2)}, u32[]{:S(2)}) collective-permute-start(f32[256,128]{1,0:T(8,128)} %bitcast.348), channel_id=1, source_target_pairs={{16,0},{32,16},{48,32},{64,48},{80,64},{96,80},{112,96},{128,112},... | collective-permute-start | bytes 393224 | tf_op jit(solution)/shard_map/ppermute | solution.py:22
Sparse Core Ops, SparseCore 0:
  20.7 65.8 all-gather.2
  88.4 55.2 all-gather.4
  234.2 101.3 reduce-scatter.3

commit v2 on v1

v2 whole, which is shorter than its diff:
```python
import functools

import jax
import jax.numpy as jnp
from jax import lax
from jax.experimental import pallas as pl
from jax.sharding import Mesh
from jax.sharding import PartitionSpec as P

HEADS = 32
KV_HEADS = 16
HD = 128
WIN = 1024
ATTN_SCALAR = 168

SEQ = ("ylo", "x", "core")
TP = ("z", "yhi")
SEQ_SPLIT = (2, 4, 2)
TP_SPLIT = (8, 2)


def from_behind(block, axis, distance):
    devices = range(lax.psum(1, axis))
    route = [(i - distance, i) for i in devices if i - distance in devices]
    return lax.ppermute(block, axis, route)


def _nt(left, right):
    return lax.dot_general(left, right, (((1,), (1,)), ((), ())), preferred_element_type=jnp.float32)


def _nn(left, right):
    return lax.dot_general(left, right, (((1,), (0,)), ((), ())), preferred_element_type=jnp.float32)


def attention_kernel(q_ref, d_ref, kv_ref, lst_ref, attn_ref, gq_ref, dkv_ref, *, scale, block_len, span, head_dim):
    n_blocks = q_ref.shape[0] // block_len
    groups = q_ref.shape[1] // head_dim
    width = span * block_len
    dkv_ref[...] = jnp.zeros(dkv_ref.shape, jnp.float32)
    rows = lax.broadcasted_iota(jnp.int32, (block_len, width), 0)
    cols = lax.broadcasted_iota(jnp.int32, (block_len, width), 1)
    inside = (cols > rows) & (cols <= rows + (width - block_len))
    for b in range(n_blocks):
        w0 = b * block_len
        kw = kv_ref[w0 : w0 + width, :head_dim]
        vw = kv_ref[w0 : w0 + width, head_dim:]
        allowed = inside & (lst_ref[b : b + 1, :] > 0.0)
        dk_acc = jnp.zeros((width, head_dim), jnp.float32)
        dv_acc = jnp.zeros((width, head_dim), jnp.float32)
        for g in range(groups):
            r0, c0 = b * block_len, g * head_dim
            qb = q_ref[r0 : r0 + block_len, c0 : c0 + head_dim]
            db = d_ref[r0 : r0 + block_len, c0 : c0 + head_dim]
            scores = _nt(qb, kw) * scale
            masked = jnp.where(allowed, scores, -1e30)
            highest = jnp.max(masked, axis=1, keepdims=True)
            weights = jnp.where(allowed, jnp.exp(masked - highest), 0.0)
            probs = weights / jnp.sum(weights, axis=1, keepdims=True)
            probs_half = probs.astype(jnp.bfloat16)
            attn = _nn(probs_half, vw).astype(jnp.bfloat16)
            attn_ref[r0 : r0 + block_len, c0 : c0 + head_dim] = attn
            delta = jnp.sum(db.astype(jnp.float32) * attn.astype(jnp.float32), axis=1, keepdims=True)
            grad_probs = _nt(db, vw)
            grad_scores = (probs * (grad_probs - delta)).astype(jnp.bfloat16)
            grad_q = _nn(grad_scores, kw) * scale
            gq_ref[r0 : r0 + block_len, c0 : c0 + head_dim] = grad_q.astype(jnp.bfloat16)
            dk_acc = dk_acc + _nn(grad_scores.T, qb)
            dv_acc = dv_acc + _nn(probs_half.T, db)
        dkv_ref[w0 : w0 + width, :head_dim] += dk_acc * scale
        dkv_ref[w0 : w0 + width, head_dim:] += dv_acc


def fused_attention(query, kv_ext, d_attn, block_lists, scale, head_dim):
    n_blocks, span = block_lists.shape
    block_len = query.shape[0] // n_blocks
    listed = jnp.repeat((block_lists >= 0).astype(jnp.float32), block_len, axis=1)
    body = functools.partial(
        attention_kernel, scale=scale, block_len=block_len, span=span, head_dim=head_dim
    )
    return pl.pallas_call(
        body,
        out_shape=(
            jax.ShapeDtypeStruct(query.shape, jnp.bfloat16),
            jax.ShapeDtypeStruct(query.shape, jnp.bfloat16),
            jax.ShapeDtypeStruct(kv_ext.shape, jnp.float32),
        ),
    )(query, d_attn, kv_ext, listed)


def contract_cols(left, right):
    return lax.dot_general(
        left, right, (((1,), (1,)), ((), ())), preferred_element_type=jnp.float32
    )


def term_maker(left, right):
    return lax.dot_general(
        left, right, (((0,), (0,)), ((), ())), preferred_element_type=jnp.float32
    )


def shards(tokens, w_query, w_key, w_value, w_out, cotangent, block_lists):
    softmax_scale = ATTN_SCALAR ** (-0.5)
    head_dim = HD
    tok_rows = tokens.shape[0]
    reach = WIN // tok_rows
    n_q = w_query.shape[1]
    n_kv = w_key.shape[1]
    n_proj = n_q + 2 * n_kv
    pair = jnp.stack([tokens, cotangent])
    pair = lax.all_gather(pair, "yhi", axis=2, tiled=True)
    pair = lax.all_gather(pair, "z", axis=2, tiled=True)
    full_tokens, full_cot = pair[0], pair[1]
    w_cat = jnp.concatenate([w_query, w_key, w_value, w_out.T], axis=1)
    w_full = lax.all_gather(w_cat, SEQ, axis=0, tiled=True)
    proj_full = w_full[:, :n_proj]
    d_attn = jnp.dot(full_cot, w_full[:, n_proj:], preferred_element_type=jnp.float32).astype(
        jnp.bfloat16
    )
    qkv = jnp.dot(full_tokens, proj_full, preferred_element_type=jnp.float32).astype(jnp.bfloat16)
    query = qkv[:, :n_q]
    kv = qkv[:, n_q:]
    earlier = [from_behind(kv, SEQ, distance) for distance in range(reach, 0, -1)]
    kv_ext = jnp.concatenate(earlier + [kv], axis=0)
    attn, grad_q, grad_kv_ext = fused_attention(
        query, kv_ext, d_attn, block_lists, softmax_scale, head_dim
    )

    def segment(array, index):
        return array[index * tok_rows : (index + 1) * tok_rows]

    summed_kv = segment(grad_kv_ext, reach)
    for distance in range(1, reach + 1):
        summed_kv = summed_kv + from_behind(segment(grad_kv_ext, reach - distance), SEQ, -distance)
    grad_kv = summed_kv.astype(jnp.bfloat16)
    grad_act = jnp.concatenate([grad_q, grad_kv], axis=1)
    token_term = contract_cols(grad_act, proj_full).astype(jnp.bfloat16)
    n_tp = lax.psum(1, TP)
    cols = token_term.shape[1] // n_tp
    parts = lax.all_to_all(token_term.reshape(tok_rows, n_tp, cols), TP, 1, 1, tiled=True)
    grad_tokens = parts.astype(jnp.float32).sum(axis=1).astype(jnp.bfloat16)
    weight_terms = jnp.concatenate(
        [
            term_maker(full_tokens, grad_act).astype(jnp.bfloat16),
            term_maker(full_cot, attn).astype(jnp.bfloat16),
        ],
        axis=1,
    )
    summed = lax.psum_scatter(weight_terms, SEQ, scatter_dimension=0, tiled=True)
    grad_query = summed[:, :n_q]
    grad_key = summed[:, n_q : n_q + n_kv]
    grad_value = summed[:, n_q + n_kv : n_proj]
    grad_w_out = summed[:, n_proj:].T
    return (grad_tokens, grad_query, grad_key, grad_value, grad_w_out)


def solution(mesh):
    fine = Mesh(mesh.devices.reshape(SEQ_SPLIT + TP_SPLIT), SEQ + TP)
    in_specs = (
        P(SEQ, TP),
        P(SEQ, TP),
        P(SEQ, TP),
        P(SEQ, TP),
        P(TP, SEQ),
        P(SEQ, TP),
        P(SEQ, None),
    )
    out_specs = (P(SEQ, TP), P(SEQ, TP), P(SEQ, TP), P(SEQ, TP), P(TP, SEQ))
    return jax.shard_map(shards, mesh=fine, in_specs=in_specs, out_specs=out_specs, check_vma=False)
```

time: 347 us -> 328 us (0.945)
  starting transfers between devices: 34.2 us -> 19.6 us
  Pallas kernels: 0 us -> 6.73 us
  matrix products: 25.4 us -> 19.6 us
    ppermute x16 -> x8, starting transfers between devices: 34.1 us -> 19.4 us  [from_behind(): return lax.ppermute(block, axis, route)]
    pallas_call x0 -> x1, Pallas kernels: none -> 6.73 us  [fused_attention(): pl.pallas_call(body, out_shape=(jax.ShapeDtypeStruct(query.shape, jnp.bfl...]
    dot_general x6 -> x0, matrix products: 4.7 us -> none  [the longest x1 1.82 us: local_attention(): jnp.einsum('bkgtw,btkgd->bwkd', probs_half, grad_blocks, preferred_elemen...]
    ppermute x16 -> x8, waiting for transfers between devices: 7.65 us -> 6.94 us  [from_behind(): return lax.ppermute(block, axis, route)]
    unnamed x56 -> x17, local copies, waits for them, and re-layouts: 12.9 us -> 13.1 us
  transfers between devices with their start and end apart: 19 -> 11, of which waited for: 7 -> 5; matrix products, arithmetic and copies ran while one was open for 6% -> 5% of each run, Pallas kernels for 0% -> 0%
where the time goes in v2:
time: 328 us; the launch traced here: 326 us
  waiting for transfers between devices  145 us (44%)
  blocking collectives  87.2 us (27%)
  local copies, waits for them, and re-layouts  21.4 us (7%)
  starting transfers between devices  19.6 us (6%)
  matrix products  19.6 us (6%)
  between operations  14 us (4%)
  other arithmetic  12 us (4%)
  Pallas kernels  6.73 us (2%)
    all_to_all x1, blocking collectives, shards(): lax.all_to_all(token_term.reshape(tok_rows, n_tp, cols), TP, 1, 1, tiled=...  75.1 us
    all_gather x1, waiting for transfers between devices, shards(): pair = lax.all_gather(pair, 'z', axis=2, tiled=True)  62.6 us
    all_gather x1, waiting for transfers between devices, shards(): w_full = lax.all_gather(w_cat, SEQ, axis=0, tiled=True)  57.1 us
    ppermute x8, starting transfers between devices, from_behind(): return lax.ppermute(block, axis, route)  19.4 us
    unnamed x4, waiting for transfers between devices  18.7 us
    unnamed x17, local copies, waits for them, and re-layouts  13.1 us
    all_gather x1, blocking collectives, shards(): pair = lax.all_gather(pair, 'yhi', axis=2, tiled=True)  12.1 us
    dot_general x2, matrix products, term_maker(): lax.dot_general(left, right, (((0,), (0,)), ((), ())), preferred_element_...  6.96 us
  transfers between devices with their start and end apart: 11, of which 5 were waited for; matrix products, arithmetic and copies ran while one was open for 5% of the time, Pallas kernels for 0%

profile of v2, /device:TPU:128, one launch (start us, length us, event | category | flops | bytes accessed | tf_op | source)
XLA Modules:
  0.0 325.9 jit_solution(8788704224993026613)
XLA Ops:
  7.2 0.0 all-gather.3.cloned.1.call-start
  7.2 1.0 pad_maximum_fusion.2
  8.2 12.1 %all_gather.9 = bf16[2,256,672]{1,2,0:T(8,128)(2,1)} all-gather(bf16[2,256,336]{1,2,0:T(8,128)(2,1)S(1)} %pad_maximum_fusion.2), channel_id=1, replica_groups=mesh['ylo'=2,'x'=4,'core'=2,'z'=8,'yhi'=2] {'yhi'}, dimensions={2}, use_global_device_ids=true | all-gather | bytes 1032192 | tf_op jit(solution)/shard_map/all_gather | solution.py:112
  20.3 0.0 all-gather.3.cloned.1.call-update
  20.4 0.0 all-gather.5.cloned.1.call-start
  20.4 1.9 pad_maximum_fusion.1
  22.3 0.0 all-gather.5.cloned.1.call-update
  22.4 0.0 reduce-scatter.4.cloned.1.call-start
  22.4 0.7 compare_convert_fusion
  23.1 0.1 broadcast_bitcast_fusion
  23.2 0.6 copy.35
  23.8 62.6 %all-gather.3.cloned.1.call-done = bf16[2,256,5376]{1,2,0:T(8,128)(2,1)} async-done(((bf16[2,256,672]{1,2,0:T(8,128)(2,1)}), bf16[2,256,5376]{1,2,0:T(8,128)(2,1)}) %all-gather.3.cloned.1.call-update) | async-done | bytes 5505040 | tf_op jit(solution)/shard_map/all_gather | solution.py:113
  86.4 57.1 %all-gather.5.cloned.1.call-done = bf16[5376,768]{1,0:T(8,128)(2,1)} async-done(((bf16[336,768]{1,0:T(8,128)(2,1)}), bf16[5376,768]{1,0:T(8,128)(2,1)}) %all-gather.5.cloned.1.call-update) | async-done | bytes 8257552 | tf_op jit(solution)/shard_map/all_gather | solution.py:116
  143.5 0.0 copy-start
  143.5 5.1 %fusion.5 = bf16[256,512]{1,0:T(8,128)(2,1)S(1)} fusion(bf16[5376,768]{1,0:T(8,128)(2,1)} %all-gather.5.cloned.1.call-done, bf16[2,256,5376]{1,2,0:T(8,128)(2,1)} %all-gather.3.cloned.1.call-done), kind=kOutput, calls=%fused_computation.11 | convolution fusion | flops 1409417216 | bytes 8519680 | tf_op jit(solution)/shard_map/dot_general | solution.py:121
  148.7 2.1 collective-permute-start.3
  150.8 3.3 %collective-permute-start.2 = (bf16[256,256]{1,0:T(8,128)(2,1)S(1)}, bf16[256,256]{1,0:T(8,128)(2,1)S(1)}, u32[]{:S(2)}, u32[]{:S(2)}) collective-permute-start(bf16[256,256]{1,0:T(8,128)(2,1)S(1)} %slice.65), channel_id=1, source_target_pairs={{0,32},{16,48},{32,64},{48,80},{64,96},{80,112},{96,128},{112,144}... | collective-permute-start | bytes 393224 | tf_op jit(solution)/shard_map/ppermute | solution.py:25
  154.1 3.8 %collective-permute-start.1 = (bf16[256,256]{1,0:T(8,128)(2,1)S(1)}, bf16[256,256]{1,0:T(8,128)(2,1)S(1)}, u32[]{:S(2)}, u32[]{:S(2)}) collective-permute-start(bf16[256,256]{1,0:T(8,128)(2,1)S(1)} %slice.65), channel_id=1, source_target_pairs={{0,48},{16,64},{32,80},{48,96},{64,112},{80,128},{96,144},{112,160... | collective-permute-start | bytes 393224 | tf_op jit(solution)/shard_map/ppermute | solution.py:25
  157.9 4.9 %collective-permute-start = (bf16[256,256]{1,0:T(8,128)(2,1)S(1)}, bf16[256,256]{1,0:T(8,128)(2,1)S(1)}, u32[]{:S(2)}, u32[]{:S(2)}) collective-permute-start(bf16[256,256]{1,0:T(8,128)(2,1)S(1)} %slice.65), channel_id=1, source_target_pairs={{0,64},{16,80},{32,96},{48,112},{64,128},{80,144},{96,160},{112,17... | collective-permute-start | bytes 393224 | tf_op jit(solution)/shard_map/ppermute | solution.py:25
  162.9 0.0 copy-done
  162.9 3.4 %fusion.8.d_ref = bf16[256,256]{1,0:T(8,128)(2,1)} fusion(bf16[5376,768]{1,0:T(8,128)(2,1)} %all-gather.5.cloned.1.call-done, bf16[2,256,5376]{1,2,0:T(8,128)(2,1)S(1)} %copy-done), kind=kOutput, calls=%fused_computation.12 | convolution fusion | flops 704708608 | bytes 5636096 | tf_op jit(solution)/shard_map/dot_general | solution.py:118
  166.2 0.0 collective-permute-done
  166.3 0.0 collective-permute-done.1
  166.3 0.0 collective-permute-done.2
  166.3 0.0 collective-permute-done.3
  166.3 0.7 constant_dynamic-update-slice_fusion
  167.0 0.0 copy-start.1
  167.0 0.9 copy-done.1
  167.9 6.7 %shard_map.110 = (bf16[256,256]{1,0:T(8,128)(2,1)}, bf16[256,256]{1,0:T(8,128)(2,1)}, f32[1280,256]{1,0:T(8,128)}) custom-call(bf16[256,256]{1,0:T(8,128)(2,1)} %get-tuple-element.35.q_ref, bf16[256,256]{1,0:T(8,128)(2,1)} %fusion.8.d_ref, bf16[1280,256]{1,0:T(8,128)(2,1)} %copy-done.1, f32[2,1152]{1,0:T(2,128)} %bitcast.32), custom_call_target="tpu_custom_call" | custom-call | tf_op jit(solution)/shard_map/pallas_call | solution.py:81
  174.6 0.0 slice-start
  174.6 1.4 fusion.13
  176.0 1.4 collective-permute-start.4
  177.5 1.3 collective-permute-start.7
  178.8 1.3 collective-permute-start.6
  180.1 1.3 collective-permute-start.5
  181.4 0.0 slice-start.1
  181.4 0.0 copy-start.2
  181.4 2.8 convolution_convert_fusion.1
  184.2 0.0 collective-permute-done.4
  184.2 6.0 %collective-permute-done.7 = f32[256,256]{1,0:T(8,128)S(1)} collective-permute-done((f32[256,256]{1,0:T(8,128)S(1)}, f32[256,256]{1,0:T(8,128)S(1)}, u32[]{:S(2)}, u32[]{:S(2)}) %collective-permute-start.7) | collective-permute-done | bytes 262176 | tf_op jit(solution)/shard_map/ppermute | solution.py:25
  190.2 0.0 collective-permute-done.6
  190.2 0.9 collective-permute-done.5
  191.1 1.0 add_convert_fusion
  192.2 0.0 slice-done
  192.2 0.0 slice-done.1
  192.2 0.0 copy-done.2
  192.2 4.1 %convolution_convert_fusion = bf16[5376,512]{0,1:T(8,128)(2,1)} fusion(bf16[2,256,5376]{1,2,0:T(8,128)(2,1)S(1)} %bitcast.27, bf16[256,256]{1,0:T(8,128)(2,1)S(1)} %add_convert_fusion, bf16[256,256]{1,0:T(8,128)(2,1)S(1)} %copy-done.2), kind=kOutput, calls=%fused_computation | convolution fusion | flops 1412562944 | bytes 8519680 | tf_op jit(solution)/shard_map/dot_general | solution.py:98
  196.3 6.3 %pad_maximum_fusion = bf16[5376,768]{0,1:T(8,128)(2,1)} fusion(bf16[5376,256]{0,1:T(8,128)(2,1)S(1)} %convolution_convert_fusion.1, bf16[5376,512]{0,1:T(8,128)(2,1)} %convolution_convert_fusion), kind=kLoop, calls=%fused_computation.1 | loop fusion | flops 16515072 | bytes 16515072 | tf_op jit(solution)/shard_map/concatenate | solution.py:143
  202.6 11.5 %copy.26 = bf16[5376,768]{1,0:T(8,128)(2,1)} copy(bf16[5376,768]{0,1:T(8,128)(2,1)} %pad_maximum_fusion) | data formatting | bytes 16515072
  214.1 0.0 reduce-scatter.4.cloned.1.call-update
  214.2 4.2 %convolution_convert_fusion.2 = bf16[256,5376]{1,0:T(8,128)(2,1)S(1)} fusion(bf16[5376,768]{1,0:T(8,128)(2,1)} %all-gather.5.cloned.1.call-done, bf16[256,256]{1,0:T(8,128)(2,1)S(1)} %add_convert_fusion, bf16[256,256]{1,0:T(8,128)(2,1)S(1)} %copy-done.2), kind=kOutput, calls=%fused_computation.3 | convolution fusion | flops 1411186688 | bytes 8519680 | tf_op jit(solution)/shard_map/dot_general | solution.py:92
  218.4 2.8 copy.21
  221.1 75.1 %all_to_all.5 = bf16[256,16,336]{0,2,1:T(8,128)(2,1)S(1)} all-to-all(bf16[256,16,336]{0,2,1:T(8,128)(2,1)} %bitcast.28), channel_id=1, replica_groups=mesh['ylo'=2,'x'=4,'core'=2,'z'=8,'yhi'=2] {'z','yhi'}, dimensions={1} | all-to-all | bytes 5505024 | tf_op jit(solution)/shard_map/all_to_all | solution.py:141
  296.3 1.1 reduce_sum.12
  297.4 18.7 %reduce-scatter.4.cloned.1.call-done = bf16[336,768]{1,0:T(8,128)(2,1)} async-done(((bf16[5376,768]{1,0:T(8,128)(2,1)}), bf16[336,768]{1,0:T(8,128)(2,1)}) %reduce-scatter.4.cloned.1.call-update) | async-done | bytes 516112
  316.0 1.6 fusion.14
  317.6 1.8 slice_bitcast_fusion.10
  (6 shorter events, 0.1 us)
Async XLA Ops:
  7.2 79.2 %all-gather.3.cloned.1.call-start = ((), (), s32[]{:S(2)}) async-start(), calls=%async_computation.2 | async-start | bytes 6193152 | tf_op jit(solution)/shard_map/all_gather | solution.py:113
  20.4 123.2 %all-gather.5.cloned.1.call-start = ((), (), s32[]{:S(2)}) async-start(), calls=%async_computation.3 | async-start | bytes 8773632 | tf_op jit(solution)/shard_map/all_gather | solution.py:116
  22.4 293.7 %reduce-scatter.4.cloned.1.call-start = ((), (), s32[]{:S(2)}) async-start(), calls=%async_computation.4 | async-start | bytes 8773632
  143.5 19.3 %copy-start = (bf16[2,256,5376]{1,2,0:T(8,128)(2,1)S(1)}, bf16[2,256,5376]{1,2,0:T(8,128)(2,1)}, u32[]{:S(2)}) copy-start(bf16[2,256,5376]{1,2,0:T(8,128)(2,1)} %all-gather.3.cloned.1.call-done) | copy-start | bytes 16515076
  148.7 17.6 %collective-permute-start.3 = (bf16[256,256]{1,0:T(8,128)(2,1)S(1)}, bf16[256,256]{1,0:T(8,128)(2,1)S(1)}, u32[]{:S(2)}, u32[]{:S(2)}) collective-permute-start(bf16[256,256]{1,0:T(8,128)(2,1)S(1)} %slice.65), channel_id=1, source_target_pairs={{0,16},{16,32},{32,48},{48,64},{64,80},{80,96},{96,112},{112,128},... | collective-permute-start | bytes 393224 | tf_op jit(solution)/shard_map/ppermute | solution.py:25
  150.8 15.4 %collective-permute-start.2 = (bf16[256,256]{1,0:T(8,128)(2,1)S(1)}, bf16[256,256]{1,0:T(8,128)(2,1)S(1)}, u32[]{:S(2)}, u32[]{:S(2)}) collective-permute-start(bf16[256,256]{1,0:T(8,128)(2,1)S(1)} %slice.65), channel_id=1, source_target_pairs={{0,32},{16,48},{32,64},{48,80},{64,96},{80,112},{96,128},{112,144}... | collective-permute-start | bytes 393224 | tf_op jit(solution)/shard_map/ppermute | solution.py:25
  154.1 12.1 %collective-permute-start.1 = (bf16[256,256]{1,0:T(8,128)(2,1)S(1)}, bf16[256,256]{1,0:T(8,128)(2,1)S(1)}, u32[]{:S(2)}, u32[]{:S(2)}) collective-permute-start(bf16[256,256]{1,0:T(8,128)(2,1)S(1)} %slice.65), channel_id=1, source_target_pairs={{0,48},{16,64},{32,80},{48,96},{64,112},{80,128},{96,144},{112,160... | collective-permute-start | bytes 393224 | tf_op jit(solution)/shard_map/ppermute | solution.py:25
  157.9 8.3 %collective-permute-start = (bf16[256,256]{1,0:T(8,128)(2,1)S(1)}, bf16[256,256]{1,0:T(8,128)(2,1)S(1)}, u32[]{:S(2)}, u32[]{:S(2)}) collective-permute-start(bf16[256,256]{1,0:T(8,128)(2,1)S(1)} %slice.65), channel_id=1, source_target_pairs={{0,64},{16,80},{32,96},{48,112},{64,128},{80,144},{96,160},{112,17... | collective-permute-start | bytes 393224 | tf_op jit(solution)/shard_map/ppermute | solution.py:25
  167.0 0.9 copy-start.1
  174.6 17.5 %slice-start = ((s8[5505024]{0:T(1024)(128)(4,1)}), s8[4194304]{0:T(1024)(128)(4,1)S(1)}, s32[]{:S(2)}) async-start(s8[5505024]{0:T(1024)(128)(4,1)} %bitcast.26), calls=%async_computation.5 | async-start | bytes 8388608
  176.0 8.2 %collective-permute-start.4 = (f32[256,256]{1,0:T(8,128)S(1)}, f32[256,256]{1,0:T(8,128)S(1)}, u32[]{:S(2)}, u32[]{:S(2)}) collective-permute-start(f32[256,256]{1,0:T(8,128)S(1)} %get-tuple-element.26), channel_id=1, source_target_pairs={{16,0},{32,16},{48,32},{64,48},{80,64},{96,80},{112,96},{128,112},... | collective-permute-start | bytes 786440 | tf_op jit(solution)/shard_map/ppermute | solution.py:25
  177.5 12.7 %collective-permute-start.7 = (f32[256,256]{1,0:T(8,128)S(1)}, f32[256,256]{1,0:T(8,128)S(1)}, u32[]{:S(2)}, u32[]{:S(2)}) collective-permute-start(f32[256,256]{1,0:T(8,128)S(1)} %get-tuple-element.27), channel_id=1, source_target_pairs={{64,0},{80,16},{96,32},{112,48},{128,64},{144,80},{160,96},{176,11... | collective-permute-start | bytes 786440 | tf_op jit(solution)/shard_map/ppermute | solution.py:25
  178.8 11.4 %collective-permute-start.6 = (f32[256,256]{1,0:T(8,128)S(1)}, f32[256,256]{1,0:T(8,128)S(1)}, u32[]{:S(2)}, u32[]{:S(2)}) collective-permute-start(f32[256,256]{1,0:T(8,128)S(1)} %get-tuple-element.28), channel_id=1, source_target_pairs={{48,0},{64,16},{80,32},{96,48},{112,64},{128,80},{144,96},{160,112... | collective-permute-start | bytes 786440 | tf_op jit(solution)/shard_map/ppermute | solution.py:25
  180.1 11.1 %collective-permute-start.5 = (f32[256,256]{1,0:T(8,128)S(1)}, f32[256,256]{1,0:T(8,128)S(1)}, u32[]{:S(2)}, u32[]{:S(2)}) collective-permute-start(f32[256,256]{1,0:T(8,128)S(1)} %get-tuple-element.29), channel_id=1, source_target_pairs={{32,0},{48,16},{64,32},{80,48},{96,64},{112,80},{128,96},{144,112}... | collective-permute-start | bytes 786440 | tf_op jit(solution)/shard_map/ppermute | solution.py:25
  181.4 10.8 %slice-start.1 = ((s8[5505024]{0:T(1024)(128)(4,1)}), s8[1310720]{0:T(1024)(128)(4,1)S(1)}, s32[]{:S(2)}) async-start(s8[5505024]{0:T(1024)(128)(4,1)} %bitcast.26), calls=%async_computation.6 | async-start | bytes 2621440
  181.4 10.8 %copy-start.2 = (bf16[256,256]{1,0:T(8,128)(2,1)S(1)}, bf16[256,256]{1,0:T(8,128)(2,1)}, u32[]{:S(2)}) copy-start(bf16[256,256]{1,0:T(8,128)(2,1)} %get-tuple-element.8) | copy-start | bytes 393220
Sparse Core Ops, SparseCore 0:
  20.5 65.8 all-gather.2
  88.2 55.2 all-gather.4
  214.3 101.7 reduce-scatter.3

commit v3 on v2

--- a/solution.py
+++ b/solution.py
@@ -88,6 +88,29 @@
     )(query, d_attn, kv_ext, listed)
 
 
+def weight_terms_kernel(tok_ref, cot_ref, ga_ref, attn_ref, out_ref):
+    n_act = ga_ref.shape[1]
+    out_ref[:, :n_act] = _nn(tok_ref[...], ga_ref[...]).astype(out_ref.dtype)
+    out_ref[:, n_act:] = _nn(cot_ref[...], attn_ref[...]).astype(out_ref.dtype)
+
+
+def weight_terms(tokens_t, cot_t, grad_act, attn, block=768):
+    feats, rows = tokens_t.shape
+    n_act, n_attn = grad_act.shape[1], attn.shape[1]
+    return pl.pallas_call(
+        weight_terms_kernel,
+        grid=(feats // block,),
+        in_specs=[
+            pl.BlockSpec((block, rows), lambda i: (i, 0)),
+            pl.BlockSpec((block, rows), lambda i: (i, 0)),
+            pl.BlockSpec((rows, n_act), lambda i: (0, 0)),
+            pl.BlockSpec((rows, n_attn), lambda i: (0, 0)),
+        ],
+        out_specs=pl.BlockSpec((block, n_act + n_attn), lambda i: (i, 0)),
+        out_shape=jax.ShapeDtypeStruct((feats, n_act + n_attn), jnp.bfloat16),
+    )(tokens_t, cot_t, grad_act, attn)
+
+
 def contract_cols(left, right):
     return lax.dot_general(
         left, right, (((1,), (1,)), ((), ())), preferred_element_type=jnp.float32
@@ -140,14 +163,8 @@
     cols = token_term.shape[1] // n_tp
     parts = lax.all_to_all(token_term.reshape(tok_rows, n_tp, cols), TP, 1, 1, tiled=True)
     grad_tokens = parts.astype(jnp.float32).sum(axis=1).astype(jnp.bfloat16)
-    weight_terms = jnp.concatenate(
-        [
-            term_maker(full_tokens, grad_act).astype(jnp.bfloat16),
-            term_maker(full_cot, attn).astype(jnp.bfloat16),
-        ],
-        axis=1,
-    )
-    summed = lax.psum_scatter(weight_terms, SEQ, scatter_dimension=0, tiled=True)
+    weight_parts = weight_terms(full_tokens.T, full_cot.T, grad_act, attn)
+    summed = lax.psum_scatter(weight_parts, SEQ, scatter_dimension=0, tiled=True)
     grad_query = summed[:, :n_q]
     grad_key = summed[:, n_q : n_q + n_kv]
     grad_value = summed[:, n_q + n_kv : n_proj]

time: 328 us -> 314 us (0.957)
  Pallas kernels: 6.73 us -> 16.1 us
  matrix products: 19.6 us -> 12.7 us
  local copies, waits for them, and re-layouts: 21.4 us -> 15 us
  other arithmetic: 12 us -> 6.52 us
    reduce_scatter x0 -> x1, waiting for transfers between devices: none -> 22 us  [shards(): lax.psum_scatter(weight_parts, SEQ, scatter_dimension=0, tiled=True)]
    unnamed x4 -> x3, waiting for transfers between devices: 18.7 us -> 0.05 us
    unnamed x17 -> x12, local copies, waits for them, and re-layouts: 13.1 us -> 1.59 us
    pallas_call x0 -> x1, Pallas kernels: none -> 9.32 us  [weight_terms(): pl.pallas_call(weight_terms_kernel, grid=(feats // block,), in_specs=[pl....]
    dot_general x2 -> x0, matrix products: 6.96 us -> none  [term_maker(): lax.dot_general(left, right, (((0,), (0,)), ((), ())), preferred_element_...]
    concatenate x1, other arithmetic: 6.27 us -> 0.73 us  [shards(): grad_act = jnp.concatenate([grad_q, grad_kv], axis=1)]
    transpose x0 -> x1, local copies, waits for them, and re-layouts: none -> 5.36 us  [shards(): weight_parts = weight_terms(full_tokens.T, full_cot.T, grad_act, attn)]
    ppermute x8, waiting for transfers between devices: 6.94 us -> 2.98 us  [from_behind(): return lax.ppermute(block, axis, route)]
  transfers between devices with their start and end apart: 11 -> 11, of which waited for: 5 -> 5; matrix products, arithmetic and copies ran while one was open for 5% -> 6% of each run, Pallas kernels for 0% -> 0%
where the time goes in v3:
time: 314 us; the launch traced here: 313 us
  waiting for transfers between devices  145 us (46%)
  blocking collectives  85.2 us (27%)
  starting transfers between devices  18.8 us (6%)
  Pallas kernels  16.1 us (5%)
  local copies, waits for them, and re-layouts  15 us (5%)
  between operations  13.9 us (4%)
  matrix products  12.7 us (4%)
  other arithmetic  6.52 us (2%)
    all_to_all x1, blocking collectives, shards(): lax.all_to_all(token_term.reshape(tok_rows, n_tp, cols), TP, 1, 1, tiled=...  73.1 us
    all_gather x1, waiting for transfers between devices, shards(): pair = lax.all_gather(pair, 'z', axis=2, tiled=True)  62.6 us
    all_gather x1, waiting for transfers between devices, shards(): w_full = lax.all_gather(w_cat, SEQ, axis=0, tiled=True)  57.1 us
    reduce_scatter x1, waiting for transfers between devices, shards(): lax.psum_scatter(weight_parts, SEQ, scatter_dimension=0, tiled=True)  22 us
    ppermute x8, starting transfers between devices, from_behind(): return lax.ppermute(block, axis, route)  18.7 us
    all_gather x1, blocking collectives, shards(): pair = lax.all_gather(pair, 'yhi', axis=2, tiled=True)  12.1 us
    pallas_call x1, Pallas kernels, weight_terms(): pl.pallas_call(weight_terms_kernel, grid=(feats // block,), in_specs=[pl....  9.32 us
    pallas_call x1, Pallas kernels, fused_attention(): pl.pallas_call(body, out_shape=(jax.ShapeDtypeStruct(query.shape, jnp.bfl...  6.73 us
  transfers between devices with their start and end apart: 11, of which 5 were waited for; matrix products, arithmetic and copies ran while one was open for 6% of the time, Pallas kernels for 0%

profile of v3, /device:TPU:128, one launch (start us, length us, event | category | flops | bytes accessed | tf_op | source)
XLA Modules:
  0.0 312.9 jit_solution(12960198749644447600)
XLA Ops:
  7.2 0.0 all-gather.3.cloned.1.call-start
  7.2 1.0 pad_maximum_fusion.1
  8.2 12.1 %all_gather.9 = bf16[2,256,672]{1,2,0:T(8,128)(2,1)} all-gather(bf16[2,256,336]{1,2,0:T(8,128)(2,1)S(1)} %pad_maximum_fusion.1), channel_id=1, replica_groups=mesh['ylo'=2,'x'=4,'core'=2,'z'=8,'yhi'=2] {'yhi'}, dimensions={2}, use_global_device_ids=true | all-gather | bytes 1032192 | tf_op jit(solution)/shard_map/all_gather | solution.py:135
  20.3 0.0 all-gather.3.cloned.1.call-update
  20.4 0.0 all-gather.5.cloned.1.call-start
  20.4 1.9 pad_maximum_fusion
  22.3 0.0 all-gather.5.cloned.1.call-update
  22.4 0.0 reduce-scatter.2.cloned.1.call-start
  22.4 0.7 compare_convert_fusion
  23.1 0.1 broadcast_bitcast_fusion
  23.2 0.6 copy.15
  23.8 62.6 %all-gather.3.cloned.1.call-done = bf16[2,256,5376]{1,2,0:T(8,128)(2,1)} async-done(((bf16[2,256,672]{1,2,0:T(8,128)(2,1)}), bf16[2,256,5376]{1,2,0:T(8,128)(2,1)}) %all-gather.3.cloned.1.call-update) | async-done | bytes 5505040 | tf_op jit(solution)/shard_map/all_gather | solution.py:136
  86.4 57.1 %all-gather.5.cloned.1.call-done = bf16[5376,768]{1,0:T(8,128)(2,1)} async-done(((bf16[336,768]{1,0:T(8,128)(2,1)}), bf16[5376,768]{1,0:T(8,128)(2,1)}) %all-gather.5.cloned.1.call-update) | async-done | bytes 8257552 | tf_op jit(solution)/shard_map/all_gather | solution.py:139
  143.5 0.0 copy-start
  143.5 5.1 %fusion.9 = bf16[256,512]{1,0:T(8,128)(2,1)S(1)} fusion(bf16[5376,768]{1,0:T(8,128)(2,1)} %all-gather.5.cloned.1.call-done, bf16[2,256,5376]{1,2,0:T(8,128)(2,1)} %all-gather.3.cloned.1.call-done), kind=kOutput, calls=%fused_computation.12 | convolution fusion | flops 1409417216 | bytes 8519680 | tf_op jit(solution)/shard_map/dot_general | solution.py:144
  148.7 4.5 %collective-permute-start = (bf16[256,256]{1,0:T(8,128)(2,1)S(1)}, bf16[256,256]{1,0:T(8,128)(2,1)S(1)}, u32[]{:S(2)}, u32[]{:S(2)}) collective-permute-start(bf16[256,256]{1,0:T(8,128)(2,1)S(1)} %slice.65), channel_id=1, source_target_pairs={{0,64},{16,80},{32,96},{48,112},{64,128},{80,144},{96,160},{112,17... | collective-permute-start | bytes 393224 | tf_op jit(solution)/shard_map/ppermute | solution.py:25
  153.2 2.3 collective-permute-start.1
  155.5 2.8 collective-permute-start.2
  158.4 3.7 %collective-permute-start.3 = (bf16[256,256]{1,0:T(8,128)(2,1)S(1)}, bf16[256,256]{1,0:T(8,128)(2,1)S(1)}, u32[]{:S(2)}, u32[]{:S(2)}) collective-permute-start(bf16[256,256]{1,0:T(8,128)(2,1)S(1)} %slice.65), channel_id=1, source_target_pairs={{0,16},{16,32},{32,48},{48,64},{64,80},{80,96},{96,112},{112,128},... | collective-permute-start | bytes 393224 | tf_op jit(solution)/shard_map/ppermute | solution.py:25
  162.1 0.0 copy-done
  162.1 3.4 %fusion.14.d_ref = bf16[256,256]{1,0:T(8,128)(2,1)} fusion(bf16[5376,768]{1,0:T(8,128)(2,1)} %all-gather.5.cloned.1.call-done, bf16[2,256,5376]{1,2,0:T(8,128)(2,1)S(1)} %copy-done), kind=kOutput, calls=%fused_computation.13 | convolution fusion | flops 704708608 | bytes 5636096 | tf_op jit(solution)/shard_map/dot_general | solution.py:141
  165.5 0.0 collective-permute-done
  165.5 0.0 collective-permute-done.1
  165.5 0.0 collective-permute-done.2
  165.5 0.0 collective-permute-done.3
  165.6 0.7 constant_dynamic-update-slice_fusion
  166.2 0.0 copy-start.1
  166.2 0.9 copy-done.1
  167.1 6.7 %shard_map.110 = (bf16[256,256]{1,0:T(8,128)(2,1)}, bf16[256,256]{1,0:T(8,128)(2,1)}, f32[1280,256]{1,0:T(8,128)}) custom-call(bf16[256,256]{1,0:T(8,128)(2,1)} %get-tuple-element.22.q_ref, bf16[256,256]{1,0:T(8,128)(2,1)} %fusion.14.d_ref, bf16[1280,256]{1,0:T(8,128)(2,1)} %copy-done.1, f32[2,1152]{1,0:T(2,128)} %bitcast.31), custom_call_target="tpu_custom_call" | custom-call | tf_op jit(solution)/shard_map/pallas_call | solution.py:81
  173.8 1.3 fusion.19
  175.1 1.3 collective-permute-start.7
  176.4 1.3 collective-permute-start.6
  177.7 1.3 collective-permute-start.5
  179.0 0.0 copy-start.2
  179.0 1.4 collective-permute-start.4
  180.4 5.4 %slice_bitcast_fusion = (bf16[5376,256]{1,0:T(8,128)(2,1)}, bf16[5376,256]{1,0:T(8,128)(2,1)}) fusion(bf16[2,256,5376]{1,2,0:T(8,128)(2,1)} %all-gather.3.cloned.1.call-done), kind=kLoop, calls=%fused_computation.8 | loop fusion | bytes 11010048 | tf_op jit(solution)/shard_map/transpose | solution.py:166
  185.8 1.3 collective-permute-done.7
  187.1 0.0 collective-permute-done.6
  187.1 1.7 collective-permute-done.5
  188.8 0.0 collective-permute-done.4
  188.8 1.0 add_convert_fusion
  189.8 0.0 copy-done.2
  189.8 0.7 pad_maximum_fusion.2.ga_ref
  190.5 9.3 %shard_map.111 = bf16[5376,768]{1,0:T(8,128)(2,1)} custom-call(bf16[5376,256]{1,0:T(8,128)(2,1)} %get-tuple-element.12.tok_ref, bf16[5376,256]{1,0:T(8,128)(2,1)} %get-tuple-element.11.cot_ref, bf16[256,512]{1,0:T(8,128)(2,1)} %pad_maximum_fusion.2.ga_ref, bf16[256,256]{1,0:T(8,128)(2,1)} %get-tuple-element.10.attn_ref), custom_call_target="tpu_custom_call" | custom-call | tf_op jit(solution)/shard_map/pallas_call | solution.py:100
  199.9 0.0 reduce-scatter.2.cloned.1.call-update
  199.9 4.2 %convolution_convert_fusion = bf16[256,5376]{1,0:T(8,128)(2,1)S(1)} fusion(bf16[5376,768]{1,0:T(8,128)(2,1)} %all-gather.5.cloned.1.call-done, bf16[256,256]{1,0:T(8,128)(2,1)S(1)} %add_convert_fusion, bf16[256,256]{1,0:T(8,128)(2,1)S(1)} %copy-done.2), kind=kOutput, calls=%fused_computation | convolution fusion | flops 1411186688 | bytes 8519680 | tf_op jit(solution)/shard_map/dot_general | solution.py:115
  204.1 2.8 copy.12
  206.9 73.1 %all_to_all.5 = bf16[256,16,336]{0,2,1:T(8,128)(2,1)S(1)} all-to-all(bf16[256,16,336]{0,2,1:T(8,128)(2,1)} %bitcast.27), channel_id=1, replica_groups=mesh['ylo'=2,'x'=4,'core'=2,'z'=8,'yhi'=2] {'z','yhi'}, dimensions={1} | all-to-all | bytes 5505024 | tf_op jit(solution)/shard_map/all_to_all | solution.py:164
  280.0 1.1 reduce_sum.12
  281.1 22.0 %reduce-scatter.2.cloned.1.call-done = bf16[336,768]{1,0:T(8,128)(2,1)} async-done(((bf16[5376,768]{1,0:T(8,128)(2,1)}), bf16[336,768]{1,0:T(8,128)(2,1)}) %reduce-scatter.2.cloned.1.call-update) | async-done | bytes 516112 | tf_op jit(solution)/shard_map/reduce_scatter | solution.py:167
  303.1 1.8 slice_bitcast_fusion.2
  304.8 1.6 fusion.20
  (5 shorter events, 0.1 us)
Async XLA Ops:
  7.2 79.2 %all-gather.3.cloned.1.call-start = ((), (), s32[]{:S(2)}) async-start(), calls=%async_computation.2 | async-start | bytes 6193152 | tf_op jit(solution)/shard_map/all_gather | solution.py:136
  20.4 123.2 %all-gather.5.cloned.1.call-start = ((), (), s32[]{:S(2)}) async-start(), calls=%async_computation.3 | async-start | bytes 8773632 | tf_op jit(solution)/shard_map/all_gather | solution.py:139
  22.4 280.7 %reduce-scatter.2.cloned.1.call-start = ((), (), s32[]{:S(2)}) async-start(), calls=%async_computation.4 | async-start | bytes 8773632 | tf_op jit(solution)/shard_map/reduce_scatter | solution.py:167
  143.5 18.6 %copy-start = (bf16[2,256,5376]{1,2,0:T(8,128)(2,1)S(1)}, bf16[2,256,5376]{1,2,0:T(8,128)(2,1)}, u32[]{:S(2)}) copy-start(bf16[2,256,5376]{1,2,0:T(8,128)(2,1)} %all-gather.3.cloned.1.call-done) | copy-start | bytes 16515076
  148.7 16.8 %collective-permute-start = (bf16[256,256]{1,0:T(8,128)(2,1)S(1)}, bf16[256,256]{1,0:T(8,128)(2,1)S(1)}, u32[]{:S(2)}, u32[]{:S(2)}) collective-permute-start(bf16[256,256]{1,0:T(8,128)(2,1)S(1)} %slice.65), channel_id=1, source_target_pairs={{0,64},{16,80},{32,96},{48,112},{64,128},{80,144},{96,160},{112,17... | collective-permute-start | bytes 393224 | tf_op jit(solution)/shard_map/ppermute | solution.py:25
  153.2 12.3 %collective-permute-start.1 = (bf16[256,256]{1,0:T(8,128)(2,1)S(1)}, bf16[256,256]{1,0:T(8,128)(2,1)S(1)}, u32[]{:S(2)}, u32[]{:S(2)}) collective-permute-start(bf16[256,256]{1,0:T(8,128)(2,1)S(1)} %slice.65), channel_id=1, source_target_pairs={{0,48},{16,64},{32,80},{48,96},{64,112},{80,128},{96,144},{112,160... | collective-permute-start | bytes 393224 | tf_op jit(solution)/shard_map/ppermute | solution.py:25
  155.5 10.0 %collective-permute-start.2 = (bf16[256,256]{1,0:T(8,128)(2,1)S(1)}, bf16[256,256]{1,0:T(8,128)(2,1)S(1)}, u32[]{:S(2)}, u32[]{:S(2)}) collective-permute-start(bf16[256,256]{1,0:T(8,128)(2,1)S(1)} %slice.65), channel_id=1, source_target_pairs={{0,32},{16,48},{32,64},{48,80},{64,96},{80,112},{96,128},{112,144}... | collective-permute-start | bytes 393224 | tf_op jit(solution)/shard_map/ppermute | solution.py:25
  158.4 7.2 %collective-permute-start.3 = (bf16[256,256]{1,0:T(8,128)(2,1)S(1)}, bf16[256,256]{1,0:T(8,128)(2,1)S(1)}, u32[]{:S(2)}, u32[]{:S(2)}) collective-permute-start(bf16[256,256]{1,0:T(8,128)(2,1)S(1)} %slice.65), channel_id=1, source_target_pairs={{0,16},{16,32},{32,48},{48,64},{64,80},{80,96},{96,112},{112,128},... | collective-permute-start | bytes 393224 | tf_op jit(solution)/shard_map/ppermute | solution.py:25
  166.2 0.9 copy-start.1
  175.1 12.0 %collective-permute-start.7 = (f32[256,256]{1,0:T(8,128)S(1)}, f32[256,256]{1,0:T(8,128)S(1)}, u32[]{:S(2)}, u32[]{:S(2)}) collective-permute-start(f32[256,256]{1,0:T(8,128)S(1)} %get-tuple-element.14), channel_id=1, source_target_pairs={{64,0},{80,16},{96,32},{112,48},{128,64},{144,80},{160,96},{176,11... | collective-permute-start | bytes 786440 | tf_op jit(solution)/shard_map/ppermute | solution.py:25
  176.4 10.7 %collective-permute-start.6 = (f32[256,256]{1,0:T(8,128)S(1)}, f32[256,256]{1,0:T(8,128)S(1)}, u32[]{:S(2)}, u32[]{:S(2)}) collective-permute-start(f32[256,256]{1,0:T(8,128)S(1)} %get-tuple-element.15), channel_id=1, source_target_pairs={{48,0},{64,16},{80,32},{96,48},{112,64},{128,80},{144,96},{160,112... | collective-permute-start | bytes 786440 | tf_op jit(solution)/shard_map/ppermute | solution.py:25
  177.7 11.1 %collective-permute-start.5 = (f32[256,256]{1,0:T(8,128)S(1)}, f32[256,256]{1,0:T(8,128)S(1)}, u32[]{:S(2)}, u32[]{:S(2)}) collective-permute-start(f32[256,256]{1,0:T(8,128)S(1)} %get-tuple-element.16), channel_id=1, source_target_pairs={{32,0},{48,16},{64,32},{80,48},{96,64},{112,80},{128,96},{144,112}... | collective-permute-start | bytes 786440 | tf_op jit(solution)/shard_map/ppermute | solution.py:25
  179.0 10.8 %copy-start.2 = (bf16[256,256]{1,0:T(8,128)(2,1)S(1)}, bf16[256,256]{1,0:T(8,128)(2,1)}, u32[]{:S(2)}) copy-start(bf16[256,256]{1,0:T(8,128)(2,1)} %get-tuple-element.8) | copy-start | bytes 393220
  179.0 9.8 %collective-permute-start.4 = (f32[256,256]{1,0:T(8,128)S(1)}, f32[256,256]{1,0:T(8,128)S(1)}, u32[]{:S(2)}, u32[]{:S(2)}) collective-permute-start(f32[256,256]{1,0:T(8,128)S(1)} %get-tuple-element.13), channel_id=1, source_target_pairs={{16,0},{32,16},{48,32},{64,48},{80,64},{96,80},{112,96},{128,112},... | collective-permute-start | bytes 786440 | tf_op jit(solution)/shard_map/ppermute | solution.py:25
Sparse Core Ops, SparseCore 0:
  20.5 65.8 all-gather.2
  88.2 55.2 all-gather.4
  200.0 102.9 reduce-scatter.1

commit v4 on v3

--- a/solution.py
+++ b/solution.py
@@ -17,6 +17,18 @@
 TP = ("z", "yhi")
 SEQ_SPLIT = (2, 4, 2)
 TP_SPLIT = (8, 2)
+
+
+def ring_gather(block, axis, dim):
+    size = lax.psum(1, axis)
+    right, left = [block], [block]
+    for _ in range(size // 2):
+        right.append(lax.ppermute(right[-1], axis, [(i, (i + 1) % size) for i in range(size)]))
+    for _ in range((size - 1) // 2):
+        left.append(lax.ppermute(left[-1], axis, [(i, (i - 1) % size) for i in range(size)]))
+    ordered = left + [right[k] for k in range(size // 2, 0, -1)]
+    relative = jnp.concatenate(ordered, axis=dim)
+    return jnp.roll(relative, lax.axis_index(axis) * block.shape[dim], axis=dim)
 
 
 def from_behind(block, axis, distance):
@@ -133,7 +145,7 @@
     n_proj = n_q + 2 * n_kv
     pair = jnp.stack([tokens, cotangent])
     pair = lax.all_gather(pair, "yhi", axis=2, tiled=True)
-    pair = lax.all_gather(pair, "z", axis=2, tiled=True)
+    pair = ring_gather(pair, "z", 2)
     full_tokens, full_cot = pair[0], pair[1]
     w_cat = jnp.concatenate([w_query, w_key, w_value, w_out.T], axis=1)
     w_full = lax.all_gather(w_cat, SEQ, axis=0, tiled=True)

time: 314 us -> 274 us (0.87)
  waiting for transfers between devices: 145 us -> 71.2 us
  local copies, waits for them, and re-layouts: 15 us -> 37.2 us
  starting transfers between devices: 18.8 us -> 28.6 us
    all_gather x1 -> x0, waiting for transfers between devices: 62.6 us -> none  [shards(): pair = lax.all_gather(pair, 'z', axis=2, tiled=True)]
    all_gather x1, waiting for transfers between devices: 57.1 us -> 0.01 us  [shards(): w_full = lax.all_gather(w_cat, SEQ, axis=0, tiled=True)]
    ppermute x0 -> x7, waiting for transfers between devices: none -> 48.2 us  [the longest x4 48.2 us: ring_gather(): lax.ppermute(right[-1], axis, [(i, (i + 1) % size) for i in range(size)])]
    unnamed x12 -> x25, local copies, waits for them, and re-layouts: 1.59 us -> 21.9 us
    ppermute x0 -> x7, starting transfers between devices: none -> 9.71 us  [the longest x3 8.69 us: ring_gather(): lax.ppermute(left[-1], axis, [(i, (i - 1) % size) for i in range(size)])]
    reduce_scatter x1, waiting for transfers between devices: 22 us -> 15 us  [shards(): lax.psum_scatter(weight_parts, SEQ, scatter_dimension=0, tiled=True)]
    ppermute x8, waiting for transfers between devices: 2.98 us -> 8 us  [from_behind(): return lax.ppermute(block, axis, route)]
  transfers between devices with their start and end apart: 11 -> 17, of which waited for: 5 -> 8; matrix products, arithmetic and copies ran while one was open for 6% -> 15% of each run, Pallas kernels for 0% -> 0%
where the time goes in v4:
time: 274 us; the launch traced here: 273 us
  blocking collectives  85.3 us (31%)
  waiting for transfers between devices  71.2 us (26%)
  local copies, waits for them, and re-layouts  37.2 us (14%)
  starting transfers between devices  28.6 us (10%)
  Pallas kernels  16.2 us (6%)
  between operations  14.2 us (5%)
  matrix products  13.4 us (5%)
  other arithmetic  6.49 us (2%)
    all_to_all x1, blocking collectives, shards(): lax.all_to_all(token_term.reshape(tok_rows, n_tp, cols), TP, 1, 1, tiled=...  73.4 us
    ppermute x4, waiting for transfers between devices, ring_gather(): lax.ppermute(right[-1], axis, [(i, (i + 1) % size) for i in range(size)])  48.2 us
    unnamed x25, local copies, waits for them, and re-layouts  21.9 us
    ppermute x8, starting transfers between devices, from_behind(): return lax.ppermute(block, axis, route)  18.9 us
    reduce_scatter x1, waiting for transfers between devices, shards(): lax.psum_scatter(weight_parts, SEQ, scatter_dimension=0, tiled=True)  15 us
    all_gather x1, blocking collectives, shards(): pair = lax.all_gather(pair, 'yhi', axis=2, tiled=True)  12 us
    pallas_call x1, Pallas kernels, weight_terms(): pl.pallas_call(weight_terms_kernel, grid=(feats // block,), in_specs=[pl....  9.36 us
    ppermute x3, starting transfers between devices, ring_gather(): lax.ppermute(left[-1], axis, [(i, (i - 1) % size) for i in range(size)])  8.69 us
  transfers between devices with their start and end apart: 17, of which 8 were waited for; matrix products, arithmetic and copies ran while one was open for 15% of the time, Pallas kernels for 0%

profile of v4, /device:TPU:128, one launch (start us, length us, event | category | flops | bytes accessed | tf_op | source)
XLA Modules:
  0.0 272.7 jit_solution(12928739933771277043)
XLA Ops:
  7.2 0.0 all-gather.2.cloned.1.call-start
  7.2 1.9 pad_maximum_fusion
  9.1 0.0 all-gather.2.cloned.1.call-update
  9.2 0.0 reduce-scatter.2.cloned.1.call-start
  9.2 1.0 pad_maximum_fusion.1
  10.2 12.0 %all_gather.6 = bf16[2,256,672]{1,2,0:T(8,128)(2,1)S(1)} all-gather(bf16[2,256,336]{1,2,0:T(8,128)(2,1)S(1)} %pad_maximum_fusion.1), channel_id=1, replica_groups=mesh['ylo'=2,'x'=4,'core'=2,'z'=8,'yhi'=2] {'yhi'}, dimensions={2}, use_global_device_ids=true | all-gather | bytes 1032192 | tf_op jit(solution)/shard_map/all_gather | solution.py:147
  22.2 1.0 collective-permute-start.3
  23.2 2.2 collective-permute-start
  25.5 14.3 %collective-permute-done.3 = bf16[2,256,672]{1,2,0:T(8,128)(2,1)S(1)} collective-permute-done((bf16[2,256,672]{1,2,0:T(8,128)(2,1)S(1)}, bf16[2,256,672]{1,2,0:T(8,128)(2,1)S(1)}, u32[]{:S(2)}, u32[]{:S(2)}) %collective-permute-start.3) | collective-permute-done | bytes 688160 | tf_op jit(solution)/shard_map/ppermute | solution.py:26
  39.7 3.2 %collective-permute-start.1 = (bf16[2,256,672]{1,2,0:T(8,128)(2,1)S(1)}, bf16[2,256,672]{1,2,0:T(8,128)(2,1)}, u32[]{:S(2)}, u32[]{:S(2)}) collective-permute-start(bf16[2,256,672]{1,2,0:T(8,128)(2,1)S(1)} %collective-permute-done), channel_id=1, source_target_pairs={{0,14},{2,0},{4,2},{6,4},{8,6},{10,8},{12,10},{14,12},{1,15},{3,1}... | collective-permute-start | bytes 2064392 | tf_op jit(solution)/shard_map/ppermute | solution.py:28
  43.0 13.4 %collective-permute-done.4 = bf16[2,256,672]{1,2,0:T(8,128)(2,1)S(1)} collective-permute-done((bf16[2,256,672]{1,2,0:T(8,128)(2,1)S(1)}, bf16[2,256,672]{1,2,0:T(8,128)(2,1)S(1)}, u32[]{:S(2)}, u32[]{:S(2)}) %collective-permute-start.4) | collective-permute-done | bytes 688160 | tf_op jit(solution)/shard_map/ppermute | solution.py:26
  56.4 0.0 collective-permute-done.1
  56.4 3.2 %collective-permute-start.2 = (bf16[2,256,672]{1,2,0:T(8,128)(2,1)}, bf16[2,256,672]{1,2,0:T(8,128)(2,1)}, u32[]{:S(2)}, u32[]{:S(2)}) collective-permute-start(bf16[2,256,672]{1,2,0:T(8,128)(2,1)} %collective-permute-done.1), channel_id=1, source_target_pairs={{0,14},{2,0},{4,2},{6,4},{8,6},{10,8},{12,10},{14,12},{1,15},{3,1}... | collective-permute-start | bytes 2064392 | tf_op jit(solution)/shard_map/ppermute | solution.py:28
  59.6 0.7 compare_convert_fusion
  60.3 11.9 %collective-permute-done.5 = bf16[2,256,672]{1,2,0:T(8,128)(2,1)S(1)} collective-permute-done((bf16[2,256,672]{1,2,0:T(8,128)(2,1)S(1)}, bf16[2,256,672]{1,2,0:T(8,128)(2,1)S(1)}, u32[]{:S(2)}, u32[]{:S(2)}) %collective-permute-start.5) | collective-permute-done | bytes 688160 | tf_op jit(solution)/shard_map/ppermute | solution.py:26
  72.2 0.1 broadcast_bitcast_fusion
  72.3 0.6 copy.15
  72.9 0.9 constant_dynamic-update-slice_fusion.15
  73.8 0.9 constant_dynamic-update-slice_fusion.14
  74.7 2.0 constant_dynamic-update-slice_fusion.13
  76.7 0.0 collective-permute-done.2
  76.7 2.0 constant_dynamic-update-slice_fusion.12
  78.7 8.6 %collective-permute-done.6 = bf16[2,256,672]{1,2,0:T(8,128)(2,1)} collective-permute-done((bf16[2,256,672]{1,2,0:T(8,128)(2,1)S(1)}, bf16[2,256,672]{1,2,0:T(8,128)(2,1)}, u32[]{:S(2)}, u32[]{:S(2)}) %collective-permute-start.6) | collective-permute-done | bytes 688160 | tf_op jit(solution)/shard_map/ppermute | solution.py:26
  87.3 2.0 constant_dynamic-update-slice_fusion.11
  89.3 0.9 constant_dynamic-update-slice_fusion.10
  90.2 0.9 constant_dynamic-update-slice_fusion.9
  91.1 1.0 constant_dynamic-update-slice_fusion.8
  92.0 0.9 constant_dynamic-update-slice_fusion.7
  93.0 1.0 constant_dynamic-update-slice_fusion.6
  93.9 2.0 constant_dynamic-update-slice_fusion.5
  96.0 2.0 constant_dynamic-update-slice_fusion.4
  98.0 2.0 constant_dynamic-update-slice_fusion.3
  100.0 0.9 constant_dynamic-update-slice_fusion.2
  100.9 0.9 constant_dynamic-update-slice_fusion.1
  101.8 0.9 constant_dynamic-update-slice_fusion
  102.7 5.0 %fusion.9 = bf16[256,512]{1,0:T(8,128)(2,1)S(1)} fusion(bf16[5376,768]{1,0:T(8,128)(2,1)} %all-gather.2.cloned.1.call-done, bf16[2,256,10752]{1,2,0:T(8,128)(2,1)} %constant_dynamic-update-slice_fusion, s32[]{:T(128)S(6)} %select_n.14), kind=kOutput, calls=%fused_computation.12 | convolution fusion | flops 1409417216 | bytes 8519684 | tf_op jit(solution)/shard_map/dot_general | solution.py:156
  107.8 4.9 %collective-permute-start.7 = (bf16[256,256]{1,0:T(8,128)(2,1)S(1)}, bf16[256,256]{1,0:T(8,128)(2,1)S(1)}, u32[]{:S(2)}, u32[]{:S(2)}) collective-permute-start(bf16[256,256]{1,0:T(8,128)(2,1)S(1)} %slice.63), channel_id=1, source_target_pairs={{0,64},{16,80},{32,96},{48,112},{64,128},{80,144},{96,160},{112,17... | collective-permute-start | bytes 393224 | tf_op jit(solution)/shard_map/ppermute | solution.py:37
  112.7 1.3 collective-permute-start.8
  114.0 2.5 collective-permute-start.9
  116.5 4.9 %collective-permute-start.10 = (bf16[256,256]{1,0:T(8,128)(2,1)S(1)}, bf16[256,256]{1,0:T(8,128)(2,1)S(1)}, u32[]{:S(2)}, u32[]{:S(2)}) collective-permute-start(bf16[256,256]{1,0:T(8,128)(2,1)S(1)} %slice.63), channel_id=1, source_target_pairs={{0,16},{16,32},{32,48},{48,64},{64,80},{80,96},{96,112},{112,128},... | collective-permute-start | bytes 393224 | tf_op jit(solution)/shard_map/ppermute | solution.py:37
  121.5 4.2 %fusion.14.d_ref = bf16[256,256]{1,0:T(8,128)(2,1)} fusion(bf16[5376,768]{1,0:T(8,128)(2,1)} %all-gather.2.cloned.1.call-done, bf16[2,256,10752]{1,2,0:T(8,128)(2,1)} %constant_dynamic-update-slice_fusion, s32[]{:T(128)S(6)} %add.30, s32[]{:T(128)S(6)} %select_n.14), kind=kOutput, calls=%fused_computation.13 | convolution fusion | flops 704708608 | bytes 5636104 | tf_op jit(solution)/shard_map/dot_general | solution.py:153
  125.8 0.7 constant_dynamic-update-slice_fusion.16
  126.5 0.8 copy-done
  127.3 6.8 %shard_map.110 = (bf16[256,256]{1,0:T(8,128)(2,1)}, bf16[256,256]{1,0:T(8,128)(2,1)}, f32[1280,256]{1,0:T(8,128)}) custom-call(bf16[256,256]{1,0:T(8,128)(2,1)} %get-tuple-element.22.q_ref, bf16[256,256]{1,0:T(8,128)(2,1)} %fusion.14.d_ref, bf16[1280,256]{1,0:T(8,128)(2,1)} %copy-done, f32[2,1152]{1,0:T(2,128)} %bitcast.31), custom_call_target="tpu_custom_call" | custom-call | tf_op jit(solution)/shard_map/pallas_call | solution.py:93
  134.2 1.3 fusion.21
  135.5 1.3 collective-permute-start.11
  136.8 1.3 collective-permute-start.12
  138.1 1.3 collective-permute-start.13
  139.4 1.3 collective-permute-start.14
  140.7 6.2 %dynamic-slice_bitcast_fusion.1 = (bf16[5376,256]{1,0:T(8,128)(2,1)}, bf16[5376,256]{1,0:T(8,128)(2,1)}) fusion(bf16[2,256,10752]{1,2,0:T(8,128)(2,1)} %constant_dynamic-update-slice_fusion, s32[]{:T(128)S(6)} %add.30, s32[]{:T(128)S(6)} %select_n.14), kind=kLoop, calls=%fused_computation.10 | loop fusion | bytes 11010056 | tf_op jit(solution)/shard_map/transpose | solution.py:178
  146.9 3.0 %collective-permute-done.12 = f32[256,256]{1,0:T(8,128)S(1)} collective-permute-done((f32[256,256]{1,0:T(8,128)S(1)}, f32[256,256]{1,0:T(8,128)S(1)}, u32[]{:S(2)}, u32[]{:S(2)}) %collective-permute-start.12) | collective-permute-done | bytes 262176 | tf_op jit(solution)/shard_map/ppermute | solution.py:37
  149.9 1.8 collective-permute-done.13
  151.8 3.1 %collective-permute-done.14 = f32[256,256]{1,0:T(8,128)S(1)} collective-permute-done((f32[256,256]{1,0:T(8,128)S(1)}, f32[256,256]{1,0:T(8,128)S(1)}, u32[]{:S(2)}, u32[]{:S(2)}) %collective-permute-start.14) | collective-permute-done | bytes 262176 | tf_op jit(solution)/shard_map/ppermute | solution.py:37
  154.9 1.0 add_convert_fusion
  155.9 0.7 pad_maximum_fusion.2.ga_ref
  156.6 9.4 %shard_map.111 = bf16[5376,768]{1,0:T(8,128)(2,1)} custom-call(bf16[5376,256]{1,0:T(8,128)(2,1)} %get-tuple-element.12.tok_ref, bf16[5376,256]{1,0:T(8,128)(2,1)} %get-tuple-element.11.cot_ref, bf16[256,512]{1,0:T(8,128)(2,1)} %pad_maximum_fusion.2.ga_ref, bf16[256,256]{1,0:T(8,128)(2,1)} %get-tuple-element.10.attn_ref), custom_call_target="tpu_custom_call" | custom-call | tf_op jit(solution)/shard_map/pallas_call | solution.py:112
  166.0 0.0 reduce-scatter.2.cloned.1.call-update
  166.0 4.2 %convolution_convert_fusion = bf16[256,5376]{1,0:T(8,128)(2,1)S(1)} fusion(bf16[5376,768]{1,0:T(8,128)(2,1)} %all-gather.2.cloned.1.call-done, bf16[256,256]{1,0:T(8,128)(2,1)S(1)} %add_convert_fusion, bf16[256,256]{1,0:T(8,128)(2,1)S(1)} %copy-done.1), kind=kOutput, calls=%fused_computation | convolution fusion | flops 1411186688 | bytes 8519680 | tf_op jit(solution)/shard_map/dot_general | solution.py:127
  170.2 2.8 %copy.12 = bf16[256,5376]{0,1:T(8,128)(2,1)} copy(bf16[256,5376]{1,0:T(8,128)(2,1)S(1)} %convolution_convert_fusion) | data formatting | bytes 5505024 | tf_op jit(solution)/shard_map/convert_element_type | solution.py:173
  173.0 73.4 %all_to_all.5 = bf16[256,16,336]{0,2,1:T(8,128)(2,1)S(1)} all-to-all(bf16[256,16,336]{0,2,1:T(8,128)(2,1)} %bitcast.27), channel_id=1, replica_groups=mesh['ylo'=2,'x'=4,'core'=2,'z'=8,'yhi'=2] {'z','yhi'}, dimensions={1} | all-to-all | bytes 5505024 | tf_op jit(solution)/shard_map/all_to_all | solution.py:176
  246.4 1.1 reduce_sum.12
  247.5 15.0 %reduce-scatter.2.cloned.1.call-done = bf16[336,768]{1,0:T(8,128)(2,1)} async-done(((bf16[5376,768]{1,0:T(8,128)(2,1)}), bf16[336,768]{1,0:T(8,128)(2,1)}) %reduce-scatter.2.cloned.1.call-update) | async-done | bytes 516112 | tf_op jit(solution)/shard_map/reduce_scatter | solution.py:179
  262.5 1.8 slice_bitcast_fusion
  264.2 1.6 fusion.22
  (18 shorter events, 0.1 us)
Async XLA Ops:
  7.2 95.6 %all-gather.2.cloned.1.call-start = ((), (), s32[]{:S(2)}) async-start(), calls=%async_computation.2 | async-start | bytes 8773632 | tf_op jit(solution)/shard_map/all_gather | solution.py:151
  9.2 253.3 %reduce-scatter.2.cloned.1.call-start = ((), (), s32[]{:S(2)}) async-start(), calls=%async_computation.3 | async-start | bytes 8773632 | tf_op jit(solution)/shard_map/reduce_scatter | solution.py:179
  22.2 17.5 %collective-permute-start.3 = (bf16[2,256,672]{1,2,0:T(8,128)(2,1)S(1)}, bf16[2,256,672]{1,2,0:T(8,128)(2,1)S(1)}, u32[]{:S(2)}, u32[]{:S(2)}) collective-permute-start(bf16[2,256,672]{1,2,0:T(8,128)(2,1)S(1)} %all_gather.6), channel_id=1, source_target_pairs={{0,2},{2,4},{4,6},{6,8},{8,10},{10,12},{12,14},{14,0},{1,3},{3,5},... | collective-permute-start | bytes 2064392 | tf_op jit(solution)/shard_map/ppermute | solution.py:26
  23.2 16.5 %collective-permute-start = (bf16[2,256,672]{1,2,0:T(8,128)(2,1)S(1)}, bf16[2,256,672]{1,2,0:T(8,128)(2,1)S(1)}, u32[]{:S(2)}, u32[]{:S(2)}) collective-permute-start(bf16[2,256,672]{1,2,0:T(8,128)(2,1)S(1)} %all_gather.6), channel_id=1, source_target_pairs={{0,14},{2,0},{4,2},{6,4},{8,6},{10,8},{12,10},{14,12},{1,15},{3,1}... | collective-permute-start | bytes 2064392 | tf_op jit(solution)/shard_map/ppermute | solution.py:28
  39.7 16.7 %collective-permute-start.4 = (bf16[2,256,672]{1,2,0:T(8,128)(2,1)S(1)}, bf16[2,256,672]{1,2,0:T(8,128)(2,1)S(1)}, u32[]{:S(2)}, u32[]{:S(2)}) collective-permute-start(bf16[2,256,672]{1,2,0:T(8,128)(2,1)S(1)} %collective-permute-done.3), channel_id=1, source_target_pairs={{0,2},{2,4},{4,6},{6,8},{8,10},{10,12},{12,14},{14,0},{1,3},{3,5},... | collective-permute-start | bytes 2064392 | tf_op jit(solution)/shard_map/ppermute | solution.py:26
  39.7 16.7 %collective-permute-start.1 = (bf16[2,256,672]{1,2,0:T(8,128)(2,1)S(1)}, bf16[2,256,672]{1,2,0:T(8,128)(2,1)}, u32[]{:S(2)}, u32[]{:S(2)}) collective-permute-start(bf16[2,256,672]{1,2,0:T(8,128)(2,1)S(1)} %collective-permute-done), channel_id=1, source_target_pairs={{0,14},{2,0},{4,2},{6,4},{8,6},{10,8},{12,10},{14,12},{1,15},{3,1}... | collective-permute-start | bytes 2064392 | tf_op jit(solution)/shard_map/ppermute | solution.py:28
  56.4 15.8 %collective-permute-start.5 = (bf16[2,256,672]{1,2,0:T(8,128)(2,1)S(1)}, bf16[2,256,672]{1,2,0:T(8,128)(2,1)S(1)}, u32[]{:S(2)}, u32[]{:S(2)}) collective-permute-start(bf16[2,256,672]{1,2,0:T(8,128)(2,1)S(1)} %collective-permute-done.4), channel_id=1, source_target_pairs={{0,2},{2,4},{4,6},{6,8},{8,10},{10,12},{12,14},{14,0},{1,3},{3,5},... | collective-permute-start | bytes 2064392 | tf_op jit(solution)/shard_map/ppermute | solution.py:26
  56.4 20.3 %collective-permute-start.2 = (bf16[2,256,672]{1,2,0:T(8,128)(2,1)}, bf16[2,256,672]{1,2,0:T(8,128)(2,1)}, u32[]{:S(2)}, u32[]{:S(2)}) collective-permute-start(bf16[2,256,672]{1,2,0:T(8,128)(2,1)} %collective-permute-done.1), channel_id=1, source_target_pairs={{0,14},{2,0},{4,2},{6,4},{8,6},{10,8},{12,10},{14,12},{1,15},{3,1}... | collective-permute-start | bytes 2064392 | tf_op jit(solution)/shard_map/ppermute | solution.py:28
  72.2 15.1 %collective-permute-start.6 = (bf16[2,256,672]{1,2,0:T(8,128)(2,1)S(1)}, bf16[2,256,672]{1,2,0:T(8,128)(2,1)}, u32[]{:S(2)}, u32[]{:S(2)}) collective-permute-start(bf16[2,256,672]{1,2,0:T(8,128)(2,1)S(1)} %collective-permute-done.5), channel_id=1, source_target_pairs={{0,2},{2,4},{4,6},{6,8},{8,10},{10,12},{12,14},{14,0},{1,3},{3,5},... | collective-permute-start | bytes 2064392 | tf_op jit(solution)/shard_map/ppermute | solution.py:26
  107.8 17.9 %collective-permute-start.7 = (bf16[256,256]{1,0:T(8,128)(2,1)S(1)}, bf16[256,256]{1,0:T(8,128)(2,1)S(1)}, u32[]{:S(2)}, u32[]{:S(2)}) collective-permute-start(bf16[256,256]{1,0:T(8,128)(2,1)S(1)} %slice.63), channel_id=1, source_target_pairs={{0,64},{16,80},{32,96},{48,112},{64,128},{80,144},{96,160},{112,17... | collective-permute-start | bytes 393224 | tf_op jit(solution)/shard_map/ppermute | solution.py:37
  112.7 13.0 %collective-permute-start.8 = (bf16[256,256]{1,0:T(8,128)(2,1)S(1)}, bf16[256,256]{1,0:T(8,128)(2,1)S(1)}, u32[]{:S(2)}, u32[]{:S(2)}) collective-permute-start(bf16[256,256]{1,0:T(8,128)(2,1)S(1)} %slice.63), channel_id=1, source_target_pairs={{0,48},{16,64},{32,80},{48,96},{64,112},{80,128},{96,144},{112,160... | collective-permute-start | bytes 393224 | tf_op jit(solution)/shard_map/ppermute | solution.py:37
  114.0 11.7 %collective-permute-start.9 = (bf16[256,256]{1,0:T(8,128)(2,1)S(1)}, bf16[256,256]{1,0:T(8,128)(2,1)S(1)}, u32[]{:S(2)}, u32[]{:S(2)}) collective-permute-start(bf16[256,256]{1,0:T(8,128)(2,1)S(1)} %slice.63), channel_id=1, source_target_pairs={{0,32},{16,48},{32,64},{48,80},{64,96},{80,112},{96,128},{112,144}... | collective-permute-start | bytes 393224 | tf_op jit(solution)/shard_map/ppermute | solution.py:37
  116.5 9.2 %collective-permute-start.10 = (bf16[256,256]{1,0:T(8,128)(2,1)S(1)}, bf16[256,256]{1,0:T(8,128)(2,1)S(1)}, u32[]{:S(2)}, u32[]{:S(2)}) collective-permute-start(bf16[256,256]{1,0:T(8,128)(2,1)S(1)} %slice.63), channel_id=1, source_target_pairs={{0,16},{16,32},{32,48},{48,64},{64,80},{80,96},{96,112},{112,128},... | collective-permute-start | bytes 393224 | tf_op jit(solution)/shard_map/ppermute | solution.py:37
  126.5 0.8 copy-start
  134.1 21.8 %copy-start.1 = (bf16[256,256]{1,0:T(8,128)(2,1)S(1)}, bf16[256,256]{1,0:T(8,128)(2,1)}, u32[]{:S(2)}) copy-start(bf16[256,256]{1,0:T(8,128)(2,1)} %get-tuple-element.8) | copy-start | bytes 393220
  135.5 11.4 %collective-permute-start.11 = (f32[256,256]{1,0:T(8,128)S(1)}, f32[256,256]{1,0:T(8,128)S(1)}, u32[]{:S(2)}, u32[]{:S(2)}) collective-permute-start(f32[256,256]{1,0:T(8,128)S(1)} %get-tuple-element.13), channel_id=1, source_target_pairs={{16,0},{32,16},{48,32},{64,48},{80,64},{96,80},{112,96},{128,112},... | collective-permute-start | bytes 786440 | tf_op jit(solution)/shard_map/ppermute | solution.py:37
  136.8 13.2 %collective-permute-start.12 = (f32[256,256]{1,0:T(8,128)S(1)}, f32[256,256]{1,0:T(8,128)S(1)}, u32[]{:S(2)}, u32[]{:S(2)}) collective-permute-start(f32[256,256]{1,0:T(8,128)S(1)} %get-tuple-element.16), channel_id=1, source_target_pairs={{32,0},{48,16},{64,32},{80,48},{96,64},{112,80},{128,96},{144,112}... | collective-permute-start | bytes 786440 | tf_op jit(solution)/shard_map/ppermute | solution.py:37
  138.1 13.7 %collective-permute-start.13 = (f32[256,256]{1,0:T(8,128)S(1)}, f32[256,256]{1,0:T(8,128)S(1)}, u32[]{:S(2)}, u32[]{:S(2)}) collective-permute-start(f32[256,256]{1,0:T(8,128)S(1)} %get-tuple-element.15), channel_id=1, source_target_pairs={{48,0},{64,16},{80,32},{96,48},{112,64},{128,80},{144,96},{160,112... | collective-permute-start | bytes 786440 | tf_op jit(solution)/shard_map/ppermute | solution.py:37
  139.4 15.5 %collective-permute-start.14 = (f32[256,256]{1,0:T(8,128)S(1)}, f32[256,256]{1,0:T(8,128)S(1)}, u32[]{:S(2)}, u32[]{:S(2)}) collective-permute-start(f32[256,256]{1,0:T(8,128)S(1)} %get-tuple-element.14), channel_id=1, source_target_pairs={{64,0},{80,16},{96,32},{112,48},{128,64},{144,80},{160,96},{176,11... | collective-permute-start | bytes 786440 | tf_op jit(solution)/shard_map/ppermute | solution.py:37
Sparse Core Ops, SparseCore 0:
  9.8 55.4 all-gather.1
  166.1 96.2 reduce-scatter.1

commit v5 on v4

--- a/solution.py
+++ b/solution.py
@@ -21,14 +21,21 @@
 
 def ring_gather(block, axis, dim):
     size = lax.psum(1, axis)
+    index = lax.axis_index(axis)
     right, left = [block], [block]
     for _ in range(size // 2):
         right.append(lax.ppermute(right[-1], axis, [(i, (i + 1) % size) for i in range(size)]))
     for _ in range((size - 1) // 2):
         left.append(lax.ppermute(left[-1], axis, [(i, (i - 1) % size) for i in range(size)]))
     ordered = left + [right[k] for k in range(size // 2, 0, -1)]
-    relative = jnp.concatenate(ordered, axis=dim)
-    return jnp.roll(relative, lax.axis_index(axis) * block.shape[dim], axis=dim)
+    shape = list(block.shape)
+    shape[dim] *= size
+    full = jnp.zeros(shape, block.dtype)
+    for offset, piece in enumerate(ordered):
+        start = [0] * len(shape)
+        start[dim] = ((index + offset) % size) * block.shape[dim]
+        full = lax.dynamic_update_slice(full, piece, start)
+    return full
 
 
 def from_behind(block, axis, distance):
@@ -145,8 +152,8 @@
     n_proj = n_q + 2 * n_kv
     pair = jnp.stack([tokens, cotangent])
     pair = lax.all_gather(pair, "yhi", axis=2, tiled=True)
-    pair = ring_gather(pair, "z", 2)
-    full_tokens, full_cot = pair[0], pair[1]
+    full_tokens = ring_gather(pair[0], "z", 1)
+    full_cot = lax.all_gather(pair[1], "z", axis=1, tiled=True)
     w_cat = jnp.concatenate([w_query, w_key, w_value, w_out.T], axis=1)
     w_full = lax.all_gather(w_cat, SEQ, axis=0, tiled=True)
     proj_full = w_full[:, :n_proj]

time: 274 us -> 260 us (0.949)
  local copies, waits for them, and re-layouts: 37.2 us -> 14.9 us
  waiting for transfers between devices: 71.2 us -> 81.7 us
    all_gather x0 -> x1, waiting for transfers between devices: none -> 25 us  [shards(): full_cot = lax.all_gather(pair[1], 'z', axis=1, tiled=True)]
    ppermute x4, waiting for transfers between devices: 48.2 us -> 24.3 us  [ring_gather(): lax.ppermute(right[-1], axis, [(i, (i + 1) % size) for i in range(size)])]
    unnamed x25 -> x14, local copies, waits for them, and re-layouts: 21.9 us -> 1.58 us
    transpose x1 -> x0, local copies, waits for them, and re-layouts: 6.23 us -> none  [shards(): weight_parts = weight_terms(full_tokens.T, full_cot.T, grad_act, attn)]
    reduce_scatter x1, waiting for transfers between devices: 15 us -> 20.9 us  [shards(): lax.psum_scatter(weight_parts, SEQ, scatter_dimension=0, tiled=True)]
    dynamic_update_slice x0 -> x8, local copies, waits for them, and re-layouts: none -> 4.15 us  [ring_gather(): full = lax.dynamic_update_slice(full, piece, start)]
    all_gather x1, waiting for transfers between devices: 0.01 us -> 2.95 us  [shards(): w_full = lax.all_gather(w_cat, SEQ, axis=0, tiled=True)]
  transfers between devices with their start and end apart: 17 -> 18, of which waited for: 8 -> 10; matrix products, arithmetic and copies ran while one was open for 15% -> 9% of each run, Pallas kernels for 0% -> 0%
where the time goes in v5:
time: 260 us; the launch traced here: 259 us
  blocking collectives  84.9 us (33%)
  waiting for transfers between devices  81.7 us (31%)
  starting transfers between devices  28.7 us (11%)
  Pallas kernels  16.1 us (6%)
  local copies, waits for them, and re-layouts  14.9 us (6%)
  between operations  14 us (5%)
  matrix products  12.5 us (5%)
  other arithmetic  5.87 us (2%)
    all_to_all x1, blocking collectives, shards(): lax.all_to_all(token_term.reshape(tok_rows, n_tp, cols), TP, 1, 1, tiled=...  72.9 us
    all_gather x1, waiting for transfers between devices, shards(): full_cot = lax.all_gather(pair[1], 'z', axis=1, tiled=True)  25 us
    ppermute x4, waiting for transfers between devices, ring_gather(): lax.ppermute(right[-1], axis, [(i, (i + 1) % size) for i in range(size)])  24.3 us
    reduce_scatter x1, waiting for transfers between devices, shards(): lax.psum_scatter(weight_parts, SEQ, scatter_dimension=0, tiled=True)  20.9 us
    ppermute x8, starting transfers between devices, from_behind(): return lax.ppermute(block, axis, route)  18.7 us
    all_gather x1, blocking collectives, shards(): pair = lax.all_gather(pair, 'yhi', axis=2, tiled=True)  12 us
    pallas_call x1, Pallas kernels, weight_terms(): pl.pallas_call(weight_terms_kernel, grid=(feats // block,), in_specs=[pl....  9.33 us
    ppermute x3, starting transfers between devices, ring_gather(): lax.ppermute(left[-1], axis, [(i, (i - 1) % size) for i in range(size)])  8.75 us
  transfers between devices with their start and end apart: 18, of which 10 were waited for; matrix products, arithmetic and copies ran while one was open for 9% of the time, Pallas kernels for 0%

profile of v5, /device:TPU:128, one launch (start us, length us, event | category | flops | bytes accessed | tf_op | source)
XLA Modules:
  0.0 258.8 jit_solution(12318297562183857485)
XLA Ops:
  7.2 0.0 all-gather.4.cloned.1.call-start
  7.2 2.0 pad_maximum_fusion
  9.2 0.0 all-gather.4.cloned.1.call-update
  9.2 0.0 all-gather.6.cloned.1.call-start
  9.3 1.0 pad_maximum_fusion.1
  10.3 12.0 %all_gather.9 = bf16[2,256,672]{1,2,0:T(8,128)(2,1)S(1)} all-gather(bf16[2,256,336]{1,2,0:T(8,128)(2,1)S(1)} %pad_maximum_fusion.1), channel_id=1, replica_groups=mesh['ylo'=2,'x'=4,'core'=2,'z'=8,'yhi'=2] {'yhi'}, dimensions={2}, use_global_device_ids=true | all-gather | bytes 1032192 | tf_op jit(solution)/shard_map/all_gather | solution.py:154
  22.3 0.8 fusion.15
  23.1 0.0 all-gather.6.cloned.1.call-update
  23.1 0.0 reduce-scatter.2.cloned.1.call-start
  23.1 1.1 collective-permute-start.3
  24.2 2.2 collective-permute-start
  26.4 7.0 %collective-permute-done.3 = bf16[256,672]{0,1:T(8,128)(2,1)} collective-permute-done((bf16[256,672]{0,1:T(8,128)(2,1)S(1)}, bf16[256,672]{0,1:T(8,128)(2,1)}, u32[]{:S(2)}, u32[]{:S(2)}) %collective-permute-start.3) | collective-permute-done | bytes 344096 | tf_op jit(solution)/shard_map/ppermute | solution.py:27
  33.5 0.0 collective-permute-start.4
  33.5 0.0 collective-permute-done
  33.5 3.2 %collective-permute-start.1 = (bf16[256,672]{0,1:T(8,128)(2,1)}, bf16[256,672]{0,1:T(8,128)(2,1)}, u32[]{:S(2)}, u32[]{:S(2)}) collective-permute-start(bf16[256,672]{0,1:T(8,128)(2,1)} %collective-permute-done), channel_id=1, source_target_pairs={{0,14},{2,0},{4,2},{6,4},{8,6},{10,8},{12,10},{14,12},{1,15},{3,1}... | collective-permute-start | bytes 1032200 | tf_op jit(solution)/shard_map/ppermute | solution.py:29
  36.7 0.2 broadcast_in_dim.6
  36.9 6.1 %collective-permute-done.4 = bf16[256,672]{0,1:T(8,128)(2,1)} collective-permute-done((bf16[256,672]{0,1:T(8,128)(2,1)}, bf16[256,672]{0,1:T(8,128)(2,1)}, u32[]{:S(2)}, u32[]{:S(2)}) %collective-permute-start.4) | collective-permute-done | bytes 344096 | tf_op jit(solution)/shard_map/ppermute | solution.py:27
  43.1 0.0 collective-permute-start.5
  43.1 0.0 collective-permute-done.1
  43.1 3.3 %collective-permute-start.2 = (bf16[256,672]{0,1:T(8,128)(2,1)}, bf16[256,672]{0,1:T(8,128)(2,1)S(1)}, u32[]{:S(2)}, u32[]{:S(2)}) collective-permute-start(bf16[256,672]{0,1:T(8,128)(2,1)} %collective-permute-done.1), channel_id=1, source_target_pairs={{0,14},{2,0},{4,2},{6,4},{8,6},{10,8},{12,10},{14,12},{1,15},{3,1}... | collective-permute-start | bytes 1032200 | tf_op jit(solution)/shard_map/ppermute | solution.py:29
  46.4 0.1 broadcast_bitcast_fusion
  46.5 0.6 copy.15
  47.1 4.7 %collective-permute-done.5 = bf16[256,672]{0,1:T(8,128)(2,1)S(1)} collective-permute-done((bf16[256,672]{0,1:T(8,128)(2,1)}, bf16[256,672]{0,1:T(8,128)(2,1)S(1)}, u32[]{:S(2)}, u32[]{:S(2)}) %collective-permute-start.5) | collective-permute-done | bytes 344096 | tf_op jit(solution)/shard_map/ppermute | solution.py:27
  51.8 0.0 collective-permute-start.6
  51.8 1.0 constant_dynamic-update-slice_fusion.11
  52.8 1.0 constant_dynamic-update-slice_fusion.10
  53.9 0.0 collective-permute-done.2
  53.9 6.4 %collective-permute-done.6 = bf16[256,672]{0,1:T(8,128)(2,1)S(1)} collective-permute-done((bf16[256,672]{0,1:T(8,128)(2,1)S(1)}, bf16[256,672]{0,1:T(8,128)(2,1)S(1)}, u32[]{:S(2)}, u32[]{:S(2)}) %collective-permute-start.6) | collective-permute-done | bytes 344096 | tf_op jit(solution)/shard_map/ppermute | solution.py:27
  60.4 1.0 constant_dynamic-update-slice_fusion.6
  61.4 1.0 constant_dynamic-update-slice_fusion.5
  62.4 2.9 %all-gather.4.cloned.1.call-done = bf16[5376,768]{1,0:T(8,128)(2,1)} async-done(((bf16[336,768]{1,0:T(8,128)(2,1)}), bf16[5376,768]{1,0:T(8,128)(2,1)}) %all-gather.4.cloned.1.call-update) | async-done | bytes 8257552 | tf_op jit(solution)/shard_map/all_gather | solution.py:158
  65.3 4.2 %fusion.6 = bf16[256,512]{1,0:T(8,128)(2,1)S(1)} fusion(bf16[256,5376]{0,1:T(8,128)(2,1)S(1)} %constant_dynamic-update-slice_fusion.5, bf16[5376,768]{1,0:T(8,128)(2,1)} %all-gather.4.cloned.1.call-done), kind=kOutput, calls=%fused_computation.7 | convolution fusion | flops 1409417216 | bytes 8519680 | tf_op jit(solution)/shard_map/dot_general | solution.py:163
  69.5 4.5 %collective-permute-start.7 = (bf16[256,256]{1,0:T(8,128)(2,1)S(1)}, bf16[256,256]{1,0:T(8,128)(2,1)S(1)}, u32[]{:S(2)}, u32[]{:S(2)}) collective-permute-start(bf16[256,256]{1,0:T(8,128)(2,1)S(1)} %slice.65), channel_id=1, source_target_pairs={{0,64},{16,80},{32,96},{48,112},{64,128},{80,144},{96,160},{112,17... | collective-permute-start | bytes 393224 | tf_op jit(solution)/shard_map/ppermute | solution.py:44
  74.1 2.3 collective-permute-start.8
  76.4 2.8 %collective-permute-start.9 = (bf16[256,256]{1,0:T(8,128)(2,1)S(1)}, bf16[256,256]{1,0:T(8,128)(2,1)S(1)}, u32[]{:S(2)}, u32[]{:S(2)}) collective-permute-start(bf16[256,256]{1,0:T(8,128)(2,1)S(1)} %slice.65), channel_id=1, source_target_pairs={{0,32},{16,48},{32,64},{48,80},{64,96},{80,112},{96,128},{112,144}... | collective-permute-start | bytes 393224 | tf_op jit(solution)/shard_map/ppermute | solution.py:44
  79.2 3.9 %collective-permute-start.10 = (bf16[256,256]{1,0:T(8,128)(2,1)S(1)}, bf16[256,256]{1,0:T(8,128)(2,1)S(1)}, u32[]{:S(2)}, u32[]{:S(2)}) collective-permute-start(bf16[256,256]{1,0:T(8,128)(2,1)S(1)} %slice.65), channel_id=1, source_target_pairs={{0,16},{16,32},{32,48},{48,64},{64,80},{80,96},{96,112},{112,128},... | collective-permute-start | bytes 393224 | tf_op jit(solution)/shard_map/ppermute | solution.py:44
  83.1 25.0 %all-gather.6.cloned.1.call-done = bf16[1,256,5376]{1,2,0:T(8,128)(2,1)} async-done(((bf16[1,256,672]{1,2,0:T(8,128)(2,1)}), bf16[1,256,5376]{1,2,0:T(8,128)(2,1)}) %all-gather.6.cloned.1.call-update) | async-done | bytes 2752528 | tf_op jit(solution)/shard_map/all_gather | solution.py:156
  108.2 4.2 %fusion.9.d_ref = bf16[256,256]{1,0:T(8,128)(2,1)} fusion(bf16[5376,768]{1,0:T(8,128)(2,1)} %all-gather.4.cloned.1.call-done, bf16[1,256,5376]{1,2,0:T(8,128)(2,1)} %all-gather.6.cloned.1.call-done), kind=kOutput, calls=%fused_computation.8 | convolution fusion | flops 704708608 | bytes 5636096 | tf_op jit(solution)/shard_map/dot_general | solution.py:160
  112.3 0.0 collective-permute-done.7
  112.4 0.0 collective-permute-done.8
  112.4 0.0 collective-permute-done.9
  112.4 0.7 constant_dynamic-update-slice_fusion
  113.1 0.8 copy-done.1
  114.0 6.8 %shard_map.110 = (bf16[256,256]{1,0:T(8,128)(2,1)}, bf16[256,256]{1,0:T(8,128)(2,1)}, f32[1280,256]{1,0:T(8,128)}) custom-call(bf16[256,256]{1,0:T(8,128)(2,1)} %get-tuple-element.22.q_ref, bf16[256,256]{1,0:T(8,128)(2,1)} %fusion.9.d_ref, bf16[1280,256]{1,0:T(8,128)(2,1)} %copy-done.1, f32[2,1152]{1,0:T(2,128)} %bitcast.30), custom_call_target="tpu_custom_call" | custom-call | tf_op jit(solution)/shard_map/pallas_call | solution.py:100
  120.8 1.3 fusion.14
  122.1 1.3 collective-permute-start.14
  123.4 1.3 collective-permute-start.13
  124.7 1.3 collective-permute-start.12
  126.0 1.3 collective-permute-start.11
  127.3 4.6 %collective-permute-done.14 = f32[256,256]{1,0:T(8,128)S(1)} collective-permute-done((f32[256,256]{1,0:T(8,128)S(1)}, f32[256,256]{1,0:T(8,128)S(1)}, u32[]{:S(2)}, u32[]{:S(2)}) %collective-permute-start.14) | collective-permute-done | bytes 262176 | tf_op jit(solution)/shard_map/ppermute | solution.py:44
  131.9 0.2 collective-permute-done.13
  132.0 3.7 %collective-permute-done.12 = f32[256,256]{1,0:T(8,128)S(1)} collective-permute-done((f32[256,256]{1,0:T(8,128)S(1)}, f32[256,256]{1,0:T(8,128)S(1)}, u32[]{:S(2)}, u32[]{:S(2)}) %collective-permute-start.12) | collective-permute-done | bytes 262176 | tf_op jit(solution)/shard_map/ppermute | solution.py:44
  135.8 0.0 collective-permute-done.11
  135.8 1.0 add_convert_fusion
  136.8 0.7 pad_maximum_fusion.2.ga_ref
  137.6 9.3 %shard_map.111 = bf16[5376,768]{1,0:T(8,128)(2,1)} custom-call(bf16[5376,256]{1,0:T(8,128)(2,1)} %bitcast.24, bf16[5376,256]{1,0:T(8,128)(2,1)} %bitcast.26, bf16[256,512]{1,0:T(8,128)(2,1)} %pad_maximum_fusion.2.ga_ref, bf16[256,256]{1,0:T(8,128)(2,1)} %get-tuple-element.10.attn_ref), custom_call_target="tpu_custom_call" | custom-call | tf_op jit(solution)/shard_map/pallas_call | solution.py:119
  146.9 0.0 reduce-scatter.2.cloned.1.call-update
  146.9 4.2 %convolution_convert_fusion = bf16[256,5376]{1,0:T(8,128)(2,1)S(1)} fusion(bf16[5376,768]{1,0:T(8,128)(2,1)} %all-gather.4.cloned.1.call-done, bf16[256,256]{1,0:T(8,128)(2,1)S(1)} %add_convert_fusion, bf16[256,256]{1,0:T(8,128)(2,1)S(1)} %copy-done.2), kind=kOutput, calls=%fused_computation | convolution fusion | flops 1411186688 | bytes 8519680 | tf_op jit(solution)/shard_map/dot_general | solution.py:134
  151.1 2.8 %copy.12 = bf16[256,5376]{0,1:T(8,128)(2,1)} copy(bf16[256,5376]{1,0:T(8,128)(2,1)S(1)} %convolution_convert_fusion) | data formatting | bytes 5505024 | tf_op jit(solution)/shard_map/convert_element_type | solution.py:180
  153.9 72.9 %all_to_all.5 = bf16[256,16,336]{0,2,1:T(8,128)(2,1)S(1)} all-to-all(bf16[256,16,336]{0,2,1:T(8,128)(2,1)} %bitcast.25), channel_id=1, replica_groups=mesh['ylo'=2,'x'=4,'core'=2,'z'=8,'yhi'=2] {'z','yhi'}, dimensions={1} | all-to-all | bytes 5505024 | tf_op jit(solution)/shard_map/all_to_all | solution.py:183
  226.8 1.1 reduce_sum.12
  228.0 20.9 %reduce-scatter.2.cloned.1.call-done = bf16[336,768]{1,0:T(8,128)(2,1)} async-done(((bf16[5376,768]{1,0:T(8,128)(2,1)}), bf16[336,768]{1,0:T(8,128)(2,1)}) %reduce-scatter.2.cloned.1.call-update) | async-done | bytes 516112 | tf_op jit(solution)/shard_map/reduce_scatter | solution.py:186
  248.9 1.8 slice_bitcast_fusion.1
  250.6 1.6 fusion.16
  (18 shorter events, 0.2 us)
Async XLA Ops:
  7.2 58.2 %all-gather.4.cloned.1.call-start = ((), (), s32[]{:S(2)}) async-start(), calls=%async_computation.2 | async-start | bytes 8773632 | tf_op jit(solution)/shard_map/all_gather | solution.py:158
  9.2 98.9 %all-gather.6.cloned.1.call-start = ((), (), s32[]{:S(2)}) async-start(), calls=%async_computation.4 | async-start | bytes 3096576 | tf_op jit(solution)/shard_map/all_gather | solution.py:156
  22.3 20.8 %copy-start.3 = (s32[2,9]{1,0:T(2,128)S(1)}, s32[2,9]{1,0:T(2,128)}, u32[]{:S(2)}) copy-start(s32[2,9]{1,0:T(2,128)} %param.13) | copy-start | bytes 220
  23.1 225.8 %reduce-scatter.2.cloned.1.call-start = ((), (), s32[]{:S(2)}) async-start(), calls=%async_computation.3 | async-start | bytes 8773632 | tf_op jit(solution)/shard_map/reduce_scatter | solution.py:186
  23.1 10.3 %collective-permute-start.3 = (bf16[256,672]{0,1:T(8,128)(2,1)S(1)}, bf16[256,672]{0,1:T(8,128)(2,1)}, u32[]{:S(2)}, u32[]{:S(2)}) collective-permute-start(bf16[256,672]{0,1:T(8,128)(2,1)S(1)} %get-tuple-element.16), channel_id=1, source_target_pairs={{0,2},{2,4},{4,6},{6,8},{8,10},{10,12},{12,14},{14,0},{1,3},{3,5},... | collective-permute-start | bytes 1032200 | tf_op jit(solution)/shard_map/ppermute | solution.py:27
  24.2 9.2 %collective-permute-start = (bf16[256,672]{0,1:T(8,128)(2,1)S(1)}, bf16[256,672]{0,1:T(8,128)(2,1)}, u32[]{:S(2)}, u32[]{:S(2)}) collective-permute-start(bf16[256,672]{0,1:T(8,128)(2,1)S(1)} %get-tuple-element.16), channel_id=1, source_target_pairs={{0,14},{2,0},{4,2},{6,4},{8,6},{10,8},{12,10},{14,12},{1,15},{3,1}... | collective-permute-start | bytes 1032200 | tf_op jit(solution)/shard_map/ppermute | solution.py:29
  33.5 9.6 %collective-permute-start.4 = (bf16[256,672]{0,1:T(8,128)(2,1)}, bf16[256,672]{0,1:T(8,128)(2,1)}, u32[]{:S(2)}, u32[]{:S(2)}) collective-permute-start(bf16[256,672]{0,1:T(8,128)(2,1)} %collective-permute-done.3), channel_id=1, source_target_pairs={{0,2},{2,4},{4,6},{6,8},{8,10},{10,12},{12,14},{14,0},{1,3},{3,5},... | collective-permute-start | bytes 1032200 | tf_op jit(solution)/shard_map/ppermute | solution.py:27
  33.5 9.6 %collective-permute-start.1 = (bf16[256,672]{0,1:T(8,128)(2,1)}, bf16[256,672]{0,1:T(8,128)(2,1)}, u32[]{:S(2)}, u32[]{:S(2)}) collective-permute-start(bf16[256,672]{0,1:T(8,128)(2,1)} %collective-permute-done), channel_id=1, source_target_pairs={{0,14},{2,0},{4,2},{6,4},{8,6},{10,8},{12,10},{14,12},{1,15},{3,1}... | collective-permute-start | bytes 1032200 | tf_op jit(solution)/shard_map/ppermute | solution.py:29
  43.1 8.8 %collective-permute-start.5 = (bf16[256,672]{0,1:T(8,128)(2,1)}, bf16[256,672]{0,1:T(8,128)(2,1)S(1)}, u32[]{:S(2)}, u32[]{:S(2)}) collective-permute-start(bf16[256,672]{0,1:T(8,128)(2,1)} %collective-permute-done.4), channel_id=1, source_target_pairs={{0,2},{2,4},{4,6},{6,8},{8,10},{10,12},{12,14},{14,0},{1,3},{3,5},... | collective-permute-start | bytes 1032200 | tf_op jit(solution)/shard_map/ppermute | solution.py:27
  43.1 10.8 %collective-permute-start.2 = (bf16[256,672]{0,1:T(8,128)(2,1)}, bf16[256,672]{0,1:T(8,128)(2,1)S(1)}, u32[]{:S(2)}, u32[]{:S(2)}) collective-permute-start(bf16[256,672]{0,1:T(8,128)(2,1)} %collective-permute-done.1), channel_id=1, source_target_pairs={{0,14},{2,0},{4,2},{6,4},{8,6},{10,8},{12,10},{14,12},{1,15},{3,1}... | collective-permute-start | bytes 1032200 | tf_op jit(solution)/shard_map/ppermute | solution.py:29
  51.8 8.5 %collective-permute-start.6 = (bf16[256,672]{0,1:T(8,128)(2,1)S(1)}, bf16[256,672]{0,1:T(8,128)(2,1)S(1)}, u32[]{:S(2)}, u32[]{:S(2)}) collective-permute-start(bf16[256,672]{0,1:T(8,128)(2,1)S(1)} %collective-permute-done.5), channel_id=1, source_target_pairs={{0,2},{2,4},{4,6},{6,8},{8,10},{10,12},{12,14},{14,0},{1,3},{3,5},... | collective-permute-start | bytes 1032200 | tf_op jit(solution)/shard_map/ppermute | solution.py:27
  62.4 7.1 %copy-start = (bf16[256,5376]{0,1:T(8,128)(2,1)}, bf16[256,5376]{0,1:T(8,128)(2,1)S(1)}, u32[]{:S(2)}) copy-start(bf16[256,5376]{0,1:T(8,128)(2,1)S(1)} %constant_dynamic-update-slice_fusion.5) | copy-start | bytes 8257540
  69.5 42.8 %collective-permute-start.7 = (bf16[256,256]{1,0:T(8,128)(2,1)S(1)}, bf16[256,256]{1,0:T(8,128)(2,1)S(1)}, u32[]{:S(2)}, u32[]{:S(2)}) collective-permute-start(bf16[256,256]{1,0:T(8,128)(2,1)S(1)} %slice.65), channel_id=1, source_target_pairs={{0,64},{16,80},{32,96},{48,112},{64,128},{80,144},{96,160},{112,17... | collective-permute-start | bytes 393224 | tf_op jit(solution)/shard_map/ppermute | solution.py:44
  74.1 38.3 %collective-permute-start.8 = (bf16[256,256]{1,0:T(8,128)(2,1)S(1)}, bf16[256,256]{1,0:T(8,128)(2,1)S(1)}, u32[]{:S(2)}, u32[]{:S(2)}) collective-permute-start(bf16[256,256]{1,0:T(8,128)(2,1)S(1)} %slice.65), channel_id=1, source_target_pairs={{0,48},{16,64},{32,80},{48,96},{64,112},{80,128},{96,144},{112,160... | collective-permute-start | bytes 393224 | tf_op jit(solution)/shard_map/ppermute | solution.py:44
  76.4 36.0 %collective-permute-start.9 = (bf16[256,256]{1,0:T(8,128)(2,1)S(1)}, bf16[256,256]{1,0:T(8,128)(2,1)S(1)}, u32[]{:S(2)}, u32[]{:S(2)}) collective-permute-start(bf16[256,256]{1,0:T(8,128)(2,1)S(1)} %slice.65), channel_id=1, source_target_pairs={{0,32},{16,48},{32,64},{48,80},{64,96},{80,112},{96,128},{112,144}... | collective-permute-start | bytes 393224 | tf_op jit(solution)/shard_map/ppermute | solution.py:44
  79.2 33.2 %collective-permute-start.10 = (bf16[256,256]{1,0:T(8,128)(2,1)S(1)}, bf16[256,256]{1,0:T(8,128)(2,1)S(1)}, u32[]{:S(2)}, u32[]{:S(2)}) collective-permute-start(bf16[256,256]{1,0:T(8,128)(2,1)S(1)} %slice.65), channel_id=1, source_target_pairs={{0,16},{16,32},{32,48},{48,64},{64,80},{80,96},{96,112},{112,128},... | collective-permute-start | bytes 393224 | tf_op jit(solution)/shard_map/ppermute | solution.py:44
  113.1 0.8 copy-start.1
  120.8 16.0 %copy-start.2 = (bf16[256,256]{1,0:T(8,128)(2,1)S(1)}, bf16[256,256]{1,0:T(8,128)(2,1)}, u32[]{:S(2)}) copy-start(bf16[256,256]{1,0:T(8,128)(2,1)} %get-tuple-element.8) | copy-start | bytes 393220
  122.1 9.8 %collective-permute-start.14 = (f32[256,256]{1,0:T(8,128)S(1)}, f32[256,256]{1,0:T(8,128)S(1)}, u32[]{:S(2)}, u32[]{:S(2)}) collective-permute-start(f32[256,256]{1,0:T(8,128)S(1)} %get-tuple-element.12), channel_id=1, source_target_pairs={{64,0},{80,16},{96,32},{112,48},{128,64},{144,80},{160,96},{176,11... | collective-permute-start | bytes 786440 | tf_op jit(solution)/shard_map/ppermute | solution.py:44
  123.4 8.6 %collective-permute-start.13 = (f32[256,256]{1,0:T(8,128)S(1)}, f32[256,256]{1,0:T(8,128)S(1)}, u32[]{:S(2)}, u32[]{:S(2)}) collective-permute-start(f32[256,256]{1,0:T(8,128)S(1)} %get-tuple-element.13), channel_id=1, source_target_pairs={{48,0},{64,16},{80,32},{96,48},{112,64},{128,80},{144,96},{160,112... | collective-permute-start | bytes 786440 | tf_op jit(solution)/shard_map/ppermute | solution.py:44
  124.7 11.1 %collective-permute-start.12 = (f32[256,256]{1,0:T(8,128)S(1)}, f32[256,256]{1,0:T(8,128)S(1)}, u32[]{:S(2)}, u32[]{:S(2)}) collective-permute-start(f32[256,256]{1,0:T(8,128)S(1)} %get-tuple-element.14), channel_id=1, source_target_pairs={{32,0},{48,16},{64,32},{80,48},{96,64},{112,80},{128,96},{144,112}... | collective-permute-start | bytes 786440 | tf_op jit(solution)/shard_map/ppermute | solution.py:44
  126.0 9.8 %collective-permute-start.11 = (f32[256,256]{1,0:T(8,128)S(1)}, f32[256,256]{1,0:T(8,128)S(1)}, u32[]{:S(2)}, u32[]{:S(2)}) collective-permute-start(f32[256,256]{1,0:T(8,128)S(1)} %get-tuple-element.11), channel_id=1, source_target_pairs={{16,0},{32,16},{48,32},{64,48},{80,64},{96,80},{112,96},{128,112},... | collective-permute-start | bytes 786440 | tf_op jit(solution)/shard_map/ppermute | solution.py:44
Sparse Core Ops, SparseCore 0:
  9.8 55.4 all-gather.3
  67.1 40.9 all-gather.5
  147.0 101.8 reduce-scatter.1

commit v6 on v5

--- a/solution.py
+++ b/solution.py
@@ -152,8 +152,11 @@
     n_proj = n_q + 2 * n_kv
     pair = jnp.stack([tokens, cotangent])
     pair = lax.all_gather(pair, "yhi", axis=2, tiled=True)
-    full_tokens = ring_gather(pair[0], "z", 1)
-    full_cot = lax.all_gather(pair[1], "z", axis=1, tiled=True)
+    half = tok_rows // 2
+    ring_full = ring_gather(jnp.concatenate([pair[0], pair[1][:half]], axis=0), "z", 1)
+    full_tokens = ring_full[:tok_rows]
+    cot_rest = lax.all_gather(pair[1][half:], "z", axis=1, tiled=True)
+    full_cot = jnp.concatenate([ring_full[tok_rows:], cot_rest], axis=0)
     w_cat = jnp.concatenate([w_query, w_key, w_value, w_out.T], axis=1)
     w_full = lax.all_gather(w_cat, SEQ, axis=0, tiled=True)
     proj_full = w_full[:, :n_proj]

time: 260 us -> 261 us (level)
  waiting for transfers between devices: 81.7 us -> 64.6 us
  local copies, waits for them, and re-layouts: 14.9 us -> 29.1 us
  other arithmetic: 5.87 us -> 8.55 us
    all_gather x1, waiting for transfers between devices: 25 us -> 0.01 us  [shards(): cot_rest = lax.all_gather(pair[1][half:], 'z', axis=1, tiled=True)]
    ppermute x4, waiting for transfers between devices: 24.3 us -> 37.2 us  [ring_gather(): lax.ppermute(right[-1], axis, [(i, (i + 1) % size) for i in range(size)])]
    unnamed x14 -> x18, local copies, waits for them, and re-layouts: 1.58 us -> 5.99 us
    transpose x0 -> x1, local copies, waits for them, and re-layouts: none -> 3.53 us  [shards(): weight_parts = weight_terms(full_tokens.T, full_cot.T, grad_act, attn)]
    all_gather x1, waiting for transfers between devices: 2.95 us -> 0.01 us  [shards(): w_full = lax.all_gather(w_cat, SEQ, axis=0, tiled=True)]
    dynamic_update_slice x8 -> x7, local copies, waits for them, and re-layouts: 4.15 us -> 7.04 us  [ring_gather(): full = lax.dynamic_update_slice(full, piece, start)]
  transfers between devices with their start and end apart: 18 -> 18, of which waited for: 10 -> 7; matrix products, arithmetic and copies ran while one was open for 9% -> 15% of each run, Pallas kernels for 0% -> 0%
where the time goes in v6:
time: 261 us; the launch traced here: 260 us
  blocking collectives  84.9 us (33%)
  waiting for transfers between devices  64.6 us (25%)
  starting transfers between devices  29.9 us (11%)
  local copies, waits for them, and re-layouts  29.1 us (11%)
  Pallas kernels  16.1 us (6%)
  between operations  13.9 us (5%)
  matrix products  13.1 us (5%)
  other arithmetic  8.55 us (3%)
    all_to_all x1, blocking collectives, shards(): lax.all_to_all(token_term.reshape(tok_rows, n_tp, cols), TP, 1, 1, tiled=...  72.9 us
    ppermute x4, waiting for transfers between devices, ring_gather(): lax.ppermute(right[-1], axis, [(i, (i + 1) % size) for i in range(size)])  37.2 us
    reduce_scatter x1, waiting for transfers between devices, shards(): lax.psum_scatter(weight_parts, SEQ, scatter_dimension=0, tiled=True)  20.8 us
    ppermute x8, starting transfers between devices, from_behind(): return lax.ppermute(block, axis, route)  20 us
    all_gather x1, blocking collectives, shards(): pair = lax.all_gather(pair, 'yhi', axis=2, tiled=True)  12 us
    pallas_call x1, Pallas kernels, weight_terms(): pl.pallas_call(weight_terms_kernel, grid=(feats // block,), in_specs=[pl....  9.33 us
    ppermute x3, starting transfers between devices, ring_gather(): lax.ppermute(left[-1], axis, [(i, (i - 1) % size) for i in range(size)])  8.76 us
    dynamic_update_slice x7, local copies, waits for them, and re-layouts, ring_gather(): full = lax.dynamic_update_slice(full, piece, start)  7.04 us
  transfers between devices with their start and end apart: 18, of which 7 were waited for; matrix products, arithmetic and copies ran while one was open for 15% of the time, Pallas kernels for 0%

profile of v6, /device:TPU:128, one launch (start us, length us, event | category | flops | bytes accessed | tf_op | source)
XLA Modules:
  0.0 260.1 jit_solution(251720946424611072)
XLA Ops:
  7.2 0.0 all-gather.4.cloned.1.call-start
  7.2 1.9 pad_maximum_fusion.5
  9.1 0.0 all-gather.4.cloned.1.call-update
  9.1 0.0 all-gather.6.cloned.1.call-start
  9.2 1.0 pad_maximum_fusion.6
  10.2 0.0 copy-start.5
  10.3 12.0 %all_gather.9 = bf16[2,256,672]{1,2,0:T(8,128)(2,1)S(1)} all-gather(bf16[2,256,336]{1,2,0:T(8,128)(2,1)S(1)} %pad_maximum_fusion.6), channel_id=1, replica_groups=mesh['ylo'=2,'x'=4,'core'=2,'z'=8,'yhi'=2] {'yhi'}, dimensions={2}, use_global_device_ids=true | all-gather | bytes 1032192 | tf_op jit(solution)/shard_map/all_gather | solution.py:154
  22.2 0.7 fusion.17
  22.9 2.3 broadcast_in_dim.6
  25.3 0.9 pad_maximum_fusion.4
  26.1 1.0 collective-permute-start.3
  27.2 2.2 collective-permute-start
  29.4 10.6 %collective-permute-done.3 = bf16[384,672]{0,1:T(8,128)(2,1)S(1)} collective-permute-done((bf16[384,672]{0,1:T(8,128)(2,1)S(1)}, bf16[384,672]{0,1:T(8,128)(2,1)S(1)}, u32[]{:S(2)}, u32[]{:S(2)}) %collective-permute-start.3) | collective-permute-done | bytes 516128 | tf_op jit(solution)/shard_map/ppermute | solution.py:27
  40.0 3.2 %collective-permute-start.1 = (bf16[384,672]{0,1:T(8,128)(2,1)S(1)}, bf16[384,672]{0,1:T(8,128)(2,1)S(1)}, u32[]{:S(2)}, u32[]{:S(2)}) collective-permute-start(bf16[384,672]{0,1:T(8,128)(2,1)S(1)} %collective-permute-done), channel_id=1, source_target_pairs={{0,14},{2,0},{4,2},{6,4},{8,6},{10,8},{12,10},{14,12},{1,15},{3,1}... | collective-permute-start | bytes 1548296 | tf_op jit(solution)/shard_map/ppermute | solution.py:29
  43.2 9.7 %collective-permute-done.4 = bf16[384,672]{0,1:T(8,128)(2,1)S(1)} collective-permute-done((bf16[384,672]{0,1:T(8,128)(2,1)S(1)}, bf16[384,672]{0,1:T(8,128)(2,1)S(1)}, u32[]{:S(2)}, u32[]{:S(2)}) %collective-permute-start.4) | collective-permute-done | bytes 516128 | tf_op jit(solution)/shard_map/ppermute | solution.py:27
  53.0 0.0 all-gather.6.cloned.1.call-update
  53.0 0.0 reduce-scatter.2.cloned.1.call-start
  53.1 3.3 %collective-permute-start.2 = (bf16[384,672]{0,1:T(8,128)(2,1)S(1)}, bf16[384,672]{0,1:T(8,128)(2,1)S(1)}, u32[]{:S(2)}, u32[]{:S(2)}) collective-permute-start(bf16[384,672]{0,1:T(8,128)(2,1)S(1)} %collective-permute-done.1), channel_id=1, source_target_pairs={{0,14},{2,0},{4,2},{6,4},{8,6},{10,8},{12,10},{14,12},{1,15},{3,1}... | collective-permute-start | bytes 1548296 | tf_op jit(solution)/shard_map/ppermute | solution.py:29
  56.4 8.7 %collective-permute-done.5 = bf16[384,672]{0,1:T(8,128)(2,1)S(1)} collective-permute-done((bf16[384,672]{0,1:T(8,128)(2,1)S(1)}, bf16[384,672]{0,1:T(8,128)(2,1)S(1)}, u32[]{:S(2)}, u32[]{:S(2)}) %collective-permute-start.5) | collective-permute-done | bytes 516128 | tf_op jit(solution)/shard_map/ppermute | solution.py:27
  65.1 0.1 broadcast_bitcast_fusion
  65.2 0.6 copy.15
  65.8 0.8 constant_dynamic-update-slice_fusion.11
  66.6 0.8 constant_dynamic-update-slice_fusion.10
  67.5 0.9 constant_dynamic-update-slice_fusion.9
  68.3 8.2 %collective-permute-done.6 = bf16[384,672]{0,1:T(8,128)(2,1)} collective-permute-done((bf16[384,672]{0,1:T(8,128)(2,1)S(1)}, bf16[384,672]{0,1:T(8,128)(2,1)}, u32[]{:S(2)}, u32[]{:S(2)}) %collective-permute-start.6) | collective-permute-done | bytes 516128 | tf_op jit(solution)/shard_map/ppermute | solution.py:27
  76.5 1.9 constant_dynamic-update-slice_fusion.8
  78.4 0.9 constant_dynamic-update-slice_fusion.7
  79.3 0.8 constant_dynamic-update-slice_fusion.6
  80.1 0.9 constant_dynamic-update-slice_fusion.5
  81.0 1.4 slice.89
  82.4 3.5 %slice_bitcast_fusion.tok_ref = bf16[5376,256]{1,0:T(8,128)(2,1)} fusion(bf16[384,5376]{0,1:T(8,128)(2,1)} %constant_dynamic-update-slice_fusion.5), kind=kLoop, calls=%fused_computation.7 | loop fusion | bytes 5505024 | tf_op jit(solution)/shard_map/transpose | solution.py:188
  85.9 5.0 %fusion.7 = bf16[256,512]{1,0:T(8,128)(2,1)S(1)} fusion(bf16[5376,768]{1,0:T(8,128)(2,1)} %all-gather.4.cloned.1.call-done, bf16[384,5376]{0,1:T(8,128)(2,1)} %constant_dynamic-update-slice_fusion.5), kind=kOutput, calls=%fused_computation.10 | convolution fusion | flops 1409417216 | bytes 8519680 | tf_op jit(solution)/shard_map/dot_general | solution.py:166
  91.0 0.7 copy-done.2
  91.7 5.6 %collective-permute-start.7 = (bf16[256,256]{1,0:T(8,128)(2,1)S(1)}, bf16[256,256]{1,0:T(8,128)(2,1)}, u32[]{:S(2)}, u32[]{:S(2)}) collective-permute-start(bf16[256,256]{1,0:T(8,128)(2,1)S(1)} %slice.92), channel_id=1, source_target_pairs={{0,64},{16,80},{32,96},{48,112},{64,128},{80,144},{96,160},{112,17... | collective-permute-start | bytes 393224 | tf_op jit(solution)/shard_map/ppermute | solution.py:44
  97.3 1.9 collective-permute-start.8
  99.2 3.1 %collective-permute-start.9 = (bf16[256,256]{1,0:T(8,128)(2,1)S(1)}, bf16[256,256]{1,0:T(8,128)(2,1)}, u32[]{:S(2)}, u32[]{:S(2)}) collective-permute-start(bf16[256,256]{1,0:T(8,128)(2,1)S(1)} %slice.92), channel_id=1, source_target_pairs={{0,32},{16,48},{32,64},{48,80},{64,96},{80,112},{96,128},{112,144}... | collective-permute-start | bytes 393224 | tf_op jit(solution)/shard_map/ppermute | solution.py:44
  102.3 4.2 %collective-permute-start.10 = (bf16[256,256]{1,0:T(8,128)(2,1)S(1)}, bf16[256,256]{1,0:T(8,128)(2,1)}, u32[]{:S(2)}, u32[]{:S(2)}) collective-permute-start(bf16[256,256]{1,0:T(8,128)(2,1)S(1)} %slice.92), channel_id=1, source_target_pairs={{0,16},{16,32},{32,48},{48,64},{64,80},{80,96},{96,112},{112,128},... | collective-permute-start | bytes 393224 | tf_op jit(solution)/shard_map/ppermute | solution.py:44
  106.5 3.8 %fusion.12.d_ref = bf16[256,256]{1,0:T(8,128)(2,1)} fusion(bf16[5376,768]{1,0:T(8,128)(2,1)} %all-gather.4.cloned.1.call-done, bf16[128,5376]{0,1:T(8,128)(2,1)} %bitcast.21, bf16[128,5376]{0,1:T(8,128)(2,1)S(1)} %slice.89), kind=kOutput, calls=%fused_computation.11 | convolution fusion | flops 710213632 | bytes 5636096 | tf_op jit(solution)/shard_map/dot_general | solution.py:163
  110.3 1.0 constant_dynamic-update-slice_fusion.4
  111.4 0.9 constant_dynamic-update-slice_fusion.3
  112.3 0.9 constant_dynamic-update-slice_fusion.2
  113.2 0.9 constant_dynamic-update-slice_fusion.1
  114.2 0.7 constant_dynamic-update-slice_fusion
  114.8 0.8 copy-done.1
  115.7 6.7 %shard_map.110 = (bf16[256,256]{1,0:T(8,128)(2,1)}, bf16[256,256]{1,0:T(8,128)(2,1)}, f32[1280,256]{1,0:T(8,128)}) custom-call(bf16[256,256]{1,0:T(8,128)(2,1)} %get-tuple-element.24.q_ref, bf16[256,256]{1,0:T(8,128)(2,1)} %fusion.12.d_ref, bf16[1280,256]{1,0:T(8,128)(2,1)} %copy-done.1, f32[2,1152]{1,0:T(2,128)} %bitcast.26), custom_call_target="tpu_custom_call" | custom-call | tf_op jit(solution)/shard_map/pallas_call | solution.py:100
  122.4 1.3 fusion.16
  123.7 1.3 collective-permute-start.14
  125.0 1.3 collective-permute-start.13
  126.3 1.3 collective-permute-start.12
  127.6 1.3 collective-permute-start.11
  128.9 1.9 fusion.6.cot_ref
  130.8 4.1 %collective-permute-done.14 = f32[256,256]{1,0:T(8,128)S(1)} collective-permute-done((f32[256,256]{1,0:T(8,128)S(1)}, f32[256,256]{1,0:T(8,128)S(1)}, u32[]{:S(2)}, u32[]{:S(2)}) %collective-permute-start.14) | collective-permute-done | bytes 262176 | tf_op jit(solution)/shard_map/ppermute | solution.py:44
  134.9 2.5 collective-permute-done.12
  137.4 1.0 add_convert_fusion
  138.4 0.7 pad_maximum_fusion.7.ga_ref
  139.2 9.3 %shard_map.111 = bf16[5376,768]{1,0:T(8,128)(2,1)} custom-call(bf16[5376,256]{1,0:T(8,128)(2,1)} %slice_bitcast_fusion.tok_ref, bf16[5376,256]{1,0:T(8,128)(2,1)} %fusion.6.cot_ref, bf16[256,512]{1,0:T(8,128)(2,1)} %pad_maximum_fusion.7.ga_ref, bf16[256,256]{1,0:T(8,128)(2,1)} %get-tuple-element.10.attn_ref), custom_call_target="tpu_custom_call" | custom-call | tf_op jit(solution)/shard_map/pallas_call | solution.py:119
  148.5 0.0 reduce-scatter.2.cloned.1.call-update
  148.5 4.2 %convolution_convert_fusion = bf16[256,5376]{1,0:T(8,128)(2,1)S(1)} fusion(bf16[5376,768]{1,0:T(8,128)(2,1)} %all-gather.4.cloned.1.call-done, bf16[256,256]{1,0:T(8,128)(2,1)S(1)} %add_convert_fusion, bf16[256,256]{1,0:T(8,128)(2,1)S(1)} %copy-done.4), kind=kOutput, calls=%fused_computation | convolution fusion | flops 1411186688 | bytes 8519680 | tf_op jit(solution)/shard_map/dot_general | solution.py:134
  152.7 2.8 %copy.12 = bf16[256,5376]{0,1:T(8,128)(2,1)} copy(bf16[256,5376]{1,0:T(8,128)(2,1)S(1)} %convolution_convert_fusion) | data formatting | bytes 5505024 | tf_op jit(solution)/shard_map/convert_element_type | solution.py:183
  155.5 72.9 %all_to_all.5 = bf16[256,16,336]{0,2,1:T(8,128)(2,1)S(1)} all-to-all(bf16[256,16,336]{0,2,1:T(8,128)(2,1)} %bitcast.20), channel_id=1, replica_groups=mesh['ylo'=2,'x'=4,'core'=2,'z'=8,'yhi'=2] {'z','yhi'}, dimensions={1} | all-to-all | bytes 5505024 | tf_op jit(solution)/shard_map/all_to_all | solution.py:186
  228.4 1.1 reduce_sum.12
  229.5 20.8 %reduce-scatter.2.cloned.1.call-done = bf16[336,768]{1,0:T(8,128)(2,1)} async-done(((bf16[5376,768]{1,0:T(8,128)(2,1)}), bf16[336,768]{1,0:T(8,128)(2,1)}) %reduce-scatter.2.cloned.1.call-update) | async-done | bytes 516112 | tf_op jit(solution)/shard_map/reduce_scatter | solution.py:189
  250.2 1.8 slice_bitcast_fusion.2
  252.0 1.6 fusion.18
  (26 shorter events, 0.1 us)
Async XLA Ops:
  7.2 78.8 %all-gather.4.cloned.1.call-start = ((), (), s32[]{:S(2)}) async-start(), calls=%async_computation.2 | async-start | bytes 8773632 | tf_op jit(solution)/shard_map/all_gather | solution.py:161
  9.1 97.4 %all-gather.6.cloned.1.call-start = ((), (), s32[]{:S(2)}) async-start(), calls=%async_computation.4 | async-start | bytes 1548288 | tf_op jit(solution)/shard_map/all_gather | solution.py:158
  10.2 46.1 %copy-start.5 = (s32[2,9]{1,0:T(2,128)S(1)}, s32[2,9]{1,0:T(2,128)}, u32[]{:S(2)}) copy-start(s32[2,9]{1,0:T(2,128)} %param.13) | copy-start | bytes 220
  26.1 13.8 %collective-permute-start.3 = (bf16[384,672]{0,1:T(8,128)(2,1)S(1)}, bf16[384,672]{0,1:T(8,128)(2,1)S(1)}, u32[]{:S(2)}, u32[]{:S(2)}) collective-permute-start(bf16[384,672]{0,1:T(8,128)(2,1)S(1)} %get-tuple-element.21), channel_id=1, source_target_pairs={{0,2},{2,4},{4,6},{6,8},{8,10},{10,12},{12,14},{14,0},{1,3},{3,5},... | collective-permute-start | bytes 1548296 | tf_op jit(solution)/shard_map/ppermute | solution.py:27
  27.2 12.8 %collective-permute-start = (bf16[384,672]{0,1:T(8,128)(2,1)S(1)}, bf16[384,672]{0,1:T(8,128)(2,1)S(1)}, u32[]{:S(2)}, u32[]{:S(2)}) collective-permute-start(bf16[384,672]{0,1:T(8,128)(2,1)S(1)} %get-tuple-element.21), channel_id=1, source_target_pairs={{0,14},{2,0},{4,2},{6,4},{8,6},{10,8},{12,10},{14,12},{1,15},{3,1}... | collective-permute-start | bytes 1548296 | tf_op jit(solution)/shard_map/ppermute | solution.py:29
  40.0 13.0 %collective-permute-start.4 = (bf16[384,672]{0,1:T(8,128)(2,1)S(1)}, bf16[384,672]{0,1:T(8,128)(2,1)S(1)}, u32[]{:S(2)}, u32[]{:S(2)}) collective-permute-start(bf16[384,672]{0,1:T(8,128)(2,1)S(1)} %collective-permute-done.3), channel_id=1, source_target_pairs={{0,2},{2,4},{4,6},{6,8},{8,10},{10,12},{12,14},{14,0},{1,3},{3,5},... | collective-permute-start | bytes 1548296 | tf_op jit(solution)/shard_map/ppermute | solution.py:27
  40.0 13.1 %collective-permute-start.1 = (bf16[384,672]{0,1:T(8,128)(2,1)S(1)}, bf16[384,672]{0,1:T(8,128)(2,1)S(1)}, u32[]{:S(2)}, u32[]{:S(2)}) collective-permute-start(bf16[384,672]{0,1:T(8,128)(2,1)S(1)} %collective-permute-done), channel_id=1, source_target_pairs={{0,14},{2,0},{4,2},{6,4},{8,6},{10,8},{12,10},{14,12},{1,15},{3,1}... | collective-permute-start | bytes 1548296 | tf_op jit(solution)/shard_map/ppermute | solution.py:29
  53.0 12.1 %collective-permute-start.5 = (bf16[384,672]{0,1:T(8,128)(2,1)S(1)}, bf16[384,672]{0,1:T(8,128)(2,1)S(1)}, u32[]{:S(2)}, u32[]{:S(2)}) collective-permute-start(bf16[384,672]{0,1:T(8,128)(2,1)S(1)} %collective-permute-done.4), channel_id=1, source_target_pairs={{0,2},{2,4},{4,6},{6,8},{8,10},{10,12},{12,14},{14,0},{1,3},{3,5},... | collective-permute-start | bytes 1548296 | tf_op jit(solution)/shard_map/ppermute | solution.py:27
  53.0 197.2 %reduce-scatter.2.cloned.1.call-start = ((), (), s32[]{:S(2)}) async-start(), calls=%async_computation.3 | async-start | bytes 8773632 | tf_op jit(solution)/shard_map/reduce_scatter | solution.py:189
  53.1 14.4 %collective-permute-start.2 = (bf16[384,672]{0,1:T(8,128)(2,1)S(1)}, bf16[384,672]{0,1:T(8,128)(2,1)S(1)}, u32[]{:S(2)}, u32[]{:S(2)}) collective-permute-start(bf16[384,672]{0,1:T(8,128)(2,1)S(1)} %collective-permute-done.1), channel_id=1, source_target_pairs={{0,14},{2,0},{4,2},{6,4},{8,6},{10,8},{12,10},{14,12},{1,15},{3,1}... | collective-permute-start | bytes 1548296 | tf_op jit(solution)/shard_map/ppermute | solution.py:29
  65.1 11.4 %collective-permute-start.6 = (bf16[384,672]{0,1:T(8,128)(2,1)S(1)}, bf16[384,672]{0,1:T(8,128)(2,1)}, u32[]{:S(2)}, u32[]{:S(2)}) collective-permute-start(bf16[384,672]{0,1:T(8,128)(2,1)S(1)} %collective-permute-done.5), channel_id=1, source_target_pairs={{0,2},{2,4},{4,6},{6,8},{8,10},{10,12},{12,14},{14,0},{1,3},{3,5},... | collective-permute-start | bytes 1548296 | tf_op jit(solution)/shard_map/ppermute | solution.py:27
  91.0 0.7 copy-start.2
  91.7 18.6 %collective-permute-start.7 = (bf16[256,256]{1,0:T(8,128)(2,1)S(1)}, bf16[256,256]{1,0:T(8,128)(2,1)}, u32[]{:S(2)}, u32[]{:S(2)}) collective-permute-start(bf16[256,256]{1,0:T(8,128)(2,1)S(1)} %slice.92), channel_id=1, source_target_pairs={{0,64},{16,80},{32,96},{48,112},{64,128},{80,144},{96,160},{112,17... | collective-permute-start | bytes 393224 | tf_op jit(solution)/shard_map/ppermute | solution.py:44
  97.3 14.1 %collective-permute-start.8 = (bf16[256,256]{1,0:T(8,128)(2,1)S(1)}, bf16[256,256]{1,0:T(8,128)(2,1)}, u32[]{:S(2)}, u32[]{:S(2)}) collective-permute-start(bf16[256,256]{1,0:T(8,128)(2,1)S(1)} %slice.92), channel_id=1, source_target_pairs={{0,48},{16,64},{32,80},{48,96},{64,112},{80,128},{96,144},{112,160... | collective-permute-start | bytes 393224 | tf_op jit(solution)/shard_map/ppermute | solution.py:44
  99.2 13.1 %collective-permute-start.9 = (bf16[256,256]{1,0:T(8,128)(2,1)S(1)}, bf16[256,256]{1,0:T(8,128)(2,1)}, u32[]{:S(2)}, u32[]{:S(2)}) collective-permute-start(bf16[256,256]{1,0:T(8,128)(2,1)S(1)} %slice.92), channel_id=1, source_target_pairs={{0,32},{16,48},{32,64},{48,80},{64,96},{80,112},{96,128},{112,144}... | collective-permute-start | bytes 393224 | tf_op jit(solution)/shard_map/ppermute | solution.py:44
  102.3 10.9 %collective-permute-start.10 = (bf16[256,256]{1,0:T(8,128)(2,1)S(1)}, bf16[256,256]{1,0:T(8,128)(2,1)}, u32[]{:S(2)}, u32[]{:S(2)}) collective-permute-start(bf16[256,256]{1,0:T(8,128)(2,1)S(1)} %slice.92), channel_id=1, source_target_pairs={{0,16},{16,32},{32,48},{48,64},{64,80},{80,96},{96,112},{112,128},... | collective-permute-start | bytes 393224 | tf_op jit(solution)/shard_map/ppermute | solution.py:44
  106.5 7.6 %copy-start.3 = (bf16[256,512]{1,0:T(8,128)(2,1)S(1)}, bf16[256,512]{1,0:T(8,128)(2,1)}, u32[]{:S(2)}) copy-start(bf16[256,512]{1,0:T(8,128)(2,1)} %copy-done.2) | copy-start | bytes 786436
  110.3 18.6 %copy-start = (bf16[1,128,5376]{1,2,0:T(8,128)(2,1)S(1)}, bf16[1,128,5376]{1,2,0:T(8,128)(2,1)}, u32[]{:S(2)}) copy-start(bf16[1,128,5376]{1,2,0:T(8,128)(2,1)} %all-gather.6.cloned.1.call-done) | copy-start | bytes 4128772
  114.8 0.9 copy-start.1
  122.4 16.0 %copy-start.4 = (bf16[256,256]{1,0:T(8,128)(2,1)S(1)}, bf16[256,256]{1,0:T(8,128)(2,1)}, u32[]{:S(2)}) copy-start(bf16[256,256]{1,0:T(8,128)(2,1)} %get-tuple-element.8) | copy-start | bytes 393220
  123.7 11.2 %collective-permute-start.14 = (f32[256,256]{1,0:T(8,128)S(1)}, f32[256,256]{1,0:T(8,128)S(1)}, u32[]{:S(2)}, u32[]{:S(2)}) collective-permute-start(f32[256,256]{1,0:T(8,128)S(1)} %get-tuple-element.12), channel_id=1, source_target_pairs={{64,0},{80,16},{96,32},{112,48},{128,64},{144,80},{160,96},{176,11... | collective-permute-start | bytes 786440 | tf_op jit(solution)/shard_map/ppermute | solution.py:44
  125.0 9.9 %collective-permute-start.13 = (f32[256,256]{1,0:T(8,128)S(1)}, f32[256,256]{1,0:T(8,128)S(1)}, u32[]{:S(2)}, u32[]{:S(2)}) collective-permute-start(f32[256,256]{1,0:T(8,128)S(1)} %get-tuple-element.13), channel_id=1, source_target_pairs={{48,0},{64,16},{80,32},{96,48},{112,64},{128,80},{144,96},{160,112... | collective-permute-start | bytes 786440 | tf_op jit(solution)/shard_map/ppermute | solution.py:44
  126.3 11.1 %collective-permute-start.12 = (f32[256,256]{1,0:T(8,128)S(1)}, f32[256,256]{1,0:T(8,128)S(1)}, u32[]{:S(2)}, u32[]{:S(2)}) collective-permute-start(f32[256,256]{1,0:T(8,128)S(1)} %get-tuple-element.14), channel_id=1, source_target_pairs={{32,0},{48,16},{64,32},{80,48},{96,64},{112,80},{128,96},{144,112}... | collective-permute-start | bytes 786440 | tf_op jit(solution)/shard_map/ppermute | solution.py:44
  127.6 9.8 %collective-permute-start.11 = (f32[256,256]{1,0:T(8,128)S(1)}, f32[256,256]{1,0:T(8,128)S(1)}, u32[]{:S(2)}, u32[]{:S(2)}) collective-permute-start(f32[256,256]{1,0:T(8,128)S(1)} %get-tuple-element.11), channel_id=1, source_target_pairs={{16,0},{32,16},{48,32},{64,48},{80,64},{96,80},{112,96},{128,112},... | collective-permute-start | bytes 786440 | tf_op jit(solution)/shard_map/ppermute | solution.py:44
Sparse Core Ops, SparseCore 0:
  9.8 55.4 all-gather.3
  67.7 37.1 all-gather.5
  148.6 101.5 reduce-scatter.1

commit v7 on v5

--- a/solution.py
+++ b/solution.py
@@ -19,7 +19,7 @@
 TP_SPLIT = (8, 2)
 
 
-def ring_gather(block, axis, dim):
+def ring_pieces(block, axis, dim):
     size = lax.psum(1, axis)
     index = lax.axis_index(axis)
     right, left = [block], [block]
@@ -28,14 +28,27 @@
     for _ in range((size - 1) // 2):
         left.append(lax.ppermute(left[-1], axis, [(i, (i - 1) % size) for i in range(size)]))
     ordered = left + [right[k] for k in range(size // 2, 0, -1)]
-    shape = list(block.shape)
-    shape[dim] *= size
-    full = jnp.zeros(shape, block.dtype)
-    for offset, piece in enumerate(ordered):
+    return [(((index + offset) % size) * block.shape[dim], piece) for offset, piece in enumerate(ordered)]
+
+
+def place(pieces, dim, extent):
+    shape = list(pieces[0][1].shape)
+    shape[dim] = extent
+    full = jnp.zeros(shape, pieces[0][1].dtype)
+    for at, piece in pieces:
         start = [0] * len(shape)
-        start[dim] = ((index + offset) % size) * block.shape[dim]
+        start[dim] = at
         full = lax.dynamic_update_slice(full, piece, start)
     return full
+
+
+def piecewise_dot(pieces, weights):
+    total = None
+    for at, piece in pieces:
+        rows = lax.dynamic_slice_in_dim(weights, at, piece.shape[1], axis=0)
+        term = jnp.dot(piece, rows, preferred_element_type=jnp.float32)
+        total = term if total is None else total + term
+    return total.astype(jnp.bfloat16)
 
 
 def from_behind(block, axis, distance):
@@ -152,15 +165,17 @@
     n_proj = n_q + 2 * n_kv
     pair = jnp.stack([tokens, cotangent])
     pair = lax.all_gather(pair, "yhi", axis=2, tiled=True)
-    full_tokens = ring_gather(pair[0], "z", 1)
-    full_cot = lax.all_gather(pair[1], "z", axis=1, tiled=True)
+    pieces = ring_pieces(pair, "z", 2)
+    feats = pair.shape[2] * len(pieces)
+    tok_pieces = [(at, piece[0]) for at, piece in pieces]
+    cot_pieces = [(at, piece[1]) for at, piece in pieces]
+    full_tokens = place(tok_pieces, 1, feats)
+    full_cot = place(cot_pieces, 1, feats)
     w_cat = jnp.concatenate([w_query, w_key, w_value, w_out.T], axis=1)
     w_full = lax.all_gather(w_cat, SEQ, axis=0, tiled=True)
     proj_full = w_full[:, :n_proj]
-    d_attn = jnp.dot(full_cot, w_full[:, n_proj:], preferred_element_type=jnp.float32).astype(
-        jnp.bfloat16
-    )
-    qkv = jnp.dot(full_tokens, proj_full, preferred_element_type=jnp.float32).astype(jnp.bfloat16)
+    d_attn = piecewise_dot(cot_pieces, w_full[:, n_proj:])
+    qkv = piecewise_dot(tok_pieces, proj_full)
     query = qkv[:, :n_q]
     kv = qkv[:, n_q:]
     earlier = [from_behind(kv, SEQ, distance) for distance in range(reach, 0, -1)]

time: 260 us -> 273 us (1.050)
  local copies, waits for them, and re-layouts: 14.9 us -> 28.4 us
  waiting for transfers between devices: 81.7 us -> 75.1 us
  matrix products: 12.5 us -> 18.5 us
    all_gather x1 -> x0, waiting for transfers between devices: 25 us -> none  [shards(): full_cot = lax.all_gather(pair[1], 'z', axis=1, tiled=True)]
    ppermute x7, waiting for transfers between devices: 24.3 us -> 47.7 us  [the longest x4 47.7 us: ring_pieces(): lax.ppermute(right[-1], axis, [(i, (i + 1) % size) for i in range(size)])]
    dynamic_update_slice x8 -> x9, local copies, waits for them, and re-layouts: 4.15 us -> 10.8 us  [place(): full = lax.dynamic_update_slice(full, piece, start)]
    dot_general x2 -> x16, matrix products: 8.34 us -> 14.4 us  [piecewise_dot(): term = jnp.dot(piece, rows, preferred_element_type=jnp.float32)]
    slice x1 -> x2, local copies, waits for them, and re-layouts: 0.79 us -> 4.87 us  [the longest x1 2.92 us: shards(): proj_full = w_full[:, :n_proj]]
    all_gather x1, waiting for transfers between devices: 2.95 us -> 0.01 us  [shards(): w_full = lax.all_gather(w_cat, SEQ, axis=0, tiled=True)]
  transfers between devices with their start and end apart: 18 -> 17, of which waited for: 10 -> 7; matrix products, arithmetic and copies ran while one was open for 9% -> 12% of each run, Pallas kernels for 0% -> 0%
where the time goes in v7:
time: 273 us; the launch traced here: 272 us
  blocking collectives  85 us (31%)
  waiting for transfers between devices  75.1 us (28%)
  starting transfers between devices  28.7 us (11%)
  local copies, waits for them, and re-layouts  28.4 us (10%)
  matrix products  18.5 us (7%)
  Pallas kernels  16.1 us (6%)
  between operations  14.4 us (5%)
  other arithmetic  5.8 us (2%)
    all_to_all x1, blocking collectives, shards(): lax.all_to_all(token_term.reshape(tok_rows, n_tp, cols), TP, 1, 1, tiled=...  73 us
    ppermute x4, waiting for transfers between devices, ring_pieces(): lax.ppermute(right[-1], axis, [(i, (i + 1) % size) for i in range(size)])  47.7 us
    reduce_scatter x1, waiting for transfers between devices, shards(): lax.psum_scatter(weight_parts, SEQ, scatter_dimension=0, tiled=True)  21.6 us
    ppermute x8, starting transfers between devices, from_behind(): return lax.ppermute(block, axis, route)  18.8 us
    dot_general x16, matrix products, piecewise_dot(): term = jnp.dot(piece, rows, preferred_element_type=jnp.float32)  14.4 us
    all_gather x1, blocking collectives, shards(): pair = lax.all_gather(pair, 'yhi', axis=2, tiled=True)  12 us
    dynamic_update_slice x9, local copies, waits for them, and re-layouts, place(): full = lax.dynamic_update_slice(full, piece, start)  10.8 us
    pallas_call x1, Pallas kernels, weight_terms(): pl.pallas_call(weight_terms_kernel, grid=(feats // block,), in_specs=[pl....  9.33 us
  transfers between devices with their start and end apart: 17, of which 7 were waited for; matrix products, arithmetic and copies ran while one was open for 12% of the time, Pallas kernels for 0%

profile of v7, /device:TPU:128, one launch (start us, length us, event | category | flops | bytes accessed | tf_op | source)
XLA Modules:
  0.0 272.0 jit_solution(12072369107422347843)
XLA Ops:
  7.2 1.9 pad_maximum_fusion
  9.2 1.0 pad_maximum_fusion.1
  10.3 12.0 %all_gather.6 = bf16[2,256,672]{1,2,0:T(8,128)(2,1)S(1)} all-gather(bf16[2,256,336]{1,2,0:T(8,128)(2,1)S(1)} %pad_maximum_fusion.1), channel_id=1, replica_groups=mesh['ylo'=2,'x'=4,'core'=2,'z'=8,'yhi'=2] {'yhi'}, dimensions={2}, use_global_device_ids=true | all-gather | bytes 1032192 | tf_op jit(solution)/shard_map/all_gather | solution.py:167
  22.2 1.0 collective-permute-start.3
  23.3 2.2 collective-permute-start
  25.5 14.3 %collective-permute-done.3 = bf16[2,256,672]{1,2,0:T(8,128)(2,1)S(1)} collective-permute-done((bf16[2,256,672]{1,2,0:T(8,128)(2,1)S(1)}, bf16[2,256,672]{1,2,0:T(8,128)(2,1)S(1)}, u32[]{:S(2)}, u32[]{:S(2)}) %collective-permute-start.3) | collective-permute-done | bytes 688160 | tf_op jit(solution)/shard_map/ppermute | solution.py:27
  39.8 3.2 %collective-permute-start.1 = (bf16[2,256,672]{1,2,0:T(8,128)(2,1)}, bf16[2,256,672]{1,2,0:T(8,128)(2,1)}, u32[]{:S(2)}, u32[]{:S(2)}) collective-permute-start(bf16[2,256,672]{1,2,0:T(8,128)(2,1)} %collective-permute-done), channel_id=1, source_target_pairs={{0,14},{2,0},{4,2},{6,4},{8,6},{10,8},{12,10},{14,12},{1,15},{3,1}... | collective-permute-start | bytes 2064392 | tf_op jit(solution)/shard_map/ppermute | solution.py:29
  43.0 13.5 %collective-permute-done.4 = bf16[2,256,672]{1,2,0:T(8,128)(2,1)} collective-permute-done((bf16[2,256,672]{1,2,0:T(8,128)(2,1)S(1)}, bf16[2,256,672]{1,2,0:T(8,128)(2,1)}, u32[]{:S(2)}, u32[]{:S(2)}) %collective-permute-start.4) | collective-permute-done | bytes 688160 | tf_op jit(solution)/shard_map/ppermute | solution.py:27
  56.6 0.6 copy.15
  57.5 3.3 %collective-permute-start.2 = (bf16[2,256,672]{1,2,0:T(8,128)(2,1)}, bf16[2,256,672]{1,2,0:T(8,128)(2,1)S(1)}, u32[]{:S(2)}, u32[]{:S(2)}) collective-permute-start(bf16[2,256,672]{1,2,0:T(8,128)(2,1)} %collective-permute-done.1), channel_id=1, source_target_pairs={{0,14},{2,0},{4,2},{6,4},{8,6},{10,8},{12,10},{14,12},{1,15},{3,1}... | collective-permute-start | bytes 2064392 | tf_op jit(solution)/shard_map/ppermute | solution.py:29
  60.8 1.8 broadcast.15.clone.1
  62.5 0.8 fusion.32
  63.3 9.4 %collective-permute-done.5 = bf16[2,256,672]{1,2,0:T(8,128)(2,1)} collective-permute-done((bf16[2,256,672]{1,2,0:T(8,128)(2,1)}, bf16[2,256,672]{1,2,0:T(8,128)(2,1)}, u32[]{:S(2)}, u32[]{:S(2)}) %collective-permute-start.5) | collective-permute-done | bytes 688160 | tf_op jit(solution)/shard_map/ppermute | solution.py:27
  72.7 1.9 fusion.41
  74.6 1.9 fusion.42
  76.4 0.9 fusion.43
  77.3 10.5 %collective-permute-done.6 = bf16[2,256,672]{1,2,0:T(8,128)(2,1)S(1)} collective-permute-done((bf16[2,256,672]{1,2,0:T(8,128)(2,1)}, bf16[2,256,672]{1,2,0:T(8,128)(2,1)S(1)}, u32[]{:S(2)}, u32[]{:S(2)}) %collective-permute-start.6) | collective-permute-done | bytes 688160 | tf_op jit(solution)/shard_map/ppermute | solution.py:27
  87.8 0.8 fusion.44
  88.8 1.9 fusion.45
  90.7 2.9 %slice.117 = bf16[5376,512]{1,0:T(8,128)(2,1)S(1)} slice(bf16[5376,768]{1,0:T(8,128)(2,1)} %all-gather.2.cloned.1.call-done), slice={[0:5376], [0:512]} | slice | bytes 11010048 | tf_op jit(solution)/shard_map/slice | solution.py:176
  93.6 0.4 fusion.18
  94.0 1.4 fusion.12
  95.4 0.4 fusion.8
  95.8 1.4 fusion.10
  97.3 1.5 convolution_add_fusion.3
  98.8 1.4 convolution_add_fusion.2
  100.2 0.4 convolution_add_fusion.1
  100.6 0.4 fusion.3
  101.0 4.9 %collective-permute-start.7 = (bf16[256,256]{1,0:T(8,128)(2,1)S(1)}, bf16[256,256]{1,0:T(8,128)(2,1)S(1)}, u32[]{:S(2)}, u32[]{:S(2)}) collective-permute-start(bf16[256,256]{1,0:T(8,128)(2,1)S(1)} %slice.135), channel_id=1, source_target_pairs={{0,64},{16,80},{32,96},{48,112},{64,128},{80,144},{96,160},{112,17... | collective-permute-start | bytes 393224 | tf_op jit(solution)/shard_map/ppermute | solution.py:57
  105.9 1.3 collective-permute-start.8
  107.2 2.5 collective-permute-start.9
  109.8 4.9 %collective-permute-start.10 = (bf16[256,256]{1,0:T(8,128)(2,1)S(1)}, bf16[256,256]{1,0:T(8,128)(2,1)S(1)}, u32[]{:S(2)}, u32[]{:S(2)}) collective-permute-start(bf16[256,256]{1,0:T(8,128)(2,1)S(1)} %slice.135), channel_id=1, source_target_pairs={{0,16},{16,32},{32,48},{48,64},{64,80},{80,96},{96,112},{112,128},... | collective-permute-start | bytes 393224 | tf_op jit(solution)/shard_map/ppermute | solution.py:57
  114.7 2.0 slice.127
  116.7 0.3 fusion.30
  117.0 0.3 fusion.20
  117.3 1.3 fusion.22
  118.6 1.3 fusion.24
  119.9 1.3 convolution_add_fusion.7
  121.2 1.3 convolution_add_fusion.6
  122.5 0.3 convolution_add_fusion.5
  122.8 1.0 fusion.7.d_ref
  123.9 0.7 constant_dynamic-update-slice_fusion
  124.6 0.8 copy-done.8
  125.4 6.8 %shard_map.110 = (bf16[256,256]{1,0:T(8,128)(2,1)}, bf16[256,256]{1,0:T(8,128)(2,1)}, f32[1280,256]{1,0:T(8,128)}) custom-call(bf16[256,256]{1,0:T(8,128)(2,1)} %get-tuple-element.34.q_ref, bf16[256,256]{1,0:T(8,128)(2,1)} %fusion.7.d_ref, bf16[1280,256]{1,0:T(8,128)(2,1)} %copy-done.8, f32[2,1152]{1,0:T(2,128)} %bitcast.98), custom_call_target="tpu_custom_call" | custom-call | tf_op jit(solution)/shard_map/pallas_call | solution.py:113
  132.2 1.3 fusion.65
  133.5 1.3 collective-permute-start.14
  134.8 1.3 collective-permute-start.13
  136.1 1.3 collective-permute-start.12
  137.4 1.3 collective-permute-start.11
  138.7 1.9 fusion.46
  140.6 0.8 fusion.47
  141.4 3.7 %collective-permute-done.14 = f32[256,256]{1,0:T(8,128)S(1)} collective-permute-done((f32[256,256]{1,0:T(8,128)S(1)}, f32[256,256]{1,0:T(8,128)S(1)}, u32[]{:S(2)}, u32[]{:S(2)}) %collective-permute-start.14) | collective-permute-done | bytes 262176 | tf_op jit(solution)/shard_map/ppermute | solution.py:57
  145.2 2.1 collective-permute-done.12
  147.2 1.0 add_convert_fusion
  148.2 0.7 pad_maximum_fusion.2.ga_ref
  149.0 9.3 %shard_map.111 = bf16[5376,768]{1,0:T(8,128)(2,1)} custom-call(bf16[5376,256]{1,0:T(8,128)(2,1)} %bitcast.20.tok_ref, bf16[5376,256]{1,0:T(8,128)(2,1)} %bitcast.93, bf16[256,512]{1,0:T(8,128)(2,1)} %pad_maximum_fusion.2.ga_ref, bf16[256,256]{1,0:T(8,128)(2,1)} %get-tuple-element.10.attn_ref), custom_call_target="tpu_custom_call" | custom-call | tf_op jit(solution)/shard_map/pallas_call | solution.py:132
  158.3 0.9 copy-done.10
  159.2 4.2 %convolution_convert_fusion = bf16[256,5376]{1,0:T(8,128)(2,1)S(1)} fusion(bf16[256,256]{1,0:T(8,128)(2,1)S(1)} %add_convert_fusion, bf16[256,256]{1,0:T(8,128)(2,1)S(1)} %copy-done.10, bf16[5376,768]{1,0:T(8,128)(2,1)} %all-gather.2.cloned.1.call-done), kind=kOutput, calls=%fused_computation | convolution fusion | flops 1411186688 | bytes 8519680 | tf_op jit(solution)/shard_map/dot_general | solution.py:147
  163.4 2.8 %copy.12 = bf16[256,5376]{0,1:T(8,128)(2,1)} copy(bf16[256,5376]{1,0:T(8,128)(2,1)S(1)} %convolution_convert_fusion) | data formatting | bytes 5505024 | tf_op jit(solution)/shard_map/convert_element_type | solution.py:195
  166.2 73.0 %all_to_all.5 = bf16[256,16,336]{0,2,1:T(8,128)(2,1)S(1)} all-to-all(bf16[256,16,336]{0,2,1:T(8,128)(2,1)} %bitcast.94), channel_id=1, replica_groups=mesh['ylo'=2,'x'=4,'core'=2,'z'=8,'yhi'=2] {'z','yhi'}, dimensions={1} | all-to-all | bytes 5505024 | tf_op jit(solution)/shard_map/all_to_all | solution.py:198
  239.2 1.1 reduce_sum.12
  240.3 21.6 %reduce-scatter.2.cloned.1.call-done = bf16[336,768]{1,0:T(8,128)(2,1)} async-done(((bf16[5376,768]{1,0:T(8,128)(2,1)}), bf16[336,768]{1,0:T(8,128)(2,1)}) %reduce-scatter.2.cloned.1.call-update) | async-done | bytes 516112 | tf_op jit(solution)/shard_map/reduce_scatter | solution.py:201
  261.8 1.8 slice_bitcast_fusion.32
  263.6 1.6 fusion.66
  (48 shorter events, 0.7 us)
Async XLA Ops:
  7.2 35.8 %copy-start.11 = (s32[2,9]{1,0:T(2,128)S(1)}, s32[2,9]{1,0:T(2,128)}, u32[]{:S(2)}) copy-start(s32[2,9]{1,0:T(2,128)} %param.13) | copy-start | bytes 220
  7.2 83.5 %all-gather.2.cloned.1.call-start = ((), (), s32[]{:S(2)}) async-start(), calls=%async_computation.2 | async-start | bytes 8773632 | tf_op jit(solution)/shard_map/all_gather | solution.py:175
  9.2 252.6 %reduce-scatter.2.cloned.1.call-start = ((), (), s32[]{:S(2)}) async-start(), calls=%async_computation.3 | async-start | bytes 8773632 | tf_op jit(solution)/shard_map/reduce_scatter | solution.py:201
  22.2 17.5 %collective-permute-start.3 = (bf16[2,256,672]{1,2,0:T(8,128)(2,1)S(1)}, bf16[2,256,672]{1,2,0:T(8,128)(2,1)S(1)}, u32[]{:S(2)}, u32[]{:S(2)}) collective-permute-start(bf16[2,256,672]{1,2,0:T(8,128)(2,1)S(1)} %all_gather.6), channel_id=1, source_target_pairs={{0,2},{2,4},{4,6},{6,8},{8,10},{10,12},{12,14},{14,0},{1,3},{3,5},... | collective-permute-start | bytes 2064392 | tf_op jit(solution)/shard_map/ppermute | solution.py:27
  23.3 16.5 %collective-permute-start = (bf16[2,256,672]{1,2,0:T(8,128)(2,1)S(1)}, bf16[2,256,672]{1,2,0:T(8,128)(2,1)}, u32[]{:S(2)}, u32[]{:S(2)}) collective-permute-start(bf16[2,256,672]{1,2,0:T(8,128)(2,1)S(1)} %all_gather.6), channel_id=1, source_target_pairs={{0,14},{2,0},{4,2},{6,4},{8,6},{10,8},{12,10},{14,12},{1,15},{3,1}... | collective-permute-start | bytes 2064392 | tf_op jit(solution)/shard_map/ppermute | solution.py:29
  39.8 17.5 %copy-start.5 = (bf16[2,256,672]{1,2,0:T(8,128)(2,1)}, bf16[2,256,672]{1,2,0:T(8,128)(2,1)S(1)}, u32[]{:S(2)}) copy-start(bf16[2,256,672]{1,2,0:T(8,128)(2,1)S(1)} %collective-permute-done.3) | copy-start | bytes 2064388
  39.8 16.8 %collective-permute-start.4 = (bf16[2,256,672]{1,2,0:T(8,128)(2,1)S(1)}, bf16[2,256,672]{1,2,0:T(8,128)(2,1)}, u32[]{:S(2)}, u32[]{:S(2)}) collective-permute-start(bf16[2,256,672]{1,2,0:T(8,128)(2,1)S(1)} %collective-permute-done.3), channel_id=1, source_target_pairs={{0,2},{2,4},{4,6},{6,8},{8,10},{10,12},{12,14},{14,0},{1,3},{3,5},... | collective-permute-start | bytes 2064392 | tf_op jit(solution)/shard_map/ppermute | solution.py:27
  39.8 17.7 %collective-permute-start.1 = (bf16[2,256,672]{1,2,0:T(8,128)(2,1)}, bf16[2,256,672]{1,2,0:T(8,128)(2,1)}, u32[]{:S(2)}, u32[]{:S(2)}) collective-permute-start(bf16[2,256,672]{1,2,0:T(8,128)(2,1)} %collective-permute-done), channel_id=1, source_target_pairs={{0,14},{2,0},{4,2},{6,4},{8,6},{10,8},{12,10},{14,12},{1,15},{3,1}... | collective-permute-start | bytes 2064392 | tf_op jit(solution)/shard_map/ppermute | solution.py:29
  56.5 16.1 %collective-permute-start.5 = (bf16[2,256,672]{1,2,0:T(8,128)(2,1)}, bf16[2,256,672]{1,2,0:T(8,128)(2,1)}, u32[]{:S(2)}, u32[]{:S(2)}) collective-permute-start(bf16[2,256,672]{1,2,0:T(8,128)(2,1)} %collective-permute-done.4), channel_id=1, source_target_pairs={{0,2},{2,4},{4,6},{6,8},{8,10},{10,12},{12,14},{14,0},{1,3},{3,5},... | collective-permute-start | bytes 2064392 | tf_op jit(solution)/shard_map/ppermute | solution.py:27
  57.5 19.0 %collective-permute-start.2 = (bf16[2,256,672]{1,2,0:T(8,128)(2,1)}, bf16[2,256,672]{1,2,0:T(8,128)(2,1)S(1)}, u32[]{:S(2)}, u32[]{:S(2)}) collective-permute-start(bf16[2,256,672]{1,2,0:T(8,128)(2,1)} %collective-permute-done.1), channel_id=1, source_target_pairs={{0,14},{2,0},{4,2},{6,4},{8,6},{10,8},{12,10},{14,12},{1,15},{3,1}... | collective-permute-start | bytes 2064392 | tf_op jit(solution)/shard_map/ppermute | solution.py:29
  72.7 15.2 %collective-permute-start.6 = (bf16[2,256,672]{1,2,0:T(8,128)(2,1)}, bf16[2,256,672]{1,2,0:T(8,128)(2,1)S(1)}, u32[]{:S(2)}, u32[]{:S(2)}) collective-permute-start(bf16[2,256,672]{1,2,0:T(8,128)(2,1)} %collective-permute-done.5), channel_id=1, source_target_pairs={{0,2},{2,4},{4,6},{6,8},{8,10},{10,12},{12,14},{14,0},{1,3},{3,5},... | collective-permute-start | bytes 2064392 | tf_op jit(solution)/shard_map/ppermute | solution.py:27
  76.4 12.2 %copy-start.1 = (bf16[2,256,672]{1,2,0:T(8,128)(2,1)}, bf16[2,256,672]{1,2,0:T(8,128)(2,1)S(1)}, u32[]{:S(2)}) copy-start(bf16[2,256,672]{1,2,0:T(8,128)(2,1)S(1)} %collective-permute-done.2) | copy-start | bytes 2064388
  87.8 1.0 copy-start.3
  93.6 1.8 copy-start.6
  95.8 4.3 %copy-start.2 = (bf16[2,256,672]{1,2,0:T(8,128)(2,1)S(1)}, bf16[2,256,672]{1,2,0:T(8,128)(2,1)}, u32[]{:S(2)}) copy-start(bf16[2,256,672]{1,2,0:T(8,128)(2,1)} %copy-done.1) | copy-start | bytes 2064388
  97.3 3.3 %copy-start.4 = (bf16[2,256,672]{1,2,0:T(8,128)(2,1)S(1)}, bf16[2,256,672]{1,2,0:T(8,128)(2,1)}, u32[]{:S(2)}) copy-start(bf16[2,256,672]{1,2,0:T(8,128)(2,1)} %copy-done.3) | copy-start | bytes 2064388
  101.0 22.8 %collective-permute-start.7 = (bf16[256,256]{1,0:T(8,128)(2,1)S(1)}, bf16[256,256]{1,0:T(8,128)(2,1)S(1)}, u32[]{:S(2)}, u32[]{:S(2)}) collective-permute-start(bf16[256,256]{1,0:T(8,128)(2,1)S(1)} %slice.135), channel_id=1, source_target_pairs={{0,64},{16,80},{32,96},{48,112},{64,128},{80,144},{96,160},{112,17... | collective-permute-start | bytes 393224 | tf_op jit(solution)/shard_map/ppermute | solution.py:57
  105.9 17.9 %collective-permute-start.8 = (bf16[256,256]{1,0:T(8,128)(2,1)S(1)}, bf16[256,256]{1,0:T(8,128)(2,1)S(1)}, u32[]{:S(2)}, u32[]{:S(2)}) collective-permute-start(bf16[256,256]{1,0:T(8,128)(2,1)S(1)} %slice.135), channel_id=1, source_target_pairs={{0,48},{16,64},{32,80},{48,96},{64,112},{80,128},{96,144},{112,160... | collective-permute-start | bytes 393224 | tf_op jit(solution)/shard_map/ppermute | solution.py:57
  107.2 16.6 %collective-permute-start.9 = (bf16[256,256]{1,0:T(8,128)(2,1)S(1)}, bf16[256,256]{1,0:T(8,128)(2,1)S(1)}, u32[]{:S(2)}, u32[]{:S(2)}) collective-permute-start(bf16[256,256]{1,0:T(8,128)(2,1)S(1)} %slice.135), channel_id=1, source_target_pairs={{0,32},{16,48},{32,64},{48,80},{64,96},{80,112},{96,128},{112,144}... | collective-permute-start | bytes 393224 | tf_op jit(solution)/shard_map/ppermute | solution.py:57
  109.8 14.1 %collective-permute-start.10 = (bf16[256,256]{1,0:T(8,128)(2,1)S(1)}, bf16[256,256]{1,0:T(8,128)(2,1)S(1)}, u32[]{:S(2)}, u32[]{:S(2)}) collective-permute-start(bf16[256,256]{1,0:T(8,128)(2,1)S(1)} %slice.135), channel_id=1, source_target_pairs={{0,16},{16,32},{32,48},{48,64},{64,80},{80,96},{96,112},{112,128},... | collective-permute-start | bytes 393224 | tf_op jit(solution)/shard_map/ppermute | solution.py:57
  123.9 16.8 %copy-start.7 = (bf16[2,256,672]{1,2,0:T(8,128)(2,1)S(1)}, bf16[2,256,672]{1,2,0:T(8,128)(2,1)}, u32[]{:S(2)}) copy-start(bf16[2,256,672]{1,2,0:T(8,128)(2,1)} %copy-done.5) | copy-start | bytes 2064388
  124.6 0.8 copy-start.8
  132.2 16.0 %copy-start.9 = (bf16[256,256]{1,0:T(8,128)(2,1)S(1)}, bf16[256,256]{1,0:T(8,128)(2,1)}, u32[]{:S(2)}) copy-start(bf16[256,256]{1,0:T(8,128)(2,1)} %get-tuple-element.8) | copy-start | bytes 393220
  133.5 11.6 %collective-permute-start.14 = (f32[256,256]{1,0:T(8,128)S(1)}, f32[256,256]{1,0:T(8,128)S(1)}, u32[]{:S(2)}, u32[]{:S(2)}) collective-permute-start(f32[256,256]{1,0:T(8,128)S(1)} %get-tuple-element.12), channel_id=1, source_target_pairs={{64,0},{80,16},{96,32},{112,48},{128,64},{144,80},{160,96},{176,11... | collective-permute-start | bytes 786440 | tf_op jit(solution)/shard_map/ppermute | solution.py:57
  134.8 10.3 %collective-permute-start.13 = (f32[256,256]{1,0:T(8,128)S(1)}, f32[256,256]{1,0:T(8,128)S(1)}, u32[]{:S(2)}, u32[]{:S(2)}) collective-permute-start(f32[256,256]{1,0:T(8,128)S(1)} %get-tuple-element.13), channel_id=1, source_target_pairs={{48,0},{64,16},{80,32},{96,48},{112,64},{128,80},{144,96},{160,112... | collective-permute-start | bytes 786440 | tf_op jit(solution)/shard_map/ppermute | solution.py:57
  136.1 11.1 %collective-permute-start.12 = (f32[256,256]{1,0:T(8,128)S(1)}, f32[256,256]{1,0:T(8,128)S(1)}, u32[]{:S(2)}, u32[]{:S(2)}) collective-permute-start(f32[256,256]{1,0:T(8,128)S(1)} %get-tuple-element.14), channel_id=1, source_target_pairs={{32,0},{48,16},{64,32},{80,48},{96,64},{112,80},{128,96},{144,112}... | collective-permute-start | bytes 786440 | tf_op jit(solution)/shard_map/ppermute | solution.py:57
  137.4 9.8 %collective-permute-start.11 = (f32[256,256]{1,0:T(8,128)S(1)}, f32[256,256]{1,0:T(8,128)S(1)}, u32[]{:S(2)}, u32[]{:S(2)}) collective-permute-start(f32[256,256]{1,0:T(8,128)S(1)} %get-tuple-element.11), channel_id=1, source_target_pairs={{16,0},{32,16},{48,32},{64,48},{80,64},{96,80},{112,96},{128,112},... | collective-permute-start | bytes 786440 | tf_op jit(solution)/shard_map/ppermute | solution.py:57
  141.4 7.6 %copy-start = (bf16[256,5376]{0,1:T(8,128)(2,1)}, bf16[256,5376]{0,1:T(8,128)(2,1)S(1)}, u32[]{:S(2)}) copy-start(bf16[256,5376]{0,1:T(8,128)(2,1)S(1)} %get-tuple-element.15) | copy-start | bytes 8257540
  158.3 0.9 copy-start.10
Sparse Core Ops, SparseCore 0:
  9.8 55.4 all-gather.1
  158.4 103.3 reduce-scatter.1

commit v8 on v5

--- a/solution.py
+++ b/solution.py
@@ -107,27 +107,49 @@
     )(query, d_attn, kv_ext, listed)
 
 
-def weight_terms_kernel(tok_ref, cot_ref, ga_ref, attn_ref, out_ref):
-    n_act = ga_ref.shape[1]
-    out_ref[:, :n_act] = _nn(tok_ref[...], ga_ref[...]).astype(out_ref.dtype)
-    out_ref[:, n_act:] = _nn(cot_ref[...], attn_ref[...]).astype(out_ref.dtype)
-
-
-def weight_terms(tokens_t, cot_t, grad_act, attn, block=768):
+def weight_terms_kernel(tok_ref, cot_ref, gq_ref, attn_ref, out_ref):
+    n_q = gq_ref.shape[1]
+    n_attn = attn_ref.shape[1]
+    width = out_ref.shape[1]
+    out_ref[:, :n_q] = _nn(tok_ref[...], gq_ref[...]).astype(out_ref.dtype)
+    out_ref[:, n_q : width - n_attn] = jnp.zeros((out_ref.shape[0], width - n_attn - n_q), out_ref.dtype)
+    out_ref[:, width - n_attn :] = _nn(cot_ref[...], attn_ref[...]).astype(out_ref.dtype)
+
+
+def kv_terms_kernel(tok_ref, gkv_ref, base_ref, out_ref):
+    del base_ref
+    out_ref[...] = _nn(tok_ref[...], gkv_ref[...]).astype(out_ref.dtype)
+
+
+def weight_terms(tokens_t, cot_t, grad_q, grad_kv, attn, block=768):
     feats, rows = tokens_t.shape
-    n_act, n_attn = grad_act.shape[1], attn.shape[1]
-    return pl.pallas_call(
+    n_q, n_kv, n_attn = grad_q.shape[1], grad_kv.shape[1], attn.shape[1]
+    width = n_q + n_kv + n_attn
+    first = pl.pallas_call(
         weight_terms_kernel,
         grid=(feats // block,),
         in_specs=[
             pl.BlockSpec((block, rows), lambda i: (i, 0)),
             pl.BlockSpec((block, rows), lambda i: (i, 0)),
-            pl.BlockSpec((rows, n_act), lambda i: (0, 0)),
+            pl.BlockSpec((rows, n_q), lambda i: (0, 0)),
             pl.BlockSpec((rows, n_attn), lambda i: (0, 0)),
         ],
-        out_specs=pl.BlockSpec((block, n_act + n_attn), lambda i: (i, 0)),
-        out_shape=jax.ShapeDtypeStruct((feats, n_act + n_attn), jnp.bfloat16),
-    )(tokens_t, cot_t, grad_act, attn)
+        out_specs=pl.BlockSpec((block, width), lambda i: (i, 0)),
+        out_shape=jax.ShapeDtypeStruct((feats, width), jnp.bfloat16),
+    )(tokens_t, cot_t, grad_q, attn)
+    column = n_q // n_kv
+    return pl.pallas_call(
+        kv_terms_kernel,
+        grid=(feats // block,),
+        in_specs=[
+            pl.BlockSpec((block, rows), lambda i: (i, 0)),
+            pl.BlockSpec((rows, n_kv), lambda i: (0, 0)),
+            pl.BlockSpec(memory_space=pl.ANY),
+        ],
+        out_specs=pl.BlockSpec((block, n_kv), lambda i: (i, column)),
+        out_shape=jax.ShapeDtypeStruct((feats, width), jnp.bfloat16),
+        input_output_aliases={2: 0},
+    )(tokens_t, grad_kv, first)
 
 
 def contract_cols(left, right):
@@ -182,7 +204,7 @@
     cols = token_term.shape[1] // n_tp
     parts = lax.all_to_all(token_term.reshape(tok_rows, n_tp, cols), TP, 1, 1, tiled=True)
     grad_tokens = parts.astype(jnp.float32).sum(axis=1).astype(jnp.bfloat16)
-    weight_parts = weight_terms(full_tokens.T, full_cot.T, grad_act, attn)
+    weight_parts = weight_terms(full_tokens.T, full_cot.T, grad_q, grad_kv, attn)
     summed = lax.psum_scatter(weight_parts, SEQ, scatter_dimension=0, tiled=True)
     grad_query = summed[:, :n_q]
     grad_key = summed[:, n_q : n_q + n_kv]

time: 260 us -> 257 us (0.988)
  waiting for transfers between devices: 81.7 us -> 70.6 us
  Pallas kernels: 16.1 us -> 22 us
    ppermute x8, waiting for transfers between devices: 8.48 us -> 0.02 us  [from_behind(): return lax.ppermute(block, axis, route)]
    pallas_call x0 -> x1, Pallas kernels: none -> 6.35 us  [weight_terms(): pl.pallas_call(kv_terms_kernel, grid=(feats // block,), in_specs=[pl.Bloc...]
    reduce_scatter x1, waiting for transfers between devices: 20.9 us -> 18.3 us  [shards(): lax.psum_scatter(weight_parts, SEQ, scatter_dimension=0, tiled=True)]
  transfers between devices with their start and end apart: 18 -> 18, of which waited for: 10 -> 7; matrix products, arithmetic and copies ran while one was open for 9% -> 9% of each run, Pallas kernels for 0% -> 3%
where the time goes in v8:
time: 257 us; the launch traced here: 256 us
  blocking collectives  86.2 us (34%)
  waiting for transfers between devices  70.6 us (27%)
  starting transfers between devices  28.7 us (11%)
  Pallas kernels  22 us (9%)
  local copies, waits for them, and re-layouts  15.8 us (6%)
  between operations  14 us (5%)
  matrix products  12.5 us (5%)
  other arithmetic  5.8 us (2%)
    all_to_all x1, blocking collectives, shards(): lax.all_to_all(token_term.reshape(tok_rows, n_tp, cols), TP, 1, 1, tiled=...  74.2 us
    all_gather x1, waiting for transfers between devices, shards(): full_cot = lax.all_gather(pair[1], 'z', axis=1, tiled=True)  25 us
    ppermute x4, waiting for transfers between devices, ring_gather(): lax.ppermute(right[-1], axis, [(i, (i + 1) % size) for i in range(size)])  24.3 us
    ppermute x8, starting transfers between devices, from_behind(): return lax.ppermute(block, axis, route)  18.7 us
    reduce_scatter x1, waiting for transfers between devices, shards(): lax.psum_scatter(weight_parts, SEQ, scatter_dimension=0, tiled=True)  18.3 us
    all_gather x1, blocking collectives, shards(): pair = lax.all_gather(pair, 'yhi', axis=2, tiled=True)  12 us
    pallas_call x1, Pallas kernels, weight_terms(): pl.pallas_call(weight_terms_kernel, grid=(feats // block,), in_specs=[pl....  8.91 us
    ppermute x3, starting transfers between devices, ring_gather(): lax.ppermute(left[-1], axis, [(i, (i - 1) % size) for i in range(size)])  8.75 us
  transfers between devices with their start and end apart: 18, of which 7 were waited for; matrix products, arithmetic and copies ran while one was open for 9% of the time, Pallas kernels for 3%

profile of v8, /device:TPU:128, one launch (start us, length us, event | category | flops | bytes accessed | tf_op | source)
XLA Modules:
  0.0 255.7 jit_solution(12541981160581706364)
XLA Ops:
  7.2 0.0 all-gather.4.cloned.1.call-start
  7.2 2.0 pad_maximum_fusion
  9.2 0.0 all-gather.4.cloned.1.call-update
  9.2 0.0 all-gather.6.cloned.1.call-start
  9.3 1.0 pad_maximum_fusion.1
  10.3 12.0 %all_gather.9 = bf16[2,256,672]{1,2,0:T(8,128)(2,1)S(1)} all-gather(bf16[2,256,336]{1,2,0:T(8,128)(2,1)S(1)} %pad_maximum_fusion.1), channel_id=1, replica_groups=mesh['ylo'=2,'x'=4,'core'=2,'z'=8,'yhi'=2] {'yhi'}, dimensions={2}, use_global_device_ids=true | all-gather | bytes 1032192 | tf_op jit(solution)/shard_map/all_gather | solution.py:176
  22.3 0.8 fusion.19
  23.1 0.0 all-gather.6.cloned.1.call-update
  23.1 0.0 reduce-scatter.2.cloned.1.call-start
  23.1 1.1 collective-permute-start.3
  24.2 2.2 collective-permute-start
  26.5 7.0 %collective-permute-done.3 = bf16[256,672]{0,1:T(8,128)(2,1)} collective-permute-done((bf16[256,672]{0,1:T(8,128)(2,1)S(1)}, bf16[256,672]{0,1:T(8,128)(2,1)}, u32[]{:S(2)}, u32[]{:S(2)}) %collective-permute-start.3) | collective-permute-done | bytes 344096 | tf_op jit(solution)/shard_map/ppermute | solution.py:27
  33.5 0.0 collective-permute-start.4
  33.5 0.0 collective-permute-done
  33.5 3.2 %collective-permute-start.1 = (bf16[256,672]{0,1:T(8,128)(2,1)}, bf16[256,672]{0,1:T(8,128)(2,1)}, u32[]{:S(2)}, u32[]{:S(2)}) collective-permute-start(bf16[256,672]{0,1:T(8,128)(2,1)} %collective-permute-done), channel_id=1, source_target_pairs={{0,14},{2,0},{4,2},{6,4},{8,6},{10,8},{12,10},{14,12},{1,15},{3,1}... | collective-permute-start | bytes 1032200 | tf_op jit(solution)/shard_map/ppermute | solution.py:29
  36.7 0.2 broadcast_in_dim.6
  36.9 6.1 %collective-permute-done.4 = bf16[256,672]{0,1:T(8,128)(2,1)} collective-permute-done((bf16[256,672]{0,1:T(8,128)(2,1)}, bf16[256,672]{0,1:T(8,128)(2,1)}, u32[]{:S(2)}, u32[]{:S(2)}) %collective-permute-start.4) | collective-permute-done | bytes 344096 | tf_op jit(solution)/shard_map/ppermute | solution.py:27
  43.1 0.0 collective-permute-start.5
  43.1 0.0 collective-permute-done.1
  43.1 3.3 %collective-permute-start.2 = (bf16[256,672]{0,1:T(8,128)(2,1)}, bf16[256,672]{0,1:T(8,128)(2,1)S(1)}, u32[]{:S(2)}, u32[]{:S(2)}) collective-permute-start(bf16[256,672]{0,1:T(8,128)(2,1)} %collective-permute-done.1), channel_id=1, source_target_pairs={{0,14},{2,0},{4,2},{6,4},{8,6},{10,8},{12,10},{14,12},{1,15},{3,1}... | collective-permute-start | bytes 1032200 | tf_op jit(solution)/shard_map/ppermute | solution.py:29
  46.4 0.1 broadcast_bitcast_fusion
  46.5 0.6 copy.16
  47.1 4.7 %collective-permute-done.5 = bf16[256,672]{0,1:T(8,128)(2,1)S(1)} collective-permute-done((bf16[256,672]{0,1:T(8,128)(2,1)}, bf16[256,672]{0,1:T(8,128)(2,1)S(1)}, u32[]{:S(2)}, u32[]{:S(2)}) %collective-permute-start.5) | collective-permute-done | bytes 344096 | tf_op jit(solution)/shard_map/ppermute | solution.py:27
  51.8 0.0 collective-permute-start.6
  51.8 1.0 constant_dynamic-update-slice_fusion.11
  52.9 1.0 constant_dynamic-update-slice_fusion.10
  53.9 0.0 collective-permute-done.2
  53.9 6.4 %collective-permute-done.6 = bf16[256,672]{0,1:T(8,128)(2,1)S(1)} collective-permute-done((bf16[256,672]{0,1:T(8,128)(2,1)S(1)}, bf16[256,672]{0,1:T(8,128)(2,1)S(1)}, u32[]{:S(2)}, u32[]{:S(2)}) %collective-permute-start.6) | collective-permute-done | bytes 344096 | tf_op jit(solution)/shard_map/ppermute | solution.py:27
  60.4 1.0 constant_dynamic-update-slice_fusion.6
  61.4 1.0 constant_dynamic-update-slice_fusion.5
  62.4 2.9 %all-gather.4.cloned.1.call-done = bf16[5376,768]{1,0:T(8,128)(2,1)} async-done(((bf16[336,768]{1,0:T(8,128)(2,1)}), bf16[5376,768]{1,0:T(8,128)(2,1)}) %all-gather.4.cloned.1.call-update) | async-done | bytes 8257552 | tf_op jit(solution)/shard_map/all_gather | solution.py:180
  65.3 4.2 %fusion.6 = bf16[256,512]{1,0:T(8,128)(2,1)S(1)} fusion(bf16[256,5376]{0,1:T(8,128)(2,1)S(1)} %constant_dynamic-update-slice_fusion.5, bf16[5376,768]{1,0:T(8,128)(2,1)} %all-gather.4.cloned.1.call-done), kind=kOutput, calls=%fused_computation.7 | convolution fusion | flops 1409417216 | bytes 8519680 | tf_op jit(solution)/shard_map/dot_general | solution.py:185
  69.5 4.5 %collective-permute-start.7 = (bf16[256,256]{1,0:T(8,128)(2,1)S(1)}, bf16[256,256]{1,0:T(8,128)(2,1)S(1)}, u32[]{:S(2)}, u32[]{:S(2)}) collective-permute-start(bf16[256,256]{1,0:T(8,128)(2,1)S(1)} %slice.65), channel_id=1, source_target_pairs={{0,64},{16,80},{32,96},{48,112},{64,128},{80,144},{96,160},{112,17... | collective-permute-start | bytes 393224 | tf_op jit(solution)/shard_map/ppermute | solution.py:44
  74.1 2.3 collective-permute-start.8
  76.4 2.8 %collective-permute-start.9 = (bf16[256,256]{1,0:T(8,128)(2,1)S(1)}, bf16[256,256]{1,0:T(8,128)(2,1)S(1)}, u32[]{:S(2)}, u32[]{:S(2)}) collective-permute-start(bf16[256,256]{1,0:T(8,128)(2,1)S(1)} %slice.65), channel_id=1, source_target_pairs={{0,32},{16,48},{32,64},{48,80},{64,96},{80,112},{96,128},{112,144}... | collective-permute-start | bytes 393224 | tf_op jit(solution)/shard_map/ppermute | solution.py:44
  79.3 3.9 %collective-permute-start.10 = (bf16[256,256]{1,0:T(8,128)(2,1)S(1)}, bf16[256,256]{1,0:T(8,128)(2,1)S(1)}, u32[]{:S(2)}, u32[]{:S(2)}) collective-permute-start(bf16[256,256]{1,0:T(8,128)(2,1)S(1)} %slice.65), channel_id=1, source_target_pairs={{0,16},{16,32},{32,48},{48,64},{64,80},{80,96},{96,112},{112,128},... | collective-permute-start | bytes 393224 | tf_op jit(solution)/shard_map/ppermute | solution.py:44
  83.1 25.0 %all-gather.6.cloned.1.call-done = bf16[1,256,5376]{1,2,0:T(8,128)(2,1)} async-done(((bf16[1,256,672]{1,2,0:T(8,128)(2,1)}), bf16[1,256,5376]{1,2,0:T(8,128)(2,1)}) %all-gather.6.cloned.1.call-update) | async-done | bytes 2752528 | tf_op jit(solution)/shard_map/all_gather | solution.py:178
  108.2 4.2 %fusion.9.d_ref = bf16[256,256]{1,0:T(8,128)(2,1)} fusion(bf16[5376,768]{1,0:T(8,128)(2,1)} %all-gather.4.cloned.1.call-done, bf16[1,256,5376]{1,2,0:T(8,128)(2,1)} %all-gather.6.cloned.1.call-done), kind=kOutput, calls=%fused_computation.8 | convolution fusion | flops 704708608 | bytes 5636096 | tf_op jit(solution)/shard_map/dot_general | solution.py:182
  112.3 0.0 collective-permute-done.7
  112.4 0.0 collective-permute-done.9
  112.4 0.0 collective-permute-done.10
  112.4 0.7 constant_dynamic-update-slice_fusion
  113.1 0.9 copy-done.1
  114.0 6.7 %shard_map.110 = (bf16[256,256]{1,0:T(8,128)(2,1)}, bf16[256,256]{1,0:T(8,128)(2,1)}, f32[1280,256]{1,0:T(8,128)}) custom-call(bf16[256,256]{1,0:T(8,128)(2,1)} %get-tuple-element.22.q_ref, bf16[256,256]{1,0:T(8,128)(2,1)} %fusion.9.d_ref, bf16[1280,256]{1,0:T(8,128)(2,1)} %copy-done.1, f32[2,1152]{1,0:T(2,128)} %bitcast.31), custom_call_target="tpu_custom_call" | custom-call | tf_op jit(solution)/shard_map/pallas_call | solution.py:100
  120.8 1.3 fusion.18
  122.1 1.3 collective-permute-start.14
  123.4 1.3 collective-permute-start.13
  124.7 1.3 collective-permute-start.12
  126.0 1.3 collective-permute-start.11
  127.3 8.9 %shard_map.111.base_ref = bf16[5376,768]{1,0:T(8,128)(2,1)} custom-call(bf16[5376,256]{1,0:T(8,128)(2,1)} %bitcast.24, bf16[5376,256]{1,0:T(8,128)(2,1)} %bitcast.27, bf16[256,256]{1,0:T(8,128)(2,1)} %get-tuple-element.8.gq_ref, bf16[256,256]{1,0:T(8,128)(2,1)} %get-tuple-element.10.attn_ref), custom_call_target="tpu_custom_call" | custom-call | tf_op jit(solution)/shard_map/pallas_call | solution.py:128
  136.2 0.0 collective-permute-done.14
  136.2 0.0 collective-permute-done.12
  136.2 1.7 add_convert_fusion.gkv_ref
  137.9 6.4 %shard_map.112 = bf16[5376,768]{1,0:T(8,128)(2,1)} custom-call(bf16[5376,256]{1,0:T(8,128)(2,1)} %bitcast.25, bf16[256,256]{1,0:T(8,128)(2,1)} %add_convert_fusion.gkv_ref, bf16[5376,768]{1,0:T(8,128)(2,1)} %shard_map.111.base_ref), custom_call_target="tpu_custom_call", output_to_operand_aliasing={{}: (2, {})} | custom-call | tf_op jit(solution)/shard_map/pallas_call | solution.py:141
  144.2 0.0 reduce-scatter.2.cloned.1.call-update
  144.3 0.9 copy-done.2
  145.1 0.1 copy-done.3
  145.2 4.2 %convolution_convert_fusion = bf16[256,5376]{1,0:T(8,128)(2,1)S(1)} fusion(bf16[5376,768]{1,0:T(8,128)(2,1)} %all-gather.4.cloned.1.call-done, bf16[256,256]{1,0:T(8,128)(2,1)S(1)} %copy-done.2, bf16[256,256]{1,0:T(8,128)(2,1)S(1)} %copy-done.3), kind=kOutput, calls=%fused_computation | convolution fusion | flops 1411186688 | bytes 8519680 | tf_op jit(solution)/shard_map/dot_general | solution.py:156
  149.4 2.8 %copy.13 = bf16[256,5376]{0,1:T(8,128)(2,1)} copy(bf16[256,5376]{1,0:T(8,128)(2,1)S(1)} %convolution_convert_fusion) | data formatting | bytes 5505024 | tf_op jit(solution)/shard_map/convert_element_type | solution.py:202
  152.2 74.2 %all_to_all.5 = bf16[256,16,336]{0,2,1:T(8,128)(2,1)S(1)} all-to-all(bf16[256,16,336]{0,2,1:T(8,128)(2,1)} %bitcast.26), channel_id=1, replica_groups=mesh['ylo'=2,'x'=4,'core'=2,'z'=8,'yhi'=2] {'z','yhi'}, dimensions={1} | all-to-all | bytes 5505024 | tf_op jit(solution)/shard_map/all_to_all | solution.py:205
  226.4 1.1 reduce_sum.12
  227.5 18.3 %reduce-scatter.2.cloned.1.call-done = bf16[336,768]{1,0:T(8,128)(2,1)} async-done(((bf16[5376,768]{1,0:T(8,128)(2,1)}), bf16[336,768]{1,0:T(8,128)(2,1)}) %reduce-scatter.2.cloned.1.call-update) | async-done | bytes 516112 | tf_op jit(solution)/shard_map/reduce_scatter | solution.py:208
  245.8 1.8 slice_bitcast_fusion.1
  247.6 1.6 fusion.20
  (20 shorter events, 0.2 us)
Async XLA Ops:
  7.2 58.2 %all-gather.4.cloned.1.call-start = ((), (), s32[]{:S(2)}) async-start(), calls=%async_computation.2 | async-start | bytes 8773632 | tf_op jit(solution)/shard_map/all_gather | solution.py:180
  9.2 98.9 %all-gather.6.cloned.1.call-start = ((), (), s32[]{:S(2)}) async-start(), calls=%async_computation.4 | async-start | bytes 3096576 | tf_op jit(solution)/shard_map/all_gather | solution.py:178
  22.3 20.8 %copy-start.4 = (s32[2,9]{1,0:T(2,128)S(1)}, s32[2,9]{1,0:T(2,128)}, u32[]{:S(2)}) copy-start(s32[2,9]{1,0:T(2,128)} %param.13) | copy-start | bytes 220
  23.1 222.7 %reduce-scatter.2.cloned.1.call-start = ((), (), s32[]{:S(2)}) async-start(), calls=%async_computation.3 | async-start | bytes 8773632 | tf_op jit(solution)/shard_map/reduce_scatter | solution.py:208
  23.1 10.3 %collective-permute-start.3 = (bf16[256,672]{0,1:T(8,128)(2,1)S(1)}, bf16[256,672]{0,1:T(8,128)(2,1)}, u32[]{:S(2)}, u32[]{:S(2)}) collective-permute-start(bf16[256,672]{0,1:T(8,128)(2,1)S(1)} %get-tuple-element.16), channel_id=1, source_target_pairs={{0,2},{2,4},{4,6},{6,8},{8,10},{10,12},{12,14},{14,0},{1,3},{3,5},... | collective-permute-start | bytes 1032200 | tf_op jit(solution)/shard_map/ppermute | solution.py:27
  24.2 9.2 %collective-permute-start = (bf16[256,672]{0,1:T(8,128)(2,1)S(1)}, bf16[256,672]{0,1:T(8,128)(2,1)}, u32[]{:S(2)}, u32[]{:S(2)}) collective-permute-start(bf16[256,672]{0,1:T(8,128)(2,1)S(1)} %get-tuple-element.16), channel_id=1, source_target_pairs={{0,14},{2,0},{4,2},{6,4},{8,6},{10,8},{12,10},{14,12},{1,15},{3,1}... | collective-permute-start | bytes 1032200 | tf_op jit(solution)/shard_map/ppermute | solution.py:29
  33.5 9.6 %collective-permute-start.4 = (bf16[256,672]{0,1:T(8,128)(2,1)}, bf16[256,672]{0,1:T(8,128)(2,1)}, u32[]{:S(2)}, u32[]{:S(2)}) collective-permute-start(bf16[256,672]{0,1:T(8,128)(2,1)} %collective-permute-done.3), channel_id=1, source_target_pairs={{0,2},{2,4},{4,6},{6,8},{8,10},{10,12},{12,14},{14,0},{1,3},{3,5},... | collective-permute-start | bytes 1032200 | tf_op jit(solution)/shard_map/ppermute | solution.py:27
  33.5 9.6 %collective-permute-start.1 = (bf16[256,672]{0,1:T(8,128)(2,1)}, bf16[256,672]{0,1:T(8,128)(2,1)}, u32[]{:S(2)}, u32[]{:S(2)}) collective-permute-start(bf16[256,672]{0,1:T(8,128)(2,1)} %collective-permute-done), channel_id=1, source_target_pairs={{0,14},{2,0},{4,2},{6,4},{8,6},{10,8},{12,10},{14,12},{1,15},{3,1}... | collective-permute-start | bytes 1032200 | tf_op jit(solution)/shard_map/ppermute | solution.py:29
  43.1 8.8 %collective-permute-start.5 = (bf16[256,672]{0,1:T(8,128)(2,1)}, bf16[256,672]{0,1:T(8,128)(2,1)S(1)}, u32[]{:S(2)}, u32[]{:S(2)}) collective-permute-start(bf16[256,672]{0,1:T(8,128)(2,1)} %collective-permute-done.4), channel_id=1, source_target_pairs={{0,2},{2,4},{4,6},{6,8},{8,10},{10,12},{12,14},{14,0},{1,3},{3,5},... | collective-permute-start | bytes 1032200 | tf_op jit(solution)/shard_map/ppermute | solution.py:27
  43.1 10.8 %collective-permute-start.2 = (bf16[256,672]{0,1:T(8,128)(2,1)}, bf16[256,672]{0,1:T(8,128)(2,1)S(1)}, u32[]{:S(2)}, u32[]{:S(2)}) collective-permute-start(bf16[256,672]{0,1:T(8,128)(2,1)} %collective-permute-done.1), channel_id=1, source_target_pairs={{0,14},{2,0},{4,2},{6,4},{8,6},{10,8},{12,10},{14,12},{1,15},{3,1}... | collective-permute-start | bytes 1032200 | tf_op jit(solution)/shard_map/ppermute | solution.py:29
  51.8 8.5 %collective-permute-start.6 = (bf16[256,672]{0,1:T(8,128)(2,1)S(1)}, bf16[256,672]{0,1:T(8,128)(2,1)S(1)}, u32[]{:S(2)}, u32[]{:S(2)}) collective-permute-start(bf16[256,672]{0,1:T(8,128)(2,1)S(1)} %collective-permute-done.5), channel_id=1, source_target_pairs={{0,2},{2,4},{4,6},{6,8},{8,10},{10,12},{12,14},{14,0},{1,3},{3,5},... | collective-permute-start | bytes 1032200 | tf_op jit(solution)/shard_map/ppermute | solution.py:27
  62.4 7.1 %copy-start = (bf16[256,5376]{0,1:T(8,128)(2,1)}, bf16[256,5376]{0,1:T(8,128)(2,1)S(1)}, u32[]{:S(2)}) copy-start(bf16[256,5376]{0,1:T(8,128)(2,1)S(1)} %constant_dynamic-update-slice_fusion.5) | copy-start | bytes 8257540
  69.5 42.8 %collective-permute-start.7 = (bf16[256,256]{1,0:T(8,128)(2,1)S(1)}, bf16[256,256]{1,0:T(8,128)(2,1)S(1)}, u32[]{:S(2)}, u32[]{:S(2)}) collective-permute-start(bf16[256,256]{1,0:T(8,128)(2,1)S(1)} %slice.65), channel_id=1, source_target_pairs={{0,64},{16,80},{32,96},{48,112},{64,128},{80,144},{96,160},{112,17... | collective-permute-start | bytes 393224 | tf_op jit(solution)/shard_map/ppermute | solution.py:44
  74.1 38.3 %collective-permute-start.8 = (bf16[256,256]{1,0:T(8,128)(2,1)S(1)}, bf16[256,256]{1,0:T(8,128)(2,1)S(1)}, u32[]{:S(2)}, u32[]{:S(2)}) collective-permute-start(bf16[256,256]{1,0:T(8,128)(2,1)S(1)} %slice.65), channel_id=1, source_target_pairs={{0,48},{16,64},{32,80},{48,96},{64,112},{80,128},{96,144},{112,160... | collective-permute-start | bytes 393224 | tf_op jit(solution)/shard_map/ppermute | solution.py:44
  76.4 36.0 %collective-permute-start.9 = (bf16[256,256]{1,0:T(8,128)(2,1)S(1)}, bf16[256,256]{1,0:T(8,128)(2,1)S(1)}, u32[]{:S(2)}, u32[]{:S(2)}) collective-permute-start(bf16[256,256]{1,0:T(8,128)(2,1)S(1)} %slice.65), channel_id=1, source_target_pairs={{0,32},{16,48},{32,64},{48,80},{64,96},{80,112},{96,128},{112,144}... | collective-permute-start | bytes 393224 | tf_op jit(solution)/shard_map/ppermute | solution.py:44
  79.3 33.2 %collective-permute-start.10 = (bf16[256,256]{1,0:T(8,128)(2,1)S(1)}, bf16[256,256]{1,0:T(8,128)(2,1)S(1)}, u32[]{:S(2)}, u32[]{:S(2)}) collective-permute-start(bf16[256,256]{1,0:T(8,128)(2,1)S(1)} %slice.65), channel_id=1, source_target_pairs={{0,16},{16,32},{32,48},{48,64},{64,80},{80,96},{96,112},{112,128},... | collective-permute-start | bytes 393224 | tf_op jit(solution)/shard_map/ppermute | solution.py:44
  113.1 0.9 copy-start.1
  122.1 14.1 %collective-permute-start.14 = (f32[256,256]{1,0:T(8,128)S(1)}, f32[256,256]{1,0:T(8,128)S(1)}, u32[]{:S(2)}, u32[]{:S(2)}) collective-permute-start(f32[256,256]{1,0:T(8,128)S(1)} %get-tuple-element.12), channel_id=1, source_target_pairs={{64,0},{80,16},{96,32},{112,48},{128,64},{144,80},{160,96},{176,11... | collective-permute-start | bytes 786440 | tf_op jit(solution)/shard_map/ppermute | solution.py:44
  123.4 12.8 %collective-permute-start.13 = (f32[256,256]{1,0:T(8,128)S(1)}, f32[256,256]{1,0:T(8,128)S(1)}, u32[]{:S(2)}, u32[]{:S(2)}) collective-permute-start(f32[256,256]{1,0:T(8,128)S(1)} %get-tuple-element.13), channel_id=1, source_target_pairs={{48,0},{64,16},{80,32},{96,48},{112,64},{128,80},{144,96},{160,112... | collective-permute-start | bytes 786440 | tf_op jit(solution)/shard_map/ppermute | solution.py:44
  124.7 11.5 %collective-permute-start.12 = (f32[256,256]{1,0:T(8,128)S(1)}, f32[256,256]{1,0:T(8,128)S(1)}, u32[]{:S(2)}, u32[]{:S(2)}) collective-permute-start(f32[256,256]{1,0:T(8,128)S(1)} %get-tuple-element.14), channel_id=1, source_target_pairs={{32,0},{48,16},{64,32},{80,48},{96,64},{112,80},{128,96},{144,112}... | collective-permute-start | bytes 786440 | tf_op jit(solution)/shard_map/ppermute | solution.py:44
  126.0 10.2 %collective-permute-start.11 = (f32[256,256]{1,0:T(8,128)S(1)}, f32[256,256]{1,0:T(8,128)S(1)}, u32[]{:S(2)}, u32[]{:S(2)}) collective-permute-start(f32[256,256]{1,0:T(8,128)S(1)} %get-tuple-element.11), channel_id=1, source_target_pairs={{16,0},{32,16},{48,32},{64,48},{80,64},{96,80},{112,96},{128,112},... | collective-permute-start | bytes 786440 | tf_op jit(solution)/shard_map/ppermute | solution.py:44
  144.2 0.9 copy-start.2
  144.2 1.0 copy-start.3
Sparse Core Ops, SparseCore 0:
  9.8 55.4 all-gather.3
  67.1 40.9 all-gather.5
  144.4 101.3 reduce-scatter.1

commit v9 on v8

--- a/solution.py
+++ b/solution.py
@@ -4,6 +4,7 @@
 import jax.numpy as jnp
 from jax import lax
 from jax.experimental import pallas as pl
+from jax.experimental.pallas import tpu as pltpu
 from jax.sharding import Mesh
 from jax.sharding import PartitionSpec as P
 
@@ -52,7 +53,8 @@
     return lax.dot_general(left, right, (((1,), (0,)), ((), ())), preferred_element_type=jnp.float32)
 
 
-def attention_kernel(q_ref, d_ref, kv_ref, lst_ref, attn_ref, gq_ref, dkv_ref, *, scale, block_len, span, head_dim):
+def attention_kernel(q_ref, d_ref, kv_ref, lst_ref, attn_ref, gq_ref, *rest, scale, block_len, span, head_dim):
+    seg_refs, dkv_ref = rest[:-1], rest[-1]
     n_blocks = q_ref.shape[0] // block_len
     groups = q_ref.shape[1] // head_dim
     width = span * block_len
@@ -88,6 +90,9 @@
             dv_acc = dv_acc + _nn(probs_half.T, db)
         dkv_ref[w0 : w0 + width, :head_dim] += dk_acc * scale
         dkv_ref[w0 : w0 + width, head_dim:] += dv_acc
+    seg = dkv_ref.shape[0] // len(seg_refs)
+    for index, seg_ref in enumerate(seg_refs):
+        seg_ref[...] = dkv_ref[index * seg : (index + 1) * seg, :]
 
 
 def fused_attention(query, kv_ext, d_attn, block_lists, scale, head_dim):
@@ -97,23 +102,28 @@
     body = functools.partial(
         attention_kernel, scale=scale, block_len=block_len, span=span, head_dim=head_dim
     )
-    return pl.pallas_call(
+    n_seg = kv_ext.shape[0] // query.shape[0]
+    seg_shape = jax.ShapeDtypeStruct((query.shape[0], kv_ext.shape[1]), jnp.float32)
+    outs = pl.pallas_call(
         body,
         out_shape=(
             jax.ShapeDtypeStruct(query.shape, jnp.bfloat16),
             jax.ShapeDtypeStruct(query.shape, jnp.bfloat16),
-            jax.ShapeDtypeStruct(kv_ext.shape, jnp.float32),
-        ),
+        )
+        + (seg_shape,) * n_seg,
+        scratch_shapes=[pltpu.VMEM(kv_ext.shape, jnp.float32)],
     )(query, d_attn, kv_ext, listed)
+    return outs[0], outs[1], outs[2:]
 
 
 def weight_terms_kernel(tok_ref, cot_ref, gq_ref, attn_ref, out_ref):
-    n_q = gq_ref.shape[1]
-    n_attn = attn_ref.shape[1]
-    width = out_ref.shape[1]
-    out_ref[:, :n_q] = _nn(tok_ref[...], gq_ref[...]).astype(out_ref.dtype)
-    out_ref[:, n_q : width - n_attn] = jnp.zeros((out_ref.shape[0], width - n_attn - n_q), out_ref.dtype)
-    out_ref[:, width - n_attn :] = _nn(cot_ref[...], attn_ref[...]).astype(out_ref.dtype)
+    @pl.when(pl.program_id(1) == 0)
+    def _():
+        out_ref[...] = _nn(tok_ref[...], gq_ref[...]).astype(out_ref.dtype)
+
+    @pl.when(pl.program_id(1) == 1)
+    def _():
+        out_ref[...] = _nn(cot_ref[...], attn_ref[...]).astype(out_ref.dtype)
 
 
 def kv_terms_kernel(tok_ref, gkv_ref, base_ref, out_ref):
@@ -127,14 +137,14 @@
     width = n_q + n_kv + n_attn
     first = pl.pallas_call(
         weight_terms_kernel,
-        grid=(feats // block,),
+        grid=(feats // block, 2),
         in_specs=[
-            pl.BlockSpec((block, rows), lambda i: (i, 0)),
-            pl.BlockSpec((block, rows), lambda i: (i, 0)),
-            pl.BlockSpec((rows, n_q), lambda i: (0, 0)),
-            pl.BlockSpec((rows, n_attn), lambda i: (0, 0)),
+            pl.BlockSpec((block, rows), lambda i, j: (i, 0)),
+            pl.BlockSpec((block, rows), lambda i, j: (i, 0)),
+            pl.BlockSpec((rows, n_q), lambda i, j: (0, 0)),
+            pl.BlockSpec((rows, n_attn), lambda i, j: (0, 0)),
         ],
-        out_specs=pl.BlockSpec((block, width), lambda i: (i, 0)),
+        out_specs=pl.BlockSpec((block, n_q), lambda i, j: (i, 2 * j)),
         out_shape=jax.ShapeDtypeStruct((feats, width), jnp.bfloat16),
     )(tokens_t, cot_t, grad_q, attn)
     column = n_q // n_kv
@@ -191,12 +201,9 @@
         query, kv_ext, d_attn, block_lists, softmax_scale, head_dim
     )
 
-    def segment(array, index):
-        return array[index * tok_rows : (index + 1) * tok_rows]
-
-    summed_kv = segment(grad_kv_ext, reach)
+    summed_kv = grad_kv_ext[reach]
     for distance in range(1, reach + 1):
-        summed_kv = summed_kv + from_behind(segment(grad_kv_ext, reach - distance), SEQ, -distance)
+        summed_kv = summed_kv + from_behind(grad_kv_ext[reach - distance], SEQ, -distance)
     grad_kv = summed_kv.astype(jnp.bfloat16)
     grad_act = jnp.concatenate([grad_q, grad_kv], axis=1)
     token_term = contract_cols(grad_act, proj_full).astype(jnp.bfloat16)

time: 257 us -> 255 us (level)
  waiting for transfers between devices: 70.6 us -> 66.1 us
  Pallas kernels: 22 us -> 25.6 us
    reduce_scatter x1, waiting for transfers between devices: 18.3 us -> 13.7 us  [shards(): lax.psum_scatter(weight_parts, SEQ, scatter_dimension=0, tiled=True)]
    pallas_call x1, Pallas kernels: 8.91 us -> 12.7 us  [weight_terms(): pl.pallas_call(weight_terms_kernel, grid=(feats // block, 2), in_specs=[p...]
  transfers between devices with their start and end apart: 18 -> 18, of which waited for: 7 -> 7; matrix products, arithmetic and copies ran while one was open for 9% -> 9% of each run, Pallas kernels for 3% -> 5%
where the time goes in v9:
time: 255 us; the launch traced here: 254 us
  blocking collectives  87.8 us (34%)
  waiting for transfers between devices  66.1 us (26%)
  starting transfers between devices  28.7 us (11%)
  Pallas kernels  25.6 us (10%)
  local copies, waits for them, and re-layouts  14.6 us (6%)
  between operations  14 us (5%)
  matrix products  12.5 us (5%)
  other arithmetic  4.85 us (2%)
    all_to_all x1, blocking collectives, shards(): lax.all_to_all(token_term.reshape(tok_rows, n_tp, cols), TP, 1, 1, tiled=...  75.8 us
    all_gather x1, waiting for transfers between devices, shards(): full_cot = lax.all_gather(pair[1], 'z', axis=1, tiled=True)  25 us
    ppermute x4, waiting for transfers between devices, ring_gather(): lax.ppermute(right[-1], axis, [(i, (i + 1) % size) for i in range(size)])  24.3 us
    ppermute x8, starting transfers between devices, from_behind(): return lax.ppermute(block, axis, route)  18.7 us
    reduce_scatter x1, waiting for transfers between devices, shards(): lax.psum_scatter(weight_parts, SEQ, scatter_dimension=0, tiled=True)  13.7 us
    pallas_call x1, Pallas kernels, weight_terms(): pl.pallas_call(weight_terms_kernel, grid=(feats // block, 2), in_specs=[p...  12.7 us
    all_gather x1, blocking collectives, shards(): pair = lax.all_gather(pair, 'yhi', axis=2, tiled=True)  12 us
    ppermute x3, starting transfers between devices, ring_gather(): lax.ppermute(left[-1], axis, [(i, (i - 1) % size) for i in range(size)])  8.75 us
  transfers between devices with their start and end apart: 18, of which 7 were waited for; matrix products, arithmetic and copies ran while one was open for 9% of the time, Pallas kernels for 5%

profile of v9, /device:TPU:128, one launch (start us, length us, event | category | flops | bytes accessed | tf_op | source)
XLA Modules:
  0.0 254.1 jit_solution(7594686498171740851)
XLA Ops:
  7.2 0.0 all-gather.4.cloned.1.call-start
  7.2 2.0 pad_maximum_fusion
  9.2 0.0 all-gather.4.cloned.1.call-update
  9.2 0.0 all-gather.6.cloned.1.call-start
  9.3 1.0 pad_maximum_fusion.1
  10.3 12.0 %all_gather.9 = bf16[2,256,672]{1,2,0:T(8,128)(2,1)S(1)} all-gather(bf16[2,256,336]{1,2,0:T(8,128)(2,1)S(1)} %pad_maximum_fusion.1), channel_id=1, replica_groups=mesh['ylo'=2,'x'=4,'core'=2,'z'=8,'yhi'=2] {'yhi'}, dimensions={2}, use_global_device_ids=true | all-gather | bytes 1032192 | tf_op jit(solution)/shard_map/all_gather | solution.py:186
  22.3 0.8 fusion.18
  23.1 0.0 all-gather.6.cloned.1.call-update
  23.1 0.0 reduce-scatter.2.cloned.1.call-start
  23.1 1.1 collective-permute-start.3
  24.2 2.2 collective-permute-start
  26.5 7.0 %collective-permute-done.3 = bf16[256,672]{0,1:T(8,128)(2,1)} collective-permute-done((bf16[256,672]{0,1:T(8,128)(2,1)S(1)}, bf16[256,672]{0,1:T(8,128)(2,1)}, u32[]{:S(2)}, u32[]{:S(2)}) %collective-permute-start.3) | collective-permute-done | bytes 344096 | tf_op jit(solution)/shard_map/ppermute | solution.py:28
  33.5 0.0 collective-permute-start.4
  33.5 0.0 collective-permute-done
  33.5 3.2 %collective-permute-start.1 = (bf16[256,672]{0,1:T(8,128)(2,1)}, bf16[256,672]{0,1:T(8,128)(2,1)}, u32[]{:S(2)}, u32[]{:S(2)}) collective-permute-start(bf16[256,672]{0,1:T(8,128)(2,1)} %collective-permute-done), channel_id=1, source_target_pairs={{0,14},{2,0},{4,2},{6,4},{8,6},{10,8},{12,10},{14,12},{1,15},{3,1}... | collective-permute-start | bytes 1032200 | tf_op jit(solution)/shard_map/ppermute | solution.py:30
  36.7 0.2 broadcast_in_dim.6
  36.9 6.1 %collective-permute-done.4 = bf16[256,672]{0,1:T(8,128)(2,1)} collective-permute-done((bf16[256,672]{0,1:T(8,128)(2,1)}, bf16[256,672]{0,1:T(8,128)(2,1)}, u32[]{:S(2)}, u32[]{:S(2)}) %collective-permute-start.4) | collective-permute-done | bytes 344096 | tf_op jit(solution)/shard_map/ppermute | solution.py:28
  43.1 0.0 collective-permute-start.5
  43.1 0.0 collective-permute-done.1
  43.1 3.3 %collective-permute-start.2 = (bf16[256,672]{0,1:T(8,128)(2,1)}, bf16[256,672]{0,1:T(8,128)(2,1)S(1)}, u32[]{:S(2)}, u32[]{:S(2)}) collective-permute-start(bf16[256,672]{0,1:T(8,128)(2,1)} %collective-permute-done.1), channel_id=1, source_target_pairs={{0,14},{2,0},{4,2},{6,4},{8,6},{10,8},{12,10},{14,12},{1,15},{3,1}... | collective-permute-start | bytes 1032200 | tf_op jit(solution)/shard_map/ppermute | solution.py:30
  46.4 0.1 broadcast_bitcast_fusion
  46.5 0.6 copy.16
  47.1 4.7 %collective-permute-done.5 = bf16[256,672]{0,1:T(8,128)(2,1)S(1)} collective-permute-done((bf16[256,672]{0,1:T(8,128)(2,1)}, bf16[256,672]{0,1:T(8,128)(2,1)S(1)}, u32[]{:S(2)}, u32[]{:S(2)}) %collective-permute-start.5) | collective-permute-done | bytes 344096 | tf_op jit(solution)/shard_map/ppermute | solution.py:28
  51.8 0.0 collective-permute-start.6
  51.8 1.0 constant_dynamic-update-slice_fusion.11
  52.9 1.0 constant_dynamic-update-slice_fusion.10
  53.9 0.0 collective-permute-done.2
  53.9 6.4 %collective-permute-done.6 = bf16[256,672]{0,1:T(8,128)(2,1)S(1)} collective-permute-done((bf16[256,672]{0,1:T(8,128)(2,1)S(1)}, bf16[256,672]{0,1:T(8,128)(2,1)S(1)}, u32[]{:S(2)}, u32[]{:S(2)}) %collective-permute-start.6) | collective-permute-done | bytes 344096 | tf_op jit(solution)/shard_map/ppermute | solution.py:28
  60.4 1.0 constant_dynamic-update-slice_fusion.6
  61.4 1.0 constant_dynamic-update-slice_fusion.5
  62.4 2.9 %all-gather.4.cloned.1.call-done = bf16[5376,768]{1,0:T(8,128)(2,1)} async-done(((bf16[336,768]{1,0:T(8,128)(2,1)}), bf16[5376,768]{1,0:T(8,128)(2,1)}) %all-gather.4.cloned.1.call-update) | async-done | bytes 8257552 | tf_op jit(solution)/shard_map/all_gather | solution.py:190
  65.3 4.2 %fusion.6 = bf16[256,512]{1,0:T(8,128)(2,1)S(1)} fusion(bf16[256,5376]{0,1:T(8,128)(2,1)S(1)} %constant_dynamic-update-slice_fusion.5, bf16[5376,768]{1,0:T(8,128)(2,1)} %all-gather.4.cloned.1.call-done), kind=kOutput, calls=%fused_computation.7 | convolution fusion | flops 1409417216 | bytes 8519680 | tf_op jit(solution)/shard_map/dot_general | solution.py:195
  69.5 4.5 %collective-permute-start.7 = (bf16[256,256]{1,0:T(8,128)(2,1)S(1)}, bf16[256,256]{1,0:T(8,128)(2,1)S(1)}, u32[]{:S(2)}, u32[]{:S(2)}) collective-permute-start(bf16[256,256]{1,0:T(8,128)(2,1)S(1)} %slice.45), channel_id=1, source_target_pairs={{0,64},{16,80},{32,96},{48,112},{64,128},{80,144},{96,160},{112,17... | collective-permute-start | bytes 393224 | tf_op jit(solution)/shard_map/ppermute | solution.py:45
  74.1 2.3 collective-permute-start.8
  76.4 2.8 %collective-permute-start.9 = (bf16[256,256]{1,0:T(8,128)(2,1)S(1)}, bf16[256,256]{1,0:T(8,128)(2,1)S(1)}, u32[]{:S(2)}, u32[]{:S(2)}) collective-permute-start(bf16[256,256]{1,0:T(8,128)(2,1)S(1)} %slice.45), channel_id=1, source_target_pairs={{0,32},{16,48},{32,64},{48,80},{64,96},{80,112},{96,128},{112,144}... | collective-permute-start | bytes 393224 | tf_op jit(solution)/shard_map/ppermute | solution.py:45
  79.3 3.9 %collective-permute-start.10 = (bf16[256,256]{1,0:T(8,128)(2,1)S(1)}, bf16[256,256]{1,0:T(8,128)(2,1)S(1)}, u32[]{:S(2)}, u32[]{:S(2)}) collective-permute-start(bf16[256,256]{1,0:T(8,128)(2,1)S(1)} %slice.45), channel_id=1, source_target_pairs={{0,16},{16,32},{32,48},{48,64},{64,80},{80,96},{96,112},{112,128},... | collective-permute-start | bytes 393224 | tf_op jit(solution)/shard_map/ppermute | solution.py:45
  83.1 25.0 %all-gather.6.cloned.1.call-done = bf16[1,256,5376]{1,2,0:T(8,128)(2,1)} async-done(((bf16[1,256,672]{1,2,0:T(8,128)(2,1)}), bf16[1,256,5376]{1,2,0:T(8,128)(2,1)}) %all-gather.6.cloned.1.call-update) | async-done | bytes 2752528 | tf_op jit(solution)/shard_map/all_gather | solution.py:188
  108.2 4.2 %fusion.9.d_ref = bf16[256,256]{1,0:T(8,128)(2,1)} fusion(bf16[5376,768]{1,0:T(8,128)(2,1)} %all-gather.4.cloned.1.call-done, bf16[1,256,5376]{1,2,0:T(8,128)(2,1)} %all-gather.6.cloned.1.call-done), kind=kOutput, calls=%fused_computation.8 | convolution fusion | flops 704708608 | bytes 5636096 | tf_op jit(solution)/shard_map/dot_general | solution.py:192
  112.3 0.0 collective-permute-done.7
  112.4 0.0 collective-permute-done.8
  112.4 0.0 collective-permute-done.9
  112.4 0.0 collective-permute-done.10
  112.4 0.7 constant_dynamic-update-slice_fusion
  113.1 0.9 copy-done.1
  114.0 6.6 %shard_map.110 = (bf16[256,256]{1,0:T(8,128)(2,1)}, bf16[256,256]{1,0:T(8,128)(2,1)}, f32[256,256]{1,0:T(8,128)}, f32[256,256]{1,0:T(8,128)}, f32[256,256]{1,0:T...) custom-call(bf16[256,256]{1,0:T(8,128)(2,1)} %get-tuple-element.26.q_ref, bf16[256,256]{1,0:T(8,128)(2,1)} %fusion.9.d_ref, ...), custom_call_target="tpu_custom_call" | custom-call | tf_op jit(solution)/shard_map/pallas_call | solution.py:107
  120.6 1.3 collective-permute-start.14
  121.9 1.3 collective-permute-start.13
  123.2 1.3 collective-permute-start.12
  124.5 1.3 collective-permute-start.11
  125.8 12.7 %shard_map.111.base_ref = bf16[5376,768]{1,0:T(8,128)(2,1)} custom-call(bf16[5376,256]{1,0:T(8,128)(2,1)} %bitcast.24, bf16[5376,256]{1,0:T(8,128)(2,1)} %bitcast.27, bf16[256,256]{1,0:T(8,128)(2,1)} %get-tuple-element.12.gq_ref, bf16[256,256]{1,0:T(8,128)(2,1)} %get-tuple-element.18.attn_ref), custom_call_target="tpu_custom_call" | custom-call | tf_op jit(solution)/shard_map/pallas_call | solution.py:138
  138.5 0.0 collective-permute-done.12
  138.5 0.0 collective-permute-done.11
  138.5 0.7 add_convert_fusion.gkv_ref
  139.3 6.4 %shard_map.112 = bf16[5376,768]{1,0:T(8,128)(2,1)} custom-call(bf16[5376,256]{1,0:T(8,128)(2,1)} %bitcast.25, bf16[256,256]{1,0:T(8,128)(2,1)} %add_convert_fusion.gkv_ref, bf16[5376,768]{1,0:T(8,128)(2,1)} %shard_map.111.base_ref), custom_call_target="tpu_custom_call", output_to_operand_aliasing={{}: (2, {})} | custom-call | tf_op jit(solution)/shard_map/pallas_call | solution.py:151
  145.6 0.0 reduce-scatter.2.cloned.1.call-update
  145.7 0.9 copy-done.2
  146.5 0.1 copy-done.4
  146.6 4.2 %convolution_convert_fusion = bf16[256,5376]{1,0:T(8,128)(2,1)S(1)} fusion(bf16[5376,768]{1,0:T(8,128)(2,1)} %all-gather.4.cloned.1.call-done, bf16[256,256]{1,0:T(8,128)(2,1)S(1)} %copy-done.2, bf16[256,256]{1,0:T(8,128)(2,1)S(1)} %copy-done.4), kind=kOutput, calls=%fused_computation | convolution fusion | flops 1411186688 | bytes 8519680 | tf_op jit(solution)/shard_map/dot_general | solution.py:166
  150.8 2.8 %copy.13 = bf16[256,5376]{0,1:T(8,128)(2,1)} copy(bf16[256,5376]{1,0:T(8,128)(2,1)S(1)} %convolution_convert_fusion) | data formatting | bytes 5505024 | tf_op jit(solution)/shard_map/convert_element_type | solution.py:209
  153.6 75.8 %all_to_all.5 = bf16[256,16,336]{0,2,1:T(8,128)(2,1)S(1)} all-to-all(bf16[256,16,336]{0,2,1:T(8,128)(2,1)} %bitcast.26), channel_id=1, replica_groups=mesh['ylo'=2,'x'=4,'core'=2,'z'=8,'yhi'=2] {'z','yhi'}, dimensions={1} | all-to-all | bytes 5505024 | tf_op jit(solution)/shard_map/all_to_all | solution.py:212
  229.4 1.1 reduce_sum.12
  230.5 13.7 %reduce-scatter.2.cloned.1.call-done = bf16[336,768]{1,0:T(8,128)(2,1)} async-done(((bf16[5376,768]{1,0:T(8,128)(2,1)}), bf16[336,768]{1,0:T(8,128)(2,1)}) %reduce-scatter.2.cloned.1.call-update) | async-done | bytes 516112 | tf_op jit(solution)/shard_map/reduce_scatter | solution.py:215
  244.2 1.8 slice_bitcast_fusion.1
  245.9 1.6 fusion.19
  (21 shorter events, 0.2 us)
Async XLA Ops:
  7.2 58.2 %all-gather.4.cloned.1.call-start = ((), (), s32[]{:S(2)}) async-start(), calls=%async_computation.2 | async-start | bytes 8773632 | tf_op jit(solution)/shard_map/all_gather | solution.py:190
  9.2 98.9 %all-gather.6.cloned.1.call-start = ((), (), s32[]{:S(2)}) async-start(), calls=%async_computation.4 | async-start | bytes 3096576 | tf_op jit(solution)/shard_map/all_gather | solution.py:188
  22.3 20.8 %copy-start.5 = (s32[2,9]{1,0:T(2,128)S(1)}, s32[2,9]{1,0:T(2,128)}, u32[]{:S(2)}) copy-start(s32[2,9]{1,0:T(2,128)} %param.13) | copy-start | bytes 220
  23.1 221.1 %reduce-scatter.2.cloned.1.call-start = ((), (), s32[]{:S(2)}) async-start(), calls=%async_computation.3 | async-start | bytes 8773632 | tf_op jit(solution)/shard_map/reduce_scatter | solution.py:215
  23.1 10.3 %collective-permute-start.3 = (bf16[256,672]{0,1:T(8,128)(2,1)S(1)}, bf16[256,672]{0,1:T(8,128)(2,1)}, u32[]{:S(2)}, u32[]{:S(2)}) collective-permute-start(bf16[256,672]{0,1:T(8,128)(2,1)S(1)} %get-tuple-element.20), channel_id=1, source_target_pairs={{0,2},{2,4},{4,6},{6,8},{8,10},{10,12},{12,14},{14,0},{1,3},{3,5},... | collective-permute-start | bytes 1032200 | tf_op jit(solution)/shard_map/ppermute | solution.py:28
  24.2 9.2 %collective-permute-start = (bf16[256,672]{0,1:T(8,128)(2,1)S(1)}, bf16[256,672]{0,1:T(8,128)(2,1)}, u32[]{:S(2)}, u32[]{:S(2)}) collective-permute-start(bf16[256,672]{0,1:T(8,128)(2,1)S(1)} %get-tuple-element.20), channel_id=1, source_target_pairs={{0,14},{2,0},{4,2},{6,4},{8,6},{10,8},{12,10},{14,12},{1,15},{3,1}... | collective-permute-start | bytes 1032200 | tf_op jit(solution)/shard_map/ppermute | solution.py:30
  33.5 9.6 %collective-permute-start.4 = (bf16[256,672]{0,1:T(8,128)(2,1)}, bf16[256,672]{0,1:T(8,128)(2,1)}, u32[]{:S(2)}, u32[]{:S(2)}) collective-permute-start(bf16[256,672]{0,1:T(8,128)(2,1)} %collective-permute-done.3), channel_id=1, source_target_pairs={{0,2},{2,4},{4,6},{6,8},{8,10},{10,12},{12,14},{14,0},{1,3},{3,5},... | collective-permute-start | bytes 1032200 | tf_op jit(solution)/shard_map/ppermute | solution.py:28
  33.5 9.6 %collective-permute-start.1 = (bf16[256,672]{0,1:T(8,128)(2,1)}, bf16[256,672]{0,1:T(8,128)(2,1)}, u32[]{:S(2)}, u32[]{:S(2)}) collective-permute-start(bf16[256,672]{0,1:T(8,128)(2,1)} %collective-permute-done), channel_id=1, source_target_pairs={{0,14},{2,0},{4,2},{6,4},{8,6},{10,8},{12,10},{14,12},{1,15},{3,1}... | collective-permute-start | bytes 1032200 | tf_op jit(solution)/shard_map/ppermute | solution.py:30
  43.1 8.8 %collective-permute-start.5 = (bf16[256,672]{0,1:T(8,128)(2,1)}, bf16[256,672]{0,1:T(8,128)(2,1)S(1)}, u32[]{:S(2)}, u32[]{:S(2)}) collective-permute-start(bf16[256,672]{0,1:T(8,128)(2,1)} %collective-permute-done.4), channel_id=1, source_target_pairs={{0,2},{2,4},{4,6},{6,8},{8,10},{10,12},{12,14},{14,0},{1,3},{3,5},... | collective-permute-start | bytes 1032200 | tf_op jit(solution)/shard_map/ppermute | solution.py:28
  43.1 10.8 %collective-permute-start.2 = (bf16[256,672]{0,1:T(8,128)(2,1)}, bf16[256,672]{0,1:T(8,128)(2,1)S(1)}, u32[]{:S(2)}, u32[]{:S(2)}) collective-permute-start(bf16[256,672]{0,1:T(8,128)(2,1)} %collective-permute-done.1), channel_id=1, source_target_pairs={{0,14},{2,0},{4,2},{6,4},{8,6},{10,8},{12,10},{14,12},{1,15},{3,1}... | collective-permute-start | bytes 1032200 | tf_op jit(solution)/shard_map/ppermute | solution.py:30
  51.8 8.5 %collective-permute-start.6 = (bf16[256,672]{0,1:T(8,128)(2,1)S(1)}, bf16[256,672]{0,1:T(8,128)(2,1)S(1)}, u32[]{:S(2)}, u32[]{:S(2)}) collective-permute-start(bf16[256,672]{0,1:T(8,128)(2,1)S(1)} %collective-permute-done.5), channel_id=1, source_target_pairs={{0,2},{2,4},{4,6},{6,8},{8,10},{10,12},{12,14},{14,0},{1,3},{3,5},... | collective-permute-start | bytes 1032200 | tf_op jit(solution)/shard_map/ppermute | solution.py:28
  62.4 7.1 %copy-start = (bf16[256,5376]{0,1:T(8,128)(2,1)}, bf16[256,5376]{0,1:T(8,128)(2,1)S(1)}, u32[]{:S(2)}) copy-start(bf16[256,5376]{0,1:T(8,128)(2,1)S(1)} %constant_dynamic-update-slice_fusion.5) | copy-start | bytes 8257540
  69.5 42.8 %collective-permute-start.7 = (bf16[256,256]{1,0:T(8,128)(2,1)S(1)}, bf16[256,256]{1,0:T(8,128)(2,1)S(1)}, u32[]{:S(2)}, u32[]{:S(2)}) collective-permute-start(bf16[256,256]{1,0:T(8,128)(2,1)S(1)} %slice.45), channel_id=1, source_target_pairs={{0,64},{16,80},{32,96},{48,112},{64,128},{80,144},{96,160},{112,17... | collective-permute-start | bytes 393224 | tf_op jit(solution)/shard_map/ppermute | solution.py:45
  74.1 38.3 %collective-permute-start.8 = (bf16[256,256]{1,0:T(8,128)(2,1)S(1)}, bf16[256,256]{1,0:T(8,128)(2,1)S(1)}, u32[]{:S(2)}, u32[]{:S(2)}) collective-permute-start(bf16[256,256]{1,0:T(8,128)(2,1)S(1)} %slice.45), channel_id=1, source_target_pairs={{0,48},{16,64},{32,80},{48,96},{64,112},{80,128},{96,144},{112,160... | collective-permute-start | bytes 393224 | tf_op jit(solution)/shard_map/ppermute | solution.py:45
  76.4 36.0 %collective-permute-start.9 = (bf16[256,256]{1,0:T(8,128)(2,1)S(1)}, bf16[256,256]{1,0:T(8,128)(2,1)S(1)}, u32[]{:S(2)}, u32[]{:S(2)}) collective-permute-start(bf16[256,256]{1,0:T(8,128)(2,1)S(1)} %slice.45), channel_id=1, source_target_pairs={{0,32},{16,48},{32,64},{48,80},{64,96},{80,112},{96,128},{112,144}... | collective-permute-start | bytes 393224 | tf_op jit(solution)/shard_map/ppermute | solution.py:45
  79.3 33.2 %collective-permute-start.10 = (bf16[256,256]{1,0:T(8,128)(2,1)S(1)}, bf16[256,256]{1,0:T(8,128)(2,1)S(1)}, u32[]{:S(2)}, u32[]{:S(2)}) collective-permute-start(bf16[256,256]{1,0:T(8,128)(2,1)S(1)} %slice.45), channel_id=1, source_target_pairs={{0,16},{16,32},{32,48},{48,64},{64,80},{80,96},{96,112},{112,128},... | collective-permute-start | bytes 393224 | tf_op jit(solution)/shard_map/ppermute | solution.py:45
  113.1 0.9 copy-start.1
  120.6 17.9 %collective-permute-start.14 = (f32[256,256]{1,0:T(8,128)}, f32[256,256]{1,0:T(8,128)S(1)}, u32[]{:S(2)}, u32[]{:S(2)}) collective-permute-start(f32[256,256]{1,0:T(8,128)} %get-tuple-element.17), channel_id=1, source_target_pairs={{64,0},{80,16},{96,32},{112,48},{128,64},{144,80},{160,96},{176,11... | collective-permute-start | bytes 786440 | tf_op jit(solution)/shard_map/ppermute | solution.py:45
  121.9 16.6 %collective-permute-start.13 = (f32[256,256]{1,0:T(8,128)}, f32[256,256]{1,0:T(8,128)S(1)}, u32[]{:S(2)}, u32[]{:S(2)}) collective-permute-start(f32[256,256]{1,0:T(8,128)} %get-tuple-element.16), channel_id=1, source_target_pairs={{48,0},{64,16},{80,32},{96,48},{112,64},{128,80},{144,96},{160,112... | collective-permute-start | bytes 786440 | tf_op jit(solution)/shard_map/ppermute | solution.py:45
  123.2 15.3 %collective-permute-start.12 = (f32[256,256]{1,0:T(8,128)}, f32[256,256]{1,0:T(8,128)S(1)}, u32[]{:S(2)}, u32[]{:S(2)}) collective-permute-start(f32[256,256]{1,0:T(8,128)} %get-tuple-element.15), channel_id=1, source_target_pairs={{32,0},{48,16},{64,32},{80,48},{96,64},{112,80},{128,96},{144,112}... | collective-permute-start | bytes 786440 | tf_op jit(solution)/shard_map/ppermute | solution.py:45
  124.5 14.0 %collective-permute-start.11 = (f32[256,256]{1,0:T(8,128)}, f32[256,256]{1,0:T(8,128)S(1)}, u32[]{:S(2)}, u32[]{:S(2)}) collective-permute-start(f32[256,256]{1,0:T(8,128)} %get-tuple-element.14), channel_id=1, source_target_pairs={{16,0},{32,16},{48,32},{64,48},{80,64},{96,80},{112,96},{128,112},... | collective-permute-start | bytes 786440 | tf_op jit(solution)/shard_map/ppermute | solution.py:45
  125.8 12.7 %copy-start.3 = (f32[256,256]{1,0:T(8,128)S(1)}, f32[256,256]{1,0:T(8,128)}, u32[]{:S(2)}) copy-start(f32[256,256]{1,0:T(8,128)} %get-tuple-element.13) | copy-start | bytes 786436
  145.6 0.9 copy-start.2
  145.6 1.0 copy-start.4
Sparse Core Ops, SparseCore 0:
  9.8 55.4 all-gather.3
  67.1 40.9 all-gather.5
  145.8 98.3 reduce-scatter.1

commit v10 on v9

--- a/solution.py
+++ b/solution.py
@@ -117,13 +117,11 @@
 
 
 def weight_terms_kernel(tok_ref, cot_ref, gq_ref, attn_ref, out_ref):
-    @pl.when(pl.program_id(1) == 0)
-    def _():
-        out_ref[...] = _nn(tok_ref[...], gq_ref[...]).astype(out_ref.dtype)
-
-    @pl.when(pl.program_id(1) == 1)
-    def _():
-        out_ref[...] = _nn(cot_ref[...], attn_ref[...]).astype(out_ref.dtype)
+    n_q = gq_ref.shape[1]
+    n_attn = attn_ref.shape[1]
+    width = out_ref.shape[1]
+    out_ref[:, :n_q] = _nn(tok_ref[...], gq_ref[...]).astype(out_ref.dtype)
+    out_ref[:, width - n_attn :] = _nn(cot_ref[...], attn_ref[...]).astype(out_ref.dtype)
 
 
 def kv_terms_kernel(tok_ref, gkv_ref, base_ref, out_ref):
@@ -137,14 +135,14 @@
     width = n_q + n_kv + n_attn
     first = pl.pallas_call(
         weight_terms_kernel,
-        grid=(feats // block, 2),
+        grid=(feats // block,),
         in_specs=[
-            pl.BlockSpec((block, rows), lambda i, j: (i, 0)),
-            pl.BlockSpec((block, rows), lambda i, j: (i, 0)),
-            pl.BlockSpec((rows, n_q), lambda i, j: (0, 0)),
-            pl.BlockSpec((rows, n_attn), lambda i, j: (0, 0)),
+            pl.BlockSpec((block, rows), lambda i: (i, 0)),
+            pl.BlockSpec((block, rows), lambda i: (i, 0)),
+            pl.BlockSpec((rows, n_q), lambda i: (0, 0)),
+            pl.BlockSpec((rows, n_attn), lambda i: (0, 0)),
         ],
-        out_specs=pl.BlockSpec((block, n_q), lambda i, j: (i, 2 * j)),
+        out_specs=pl.BlockSpec((block, width), lambda i: (i, 0)),
         out_shape=jax.ShapeDtypeStruct((feats, width), jnp.bfloat16),
     )(tokens_t, cot_t, grad_q, attn)
     column = n_q // n_kv

time: 255 us -> 254 us (level)
  waiting for transfers between devices: 66.1 us -> 71.2 us
  Pallas kernels: 25.6 us -> 21.9 us
    reduce_scatter x1, waiting for transfers between devices: 13.7 us -> 18.8 us  [shards(): lax.psum_scatter(weight_parts, SEQ, scatter_dimension=0, tiled=True)]
    pallas_call x1, Pallas kernels: 12.7 us -> 8.95 us  [weight_terms(): pl.pallas_call(weight_terms_kernel, grid=(feats // block,), in_specs=[pl....]
  transfers between devices with their start and end apart: 18 -> 18, of which waited for: 7 -> 7; matrix products, arithmetic and copies ran while one was open for 9% -> 9% of each run, Pallas kernels for 5% -> 4%
where the time goes in v10:
time: 254 us; the launch traced here: 253 us
  blocking collectives  85.7 us (34%)
  waiting for transfers between devices  71.2 us (28%)
  starting transfers between devices  28.7 us (11%)
  Pallas kernels  21.9 us (9%)
  local copies, waits for them, and re-layouts  14.6 us (6%)
  between operations  14 us (6%)
  matrix products  12.5 us (5%)
  other arithmetic  4.85 us (2%)
    all_to_all x1, blocking collectives, shards(): lax.all_to_all(token_term.reshape(tok_rows, n_tp, cols), TP, 1, 1, tiled=...  73.7 us
    all_gather x1, waiting for transfers between devices, shards(): full_cot = lax.all_gather(pair[1], 'z', axis=1, tiled=True)  25 us
    ppermute x4, waiting for transfers between devices, ring_gather(): lax.ppermute(right[-1], axis, [(i, (i + 1) % size) for i in range(size)])  24.3 us
    reduce_scatter x1, waiting for transfers between devices, shards(): lax.psum_scatter(weight_parts, SEQ, scatter_dimension=0, tiled=True)  18.8 us
    ppermute x8, starting transfers between devices, from_behind(): return lax.ppermute(block, axis, route)  18.7 us
    all_gather x1, blocking collectives, shards(): pair = lax.all_gather(pair, 'yhi', axis=2, tiled=True)  12 us
    pallas_call x1, Pallas kernels, weight_terms(): pl.pallas_call(weight_terms_kernel, grid=(feats // block,), in_specs=[pl....  8.95 us
    ppermute x3, starting transfers between devices, ring_gather(): lax.ppermute(left[-1], axis, [(i, (i - 1) % size) for i in range(size)])  8.75 us
  transfers between devices with their start and end apart: 18, of which 7 were waited for; matrix products, arithmetic and copies ran while one was open for 9% of the time, Pallas kernels for 4%

profile of v10, /device:TPU:128, one launch (start us, length us, event | category | flops | bytes accessed | tf_op | source)
XLA Modules:
  0.0 253.4 jit_solution(14484027038253349243)
XLA Ops:
  7.2 0.0 all-gather.4.cloned.1.call-start
  7.2 2.0 pad_maximum_fusion
  9.2 0.0 all-gather.4.cloned.1.call-update
  9.2 0.0 all-gather.6.cloned.1.call-start
  9.3 1.0 pad_maximum_fusion.1
  10.3 12.0 %all_gather.9 = bf16[2,256,672]{1,2,0:T(8,128)(2,1)S(1)} all-gather(bf16[2,256,336]{1,2,0:T(8,128)(2,1)S(1)} %pad_maximum_fusion.1), channel_id=1, replica_groups=mesh['ylo'=2,'x'=4,'core'=2,'z'=8,'yhi'=2] {'yhi'}, dimensions={2}, use_global_device_ids=true | all-gather | bytes 1032192 | tf_op jit(solution)/shard_map/all_gather | solution.py:184
  22.3 0.8 fusion.18
  23.1 0.0 all-gather.6.cloned.1.call-update
  23.1 0.0 reduce-scatter.2.cloned.1.call-start
  23.1 1.1 collective-permute-start.3
  24.2 2.2 collective-permute-start
  26.5 7.0 %collective-permute-done.3 = bf16[256,672]{0,1:T(8,128)(2,1)} collective-permute-done((bf16[256,672]{0,1:T(8,128)(2,1)S(1)}, bf16[256,672]{0,1:T(8,128)(2,1)}, u32[]{:S(2)}, u32[]{:S(2)}) %collective-permute-start.3) | collective-permute-done | bytes 344096 | tf_op jit(solution)/shard_map/ppermute | solution.py:28
  33.5 0.0 collective-permute-start.4
  33.5 0.0 collective-permute-done
  33.5 3.2 %collective-permute-start.1 = (bf16[256,672]{0,1:T(8,128)(2,1)}, bf16[256,672]{0,1:T(8,128)(2,1)}, u32[]{:S(2)}, u32[]{:S(2)}) collective-permute-start(bf16[256,672]{0,1:T(8,128)(2,1)} %collective-permute-done), channel_id=1, source_target_pairs={{0,14},{2,0},{4,2},{6,4},{8,6},{10,8},{12,10},{14,12},{1,15},{3,1}... | collective-permute-start | bytes 1032200 | tf_op jit(solution)/shard_map/ppermute | solution.py:30
  36.7 0.2 broadcast_in_dim.6
  36.9 6.1 %collective-permute-done.4 = bf16[256,672]{0,1:T(8,128)(2,1)} collective-permute-done((bf16[256,672]{0,1:T(8,128)(2,1)}, bf16[256,672]{0,1:T(8,128)(2,1)}, u32[]{:S(2)}, u32[]{:S(2)}) %collective-permute-start.4) | collective-permute-done | bytes 344096 | tf_op jit(solution)/shard_map/ppermute | solution.py:28
  43.1 0.0 collective-permute-start.5
  43.1 0.0 collective-permute-done.1
  43.1 3.3 %collective-permute-start.2 = (bf16[256,672]{0,1:T(8,128)(2,1)}, bf16[256,672]{0,1:T(8,128)(2,1)S(1)}, u32[]{:S(2)}, u32[]{:S(2)}) collective-permute-start(bf16[256,672]{0,1:T(8,128)(2,1)} %collective-permute-done.1), channel_id=1, source_target_pairs={{0,14},{2,0},{4,2},{6,4},{8,6},{10,8},{12,10},{14,12},{1,15},{3,1}... | collective-permute-start | bytes 1032200 | tf_op jit(solution)/shard_map/ppermute | solution.py:30
  46.4 0.1 broadcast_bitcast_fusion
  46.5 0.6 copy.16
  47.1 4.7 %collective-permute-done.5 = bf16[256,672]{0,1:T(8,128)(2,1)S(1)} collective-permute-done((bf16[256,672]{0,1:T(8,128)(2,1)}, bf16[256,672]{0,1:T(8,128)(2,1)S(1)}, u32[]{:S(2)}, u32[]{:S(2)}) %collective-permute-start.5) | collective-permute-done | bytes 344096 | tf_op jit(solution)/shard_map/ppermute | solution.py:28
  51.8 0.0 collective-permute-start.6
  51.8 1.0 constant_dynamic-update-slice_fusion.11
  52.9 1.0 constant_dynamic-update-slice_fusion.10
  53.9 0.0 collective-permute-done.2
  53.9 6.4 %collective-permute-done.6 = bf16[256,672]{0,1:T(8,128)(2,1)S(1)} collective-permute-done((bf16[256,672]{0,1:T(8,128)(2,1)S(1)}, bf16[256,672]{0,1:T(8,128)(2,1)S(1)}, u32[]{:S(2)}, u32[]{:S(2)}) %collective-permute-start.6) | collective-permute-done | bytes 344096 | tf_op jit(solution)/shard_map/ppermute | solution.py:28
  60.4 1.0 constant_dynamic-update-slice_fusion.6
  61.4 1.0 constant_dynamic-update-slice_fusion.5
  62.4 2.9 %all-gather.4.cloned.1.call-done = bf16[5376,768]{1,0:T(8,128)(2,1)} async-done(((bf16[336,768]{1,0:T(8,128)(2,1)}), bf16[5376,768]{1,0:T(8,128)(2,1)}) %all-gather.4.cloned.1.call-update) | async-done | bytes 8257552 | tf_op jit(solution)/shard_map/all_gather | solution.py:188
  65.3 4.2 %fusion.6 = bf16[256,512]{1,0:T(8,128)(2,1)S(1)} fusion(bf16[256,5376]{0,1:T(8,128)(2,1)S(1)} %constant_dynamic-update-slice_fusion.5, bf16[5376,768]{1,0:T(8,128)(2,1)} %all-gather.4.cloned.1.call-done), kind=kOutput, calls=%fused_computation.7 | convolution fusion | flops 1409417216 | bytes 8519680 | tf_op jit(solution)/shard_map/dot_general | solution.py:193
  69.5 4.5 %collective-permute-start.7 = (bf16[256,256]{1,0:T(8,128)(2,1)S(1)}, bf16[256,256]{1,0:T(8,128)(2,1)S(1)}, u32[]{:S(2)}, u32[]{:S(2)}) collective-permute-start(bf16[256,256]{1,0:T(8,128)(2,1)S(1)} %slice.45), channel_id=1, source_target_pairs={{0,64},{16,80},{32,96},{48,112},{64,128},{80,144},{96,160},{112,17... | collective-permute-start | bytes 393224 | tf_op jit(solution)/shard_map/ppermute | solution.py:45
  74.1 2.3 collective-permute-start.8
  76.4 2.8 %collective-permute-start.9 = (bf16[256,256]{1,0:T(8,128)(2,1)S(1)}, bf16[256,256]{1,0:T(8,128)(2,1)S(1)}, u32[]{:S(2)}, u32[]{:S(2)}) collective-permute-start(bf16[256,256]{1,0:T(8,128)(2,1)S(1)} %slice.45), channel_id=1, source_target_pairs={{0,32},{16,48},{32,64},{48,80},{64,96},{80,112},{96,128},{112,144}... | collective-permute-start | bytes 393224 | tf_op jit(solution)/shard_map/ppermute | solution.py:45
  79.3 3.9 %collective-permute-start.10 = (bf16[256,256]{1,0:T(8,128)(2,1)S(1)}, bf16[256,256]{1,0:T(8,128)(2,1)S(1)}, u32[]{:S(2)}, u32[]{:S(2)}) collective-permute-start(bf16[256,256]{1,0:T(8,128)(2,1)S(1)} %slice.45), channel_id=1, source_target_pairs={{0,16},{16,32},{32,48},{48,64},{64,80},{80,96},{96,112},{112,128},... | collective-permute-start | bytes 393224 | tf_op jit(solution)/shard_map/ppermute | solution.py:45
  83.1 25.0 %all-gather.6.cloned.1.call-done = bf16[1,256,5376]{1,2,0:T(8,128)(2,1)} async-done(((bf16[1,256,672]{1,2,0:T(8,128)(2,1)}), bf16[1,256,5376]{1,2,0:T(8,128)(2,1)}) %all-gather.6.cloned.1.call-update) | async-done | bytes 2752528 | tf_op jit(solution)/shard_map/all_gather | solution.py:186
  108.2 4.2 %fusion.9.d_ref = bf16[256,256]{1,0:T(8,128)(2,1)} fusion(bf16[5376,768]{1,0:T(8,128)(2,1)} %all-gather.4.cloned.1.call-done, bf16[1,256,5376]{1,2,0:T(8,128)(2,1)} %all-gather.6.cloned.1.call-done), kind=kOutput, calls=%fused_computation.8 | convolution fusion | flops 704708608 | bytes 5636096 | tf_op jit(solution)/shard_map/dot_general | solution.py:190
  112.3 0.0 collective-permute-done.7
  112.4 0.0 collective-permute-done.8
  112.4 0.0 collective-permute-done.9
  112.4 0.0 collective-permute-done.10
  112.4 0.7 constant_dynamic-update-slice_fusion
  113.1 0.9 copy-done.1
  114.0 6.6 %shard_map.110 = (bf16[256,256]{1,0:T(8,128)(2,1)}, bf16[256,256]{1,0:T(8,128)(2,1)}, f32[256,256]{1,0:T(8,128)}, f32[256,256]{1,0:T(8,128)}, f32[256,256]{1,0:T...) custom-call(bf16[256,256]{1,0:T(8,128)(2,1)} %get-tuple-element.26.q_ref, bf16[256,256]{1,0:T(8,128)(2,1)} %fusion.9.d_ref, ...), custom_call_target="tpu_custom_call" | custom-call | tf_op jit(solution)/shard_map/pallas_call | solution.py:107
  120.6 1.3 collective-permute-start.14
  121.9 1.3 collective-permute-start.13
  123.2 1.3 collective-permute-start.12
  124.5 1.3 collective-permute-start.11
  125.8 8.9 %shard_map.111.base_ref = bf16[5376,768]{1,0:T(8,128)(2,1)} custom-call(bf16[5376,256]{1,0:T(8,128)(2,1)} %bitcast.24, bf16[5376,256]{1,0:T(8,128)(2,1)} %bitcast.27, bf16[256,256]{1,0:T(8,128)(2,1)} %get-tuple-element.12.gq_ref, bf16[256,256]{1,0:T(8,128)(2,1)} %get-tuple-element.18.attn_ref), custom_call_target="tpu_custom_call" | custom-call | tf_op jit(solution)/shard_map/pallas_call | solution.py:136
  134.8 0.0 collective-permute-done.13
  134.8 0.0 collective-permute-done.11
  134.8 0.7 add_convert_fusion.gkv_ref
  135.5 6.4 %shard_map.112 = bf16[5376,768]{1,0:T(8,128)(2,1)} custom-call(bf16[5376,256]{1,0:T(8,128)(2,1)} %bitcast.25, bf16[256,256]{1,0:T(8,128)(2,1)} %add_convert_fusion.gkv_ref, bf16[5376,768]{1,0:T(8,128)(2,1)} %shard_map.111.base_ref), custom_call_target="tpu_custom_call", output_to_operand_aliasing={{}: (2, {})} | custom-call | tf_op jit(solution)/shard_map/pallas_call | solution.py:149
  141.9 0.0 reduce-scatter.2.cloned.1.call-update
  141.9 0.9 copy-done.2
  142.8 0.1 copy-done.4
  142.9 4.2 %convolution_convert_fusion = bf16[256,5376]{1,0:T(8,128)(2,1)S(1)} fusion(bf16[5376,768]{1,0:T(8,128)(2,1)} %all-gather.4.cloned.1.call-done, bf16[256,256]{1,0:T(8,128)(2,1)S(1)} %copy-done.2, bf16[256,256]{1,0:T(8,128)(2,1)S(1)} %copy-done.4), kind=kOutput, calls=%fused_computation | convolution fusion | flops 1411186688 | bytes 8519680 | tf_op jit(solution)/shard_map/dot_general | solution.py:164
  147.1 2.8 %copy.13 = bf16[256,5376]{0,1:T(8,128)(2,1)} copy(bf16[256,5376]{1,0:T(8,128)(2,1)S(1)} %convolution_convert_fusion) | data formatting | bytes 5505024 | tf_op jit(solution)/shard_map/convert_element_type | solution.py:207
  149.9 73.7 %all_to_all.5 = bf16[256,16,336]{0,2,1:T(8,128)(2,1)S(1)} all-to-all(bf16[256,16,336]{0,2,1:T(8,128)(2,1)} %bitcast.26), channel_id=1, replica_groups=mesh['ylo'=2,'x'=4,'core'=2,'z'=8,'yhi'=2] {'z','yhi'}, dimensions={1} | all-to-all | bytes 5505024 | tf_op jit(solution)/shard_map/all_to_all | solution.py:210
  223.6 1.1 reduce_sum.12
  224.7 18.8 %reduce-scatter.2.cloned.1.call-done = bf16[336,768]{1,0:T(8,128)(2,1)} async-done(((bf16[5376,768]{1,0:T(8,128)(2,1)}), bf16[336,768]{1,0:T(8,128)(2,1)}) %reduce-scatter.2.cloned.1.call-update) | async-done | bytes 516112 | tf_op jit(solution)/shard_map/reduce_scatter | solution.py:213
  243.5 1.8 slice_bitcast_fusion.1
  245.3 1.6 fusion.19
  (21 shorter events, 0.2 us)
Async XLA Ops:
  7.2 58.2 %all-gather.4.cloned.1.call-start = ((), (), s32[]{:S(2)}) async-start(), calls=%async_computation.2 | async-start | bytes 8773632 | tf_op jit(solution)/shard_map/all_gather | solution.py:188
  9.2 98.9 %all-gather.6.cloned.1.call-start = ((), (), s32[]{:S(2)}) async-start(), calls=%async_computation.4 | async-start | bytes 3096576 | tf_op jit(solution)/shard_map/all_gather | solution.py:186
  22.3 20.8 %copy-start.5 = (s32[2,9]{1,0:T(2,128)S(1)}, s32[2,9]{1,0:T(2,128)}, u32[]{:S(2)}) copy-start(s32[2,9]{1,0:T(2,128)} %param.13) | copy-start | bytes 220
  23.1 220.4 %reduce-scatter.2.cloned.1.call-start = ((), (), s32[]{:S(2)}) async-start(), calls=%async_computation.3 | async-start | bytes 8773632 | tf_op jit(solution)/shard_map/reduce_scatter | solution.py:213
  23.1 10.3 %collective-permute-start.3 = (bf16[256,672]{0,1:T(8,128)(2,1)S(1)}, bf16[256,672]{0,1:T(8,128)(2,1)}, u32[]{:S(2)}, u32[]{:S(2)}) collective-permute-start(bf16[256,672]{0,1:T(8,128)(2,1)S(1)} %get-tuple-element.20), channel_id=1, source_target_pairs={{0,2},{2,4},{4,6},{6,8},{8,10},{10,12},{12,14},{14,0},{1,3},{3,5},... | collective-permute-start | bytes 1032200 | tf_op jit(solution)/shard_map/ppermute | solution.py:28
  24.2 9.2 %collective-permute-start = (bf16[256,672]{0,1:T(8,128)(2,1)S(1)}, bf16[256,672]{0,1:T(8,128)(2,1)}, u32[]{:S(2)}, u32[]{:S(2)}) collective-permute-start(bf16[256,672]{0,1:T(8,128)(2,1)S(1)} %get-tuple-element.20), channel_id=1, source_target_pairs={{0,14},{2,0},{4,2},{6,4},{8,6},{10,8},{12,10},{14,12},{1,15},{3,1}... | collective-permute-start | bytes 1032200 | tf_op jit(solution)/shard_map/ppermute | solution.py:30
  33.5 9.6 %collective-permute-start.4 = (bf16[256,672]{0,1:T(8,128)(2,1)}, bf16[256,672]{0,1:T(8,128)(2,1)}, u32[]{:S(2)}, u32[]{:S(2)}) collective-permute-start(bf16[256,672]{0,1:T(8,128)(2,1)} %collective-permute-done.3), channel_id=1, source_target_pairs={{0,2},{2,4},{4,6},{6,8},{8,10},{10,12},{12,14},{14,0},{1,3},{3,5},... | collective-permute-start | bytes 1032200 | tf_op jit(solution)/shard_map/ppermute | solution.py:28
  33.5 9.6 %collective-permute-start.1 = (bf16[256,672]{0,1:T(8,128)(2,1)}, bf16[256,672]{0,1:T(8,128)(2,1)}, u32[]{:S(2)}, u32[]{:S(2)}) collective-permute-start(bf16[256,672]{0,1:T(8,128)(2,1)} %collective-permute-done), channel_id=1, source_target_pairs={{0,14},{2,0},{4,2},{6,4},{8,6},{10,8},{12,10},{14,12},{1,15},{3,1}... | collective-permute-start | bytes 1032200 | tf_op jit(solution)/shard_map/ppermute | solution.py:30
  43.1 8.8 %collective-permute-start.5 = (bf16[256,672]{0,1:T(8,128)(2,1)}, bf16[256,672]{0,1:T(8,128)(2,1)S(1)}, u32[]{:S(2)}, u32[]{:S(2)}) collective-permute-start(bf16[256,672]{0,1:T(8,128)(2,1)} %collective-permute-done.4), channel_id=1, source_target_pairs={{0,2},{2,4},{4,6},{6,8},{8,10},{10,12},{12,14},{14,0},{1,3},{3,5},... | collective-permute-start | bytes 1032200 | tf_op jit(solution)/shard_map/ppermute | solution.py:28
  43.1 10.8 %collective-permute-start.2 = (bf16[256,672]{0,1:T(8,128)(2,1)}, bf16[256,672]{0,1:T(8,128)(2,1)S(1)}, u32[]{:S(2)}, u32[]{:S(2)}) collective-permute-start(bf16[256,672]{0,1:T(8,128)(2,1)} %collective-permute-done.1), channel_id=1, source_target_pairs={{0,14},{2,0},{4,2},{6,4},{8,6},{10,8},{12,10},{14,12},{1,15},{3,1}... | collective-permute-start | bytes 1032200 | tf_op jit(solution)/shard_map/ppermute | solution.py:30
  51.8 8.5 %collective-permute-start.6 = (bf16[256,672]{0,1:T(8,128)(2,1)S(1)}, bf16[256,672]{0,1:T(8,128)(2,1)S(1)}, u32[]{:S(2)}, u32[]{:S(2)}) collective-permute-start(bf16[256,672]{0,1:T(8,128)(2,1)S(1)} %collective-permute-done.5), channel_id=1, source_target_pairs={{0,2},{2,4},{4,6},{6,8},{8,10},{10,12},{12,14},{14,0},{1,3},{3,5},... | collective-permute-start | bytes 1032200 | tf_op jit(solution)/shard_map/ppermute | solution.py:28
  62.4 7.1 %copy-start = (bf16[256,5376]{0,1:T(8,128)(2,1)}, bf16[256,5376]{0,1:T(8,128)(2,1)S(1)}, u32[]{:S(2)}) copy-start(bf16[256,5376]{0,1:T(8,128)(2,1)S(1)} %constant_dynamic-update-slice_fusion.5) | copy-start | bytes 8257540
  69.5 42.8 %collective-permute-start.7 = (bf16[256,256]{1,0:T(8,128)(2,1)S(1)}, bf16[256,256]{1,0:T(8,128)(2,1)S(1)}, u32[]{:S(2)}, u32[]{:S(2)}) collective-permute-start(bf16[256,256]{1,0:T(8,128)(2,1)S(1)} %slice.45), channel_id=1, source_target_pairs={{0,64},{16,80},{32,96},{48,112},{64,128},{80,144},{96,160},{112,17... | collective-permute-start | bytes 393224 | tf_op jit(solution)/shard_map/ppermute | solution.py:45
  74.1 38.3 %collective-permute-start.8 = (bf16[256,256]{1,0:T(8,128)(2,1)S(1)}, bf16[256,256]{1,0:T(8,128)(2,1)S(1)}, u32[]{:S(2)}, u32[]{:S(2)}) collective-permute-start(bf16[256,256]{1,0:T(8,128)(2,1)S(1)} %slice.45), channel_id=1, source_target_pairs={{0,48},{16,64},{32,80},{48,96},{64,112},{80,128},{96,144},{112,160... | collective-permute-start | bytes 393224 | tf_op jit(solution)/shard_map/ppermute | solution.py:45
  76.4 36.0 %collective-permute-start.9 = (bf16[256,256]{1,0:T(8,128)(2,1)S(1)}, bf16[256,256]{1,0:T(8,128)(2,1)S(1)}, u32[]{:S(2)}, u32[]{:S(2)}) collective-permute-start(bf16[256,256]{1,0:T(8,128)(2,1)S(1)} %slice.45), channel_id=1, source_target_pairs={{0,32},{16,48},{32,64},{48,80},{64,96},{80,112},{96,128},{112,144}... | collective-permute-start | bytes 393224 | tf_op jit(solution)/shard_map/ppermute | solution.py:45
  79.3 33.2 %collective-permute-start.10 = (bf16[256,256]{1,0:T(8,128)(2,1)S(1)}, bf16[256,256]{1,0:T(8,128)(2,1)S(1)}, u32[]{:S(2)}, u32[]{:S(2)}) collective-permute-start(bf16[256,256]{1,0:T(8,128)(2,1)S(1)} %slice.45), channel_id=1, source_target_pairs={{0,16},{16,32},{32,48},{48,64},{64,80},{80,96},{96,112},{112,128},... | collective-permute-start | bytes 393224 | tf_op jit(solution)/shard_map/ppermute | solution.py:45
  113.1 0.9 copy-start.1
  120.6 14.1 %collective-permute-start.14 = (f32[256,256]{1,0:T(8,128)}, f32[256,256]{1,0:T(8,128)S(1)}, u32[]{:S(2)}, u32[]{:S(2)}) collective-permute-start(f32[256,256]{1,0:T(8,128)} %get-tuple-element.17), channel_id=1, source_target_pairs={{64,0},{80,16},{96,32},{112,48},{128,64},{144,80},{160,96},{176,11... | collective-permute-start | bytes 786440 | tf_op jit(solution)/shard_map/ppermute | solution.py:45
  121.9 12.9 %collective-permute-start.13 = (f32[256,256]{1,0:T(8,128)}, f32[256,256]{1,0:T(8,128)S(1)}, u32[]{:S(2)}, u32[]{:S(2)}) collective-permute-start(f32[256,256]{1,0:T(8,128)} %get-tuple-element.16), channel_id=1, source_target_pairs={{48,0},{64,16},{80,32},{96,48},{112,64},{128,80},{144,96},{160,112... | collective-permute-start | bytes 786440 | tf_op jit(solution)/shard_map/ppermute | solution.py:45
  123.2 11.6 %collective-permute-start.12 = (f32[256,256]{1,0:T(8,128)}, f32[256,256]{1,0:T(8,128)S(1)}, u32[]{:S(2)}, u32[]{:S(2)}) collective-permute-start(f32[256,256]{1,0:T(8,128)} %get-tuple-element.15), channel_id=1, source_target_pairs={{32,0},{48,16},{64,32},{80,48},{96,64},{112,80},{128,96},{144,112}... | collective-permute-start | bytes 786440 | tf_op jit(solution)/shard_map/ppermute | solution.py:45
  124.5 10.3 %collective-permute-start.11 = (f32[256,256]{1,0:T(8,128)}, f32[256,256]{1,0:T(8,128)S(1)}, u32[]{:S(2)}, u32[]{:S(2)}) collective-permute-start(f32[256,256]{1,0:T(8,128)} %get-tuple-element.14), channel_id=1, source_target_pairs={{16,0},{32,16},{48,32},{64,48},{80,64},{96,80},{112,96},{128,112},... | collective-permute-start | bytes 786440 | tf_op jit(solution)/shard_map/ppermute | solution.py:45
  125.8 9.0 %copy-start.3 = (f32[256,256]{1,0:T(8,128)S(1)}, f32[256,256]{1,0:T(8,128)}, u32[]{:S(2)}) copy-start(f32[256,256]{1,0:T(8,128)} %get-tuple-element.13) | copy-start | bytes 786436
  141.9 0.9 copy-start.2
  141.9 1.0 copy-start.4
Sparse Core Ops, SparseCore 0:
  9.8 55.4 all-gather.3
  67.1 40.9 all-gather.5
  142.0 101.4 reduce-scatter.1

commit v11 on v10

--- a/solution.py
+++ b/solution.py
@@ -53,9 +53,10 @@
     return lax.dot_general(left, right, (((1,), (0,)), ((), ())), preferred_element_type=jnp.float32)
 
 
-def attention_kernel(q_ref, d_ref, kv_ref, lst_ref, attn_ref, gq_ref, *rest, scale, block_len, span, head_dim):
+def attention_kernel(q_ref, cot_ref, wo_ref, kv_ref, lst_ref, attn_ref, gq_ref, *rest, scale, block_len, span, head_dim):
     seg_refs, dkv_ref = rest[:-1], rest[-1]
     n_blocks = q_ref.shape[0] // block_len
+    d_all = _nn(cot_ref[...], wo_ref[...]).astype(jnp.bfloat16)
     groups = q_ref.shape[1] // head_dim
     width = span * block_len
     dkv_ref[...] = jnp.zeros(dkv_ref.shape, jnp.float32)
@@ -72,7 +73,7 @@
         for g in range(groups):
             r0, c0 = b * block_len, g * head_dim
             qb = q_ref[r0 : r0 + block_len, c0 : c0 + head_dim]
-            db = d_ref[r0 : r0 + block_len, c0 : c0 + head_dim]
+            db = d_all[r0 : r0 + block_len, c0 : c0 + head_dim]
             scores = _nt(qb, kw) * scale
             masked = jnp.where(allowed, scores, -1e30)
             highest = jnp.max(masked, axis=1, keepdims=True)
@@ -95,7 +96,7 @@
         seg_ref[...] = dkv_ref[index * seg : (index + 1) * seg, :]
 
 
-def fused_attention(query, kv_ext, d_attn, block_lists, scale, head_dim):
+def fused_attention(query, kv_ext, full_cot, wo_t, block_lists, scale, head_dim):
     n_blocks, span = block_lists.shape
     block_len = query.shape[0] // n_blocks
     listed = jnp.repeat((block_lists >= 0).astype(jnp.float32), block_len, axis=1)
@@ -112,7 +113,7 @@
         )
         + (seg_shape,) * n_seg,
         scratch_shapes=[pltpu.VMEM(kv_ext.shape, jnp.float32)],
-    )(query, d_attn, kv_ext, listed)
+    )(query, full_cot, wo_t, kv_ext, listed)
     return outs[0], outs[1], outs[2:]
 
 
@@ -187,16 +188,13 @@
     w_cat = jnp.concatenate([w_query, w_key, w_value, w_out.T], axis=1)
     w_full = lax.all_gather(w_cat, SEQ, axis=0, tiled=True)
     proj_full = w_full[:, :n_proj]
-    d_attn = jnp.dot(full_cot, w_full[:, n_proj:], preferred_element_type=jnp.float32).astype(
-        jnp.bfloat16
-    )
     qkv = jnp.dot(full_tokens, proj_full, preferred_element_type=jnp.float32).astype(jnp.bfloat16)
     query = qkv[:, :n_q]
     kv = qkv[:, n_q:]
     earlier = [from_behind(kv, SEQ, distance) for distance in range(reach, 0, -1)]
     kv_ext = jnp.concatenate(earlier + [kv], axis=0)
     attn, grad_q, grad_kv_ext = fused_attention(
-        query, kv_ext, d_attn, block_lists, softmax_scale, head_dim
+        query, kv_ext, full_cot, w_full[:, n_proj:], block_lists, softmax_scale, head_dim
     )
 
     summed_kv = grad_kv_ext[reach]

time: 254 us -> 270 us (1.063)
  waiting for transfers between devices: 71.2 us -> 81.3 us
  local copies, waits for them, and re-layouts: 14.6 us -> 22.7 us
  matrix products: 12.5 us -> 8.34 us
  Pallas kernels: 21.9 us -> 25 us
    all_gather x1, waiting for transfers between devices: 25 us -> 31.1 us  [shards(): full_cot = lax.all_gather(pair[1], 'z', axis=1, tiled=True)]
    all_gather x0 -> x1, local copies, waits for them, and re-layouts: none -> 4.57 us  [shards(): full_cot = lax.all_gather(pair[1], 'z', axis=1, tiled=True)]
    dot_general x1 -> x0, matrix products: 4.19 us -> none  [shards(): jnp.dot(full_cot, w_full[:, n_proj:], preferred_element_type=jnp.float32)]
    slice x0 -> x1, local copies, waits for them, and re-layouts: none -> 3.58 us  [shards(): w_full[:, n_proj:]]
    reduce_scatter x1, waiting for transfers between devices: 18.8 us -> 22 us  [shards(): lax.psum_scatter(weight_parts, SEQ, scatter_dimension=0, tiled=True)]
    pallas_call x1, Pallas kernels: 6.57 us -> 9.72 us  [fused_attention(): pl.pallas_call(body, out_shape=(jax.ShapeDtypeStruct(query.shape, jnp.bfl...]
  transfers between devices with their start and end apart: 18 -> 18, of which waited for: 7 -> 8; matrix products, arithmetic and copies ran while one was open for 9% -> 10% of each run, Pallas kernels for 4% -> 3%
where the time goes in v11:
time: 270 us; the launch traced here: 268 us
  blocking collectives  85.5 us (32%)
  waiting for transfers between devices  81.3 us (30%)
  starting transfers between devices  26.8 us (10%)
  Pallas kernels  25 us (9%)
  local copies, waits for them, and re-layouts  22.7 us (8%)
  between operations  14 us (5%)
  matrix products  8.34 us (3%)
  other arithmetic  4.85 us (2%)
    all_to_all x1, blocking collectives, shards(): lax.all_to_all(token_term.reshape(tok_rows, n_tp, cols), TP, 1, 1, tiled=...  73.5 us
    all_gather x1, waiting for transfers between devices, shards(): full_cot = lax.all_gather(pair[1], 'z', axis=1, tiled=True)  31.1 us
    ppermute x4, waiting for transfers between devices, ring_gather(): lax.ppermute(right[-1], axis, [(i, (i + 1) % size) for i in range(size)])  24.9 us
    reduce_scatter x1, waiting for transfers between devices, shards(): lax.psum_scatter(weight_parts, SEQ, scatter_dimension=0, tiled=True)  22 us
    ppermute x8, starting transfers between devices, from_behind(): return lax.ppermute(block, axis, route)  16.9 us
    all_gather x1, blocking collectives, shards(): pair = lax.all_gather(pair, 'yhi', axis=2, tiled=True)  12 us
    pallas_call x1, Pallas kernels, fused_attention(): pl.pallas_call(body, out_shape=(jax.ShapeDtypeStruct(query.shape, jnp.bfl...  9.72 us
    pallas_call x1, Pallas kernels, weight_terms(): pl.pallas_call(weight_terms_kernel, grid=(feats // block,), in_specs=[pl....  8.96 us
  transfers between devices with their start and end apart: 18, of which 8 were waited for; matrix products, arithmetic and copies ran while one was open for 10% of the time, Pallas kernels for 3%

profile of v11, /device:TPU:128, one launch (start us, length us, event | category | flops | bytes accessed | tf_op | source)
XLA Modules:
  0.0 268.5 jit_solution(3566855827548341425)
XLA Ops:
  7.2 0.0 all-gather.4.cloned.1.call-start
  7.2 2.0 pad_maximum_fusion
  9.2 0.0 all-gather.4.cloned.1.call-update
  9.2 0.0 all-gather.6.cloned.1.call-start
  9.3 1.0 pad_maximum_fusion.1
  10.3 12.0 %all_gather.9 = bf16[2,256,672]{1,2,0:T(8,128)(2,1)S(1)} all-gather(bf16[2,256,336]{1,2,0:T(8,128)(2,1)S(1)} %pad_maximum_fusion.1), channel_id=1, replica_groups=mesh['ylo'=2,'x'=4,'core'=2,'z'=8,'yhi'=2] {'yhi'}, dimensions={2}, use_global_device_ids=true | all-gather | bytes 1032192 | tf_op jit(solution)/shard_map/all_gather | solution.py:185
  22.3 0.8 fusion.10
  23.1 0.0 all-gather.6.cloned.1.call-update
  23.1 0.0 reduce-scatter.2.cloned.1.call-start
  23.2 1.1 collective-permute-start.3
  24.3 2.2 collective-permute-start
  26.5 6.9 %collective-permute-done.3 = bf16[256,672]{0,1:T(8,128)(2,1)S(1)} collective-permute-done((bf16[256,672]{0,1:T(8,128)(2,1)S(1)}, bf16[256,672]{0,1:T(8,128)(2,1)S(1)}, u32[]{:S(2)}, u32[]{:S(2)}) %collective-permute-start.3) | collective-permute-done | bytes 344096 | tf_op jit(solution)/shard_map/ppermute | solution.py:28
  33.4 0.0 collective-permute-start.4
  33.4 0.0 collective-permute-done
  33.4 3.2 %collective-permute-start.1 = (bf16[256,672]{0,1:T(8,128)(2,1)}, bf16[256,672]{0,1:T(8,128)(2,1)}, u32[]{:S(2)}, u32[]{:S(2)}) collective-permute-start(bf16[256,672]{0,1:T(8,128)(2,1)} %collective-permute-done), channel_id=1, source_target_pairs={{0,14},{2,0},{4,2},{6,4},{8,6},{10,8},{12,10},{14,12},{1,15},{3,1}... | collective-permute-start | bytes 1032200 | tf_op jit(solution)/shard_map/ppermute | solution.py:30
  36.6 6.2 %collective-permute-done.4 = bf16[256,672]{0,1:T(8,128)(2,1)} collective-permute-done((bf16[256,672]{0,1:T(8,128)(2,1)S(1)}, bf16[256,672]{0,1:T(8,128)(2,1)}, u32[]{:S(2)}, u32[]{:S(2)}) %collective-permute-start.4) | collective-permute-done | bytes 344096 | tf_op jit(solution)/shard_map/ppermute | solution.py:28
  42.8 0.0 collective-permute-start.5
  42.8 0.2 broadcast_in_dim.6
  43.0 0.0 collective-permute-done.1
  43.0 3.3 %collective-permute-start.2 = (bf16[256,672]{0,1:T(8,128)(2,1)}, bf16[256,672]{0,1:T(8,128)(2,1)S(1)}, u32[]{:S(2)}, u32[]{:S(2)}) collective-permute-start(bf16[256,672]{0,1:T(8,128)(2,1)} %collective-permute-done.1), channel_id=1, source_target_pairs={{0,14},{2,0},{4,2},{6,4},{8,6},{10,8},{12,10},{14,12},{1,15},{3,1}... | collective-permute-start | bytes 1032200 | tf_op jit(solution)/shard_map/ppermute | solution.py:30
  46.4 5.2 %collective-permute-done.5 = bf16[256,672]{0,1:T(8,128)(2,1)} collective-permute-done((bf16[256,672]{0,1:T(8,128)(2,1)}, bf16[256,672]{0,1:T(8,128)(2,1)}, u32[]{:S(2)}, u32[]{:S(2)}) %collective-permute-start.5) | collective-permute-done | bytes 344096 | tf_op jit(solution)/shard_map/ppermute | solution.py:28
  51.6 1.0 constant_dynamic-update-slice_fusion.11
  52.6 1.0 constant_dynamic-update-slice_fusion.10
  53.6 6.6 %collective-permute-done.6 = bf16[256,672]{0,1:T(8,128)(2,1)S(1)} collective-permute-done((bf16[256,672]{0,1:T(8,128)(2,1)}, bf16[256,672]{0,1:T(8,128)(2,1)S(1)}, u32[]{:S(2)}, u32[]{:S(2)}) %collective-permute-start.6) | collective-permute-done | bytes 344096 | tf_op jit(solution)/shard_map/ppermute | solution.py:28
  60.3 1.0 constant_dynamic-update-slice_fusion.7
  61.3 1.0 constant_dynamic-update-slice_fusion.6
  62.4 3.0 %all-gather.4.cloned.1.call-done = bf16[5376,768]{1,0:T(8,128)(2,1)} async-done(((bf16[336,768]{1,0:T(8,128)(2,1)}), bf16[5376,768]{1,0:T(8,128)(2,1)}) %all-gather.4.cloned.1.call-update) | async-done | bytes 8257552 | tf_op jit(solution)/shard_map/all_gather | solution.py:189
  65.3 4.2 %fusion.3 = bf16[256,512]{1,0:T(8,128)(2,1)S(1)} fusion(bf16[256,5376]{0,1:T(8,128)(2,1)S(1)} %constant_dynamic-update-slice_fusion.5, bf16[5376,768]{1,0:T(8,128)(2,1)} %all-gather.4.cloned.1.call-done), kind=kOutput, calls=%fused_computation.4 | convolution fusion | flops 1409417216 | bytes 8519680 | tf_op jit(solution)/shard_map/dot_general | solution.py:191
  69.5 4.5 %collective-permute-start.7 = (bf16[256,256]{1,0:T(8,128)(2,1)S(1)}, bf16[256,256]{1,0:T(8,128)(2,1)S(1)}, u32[]{:S(2)}, u32[]{:S(2)}) collective-permute-start(bf16[256,256]{1,0:T(8,128)(2,1)S(1)} %slice.45), channel_id=1, source_target_pairs={{0,64},{16,80},{32,96},{48,112},{64,128},{80,144},{96,160},{112,17... | collective-permute-start | bytes 393224 | tf_op jit(solution)/shard_map/ppermute | solution.py:45
  74.1 2.3 collective-permute-start.8
  76.4 0.1 broadcast_bitcast_fusion
  76.5 0.6 copy.18
  77.1 31.1 %all-gather.6.cloned.1.call-done = bf16[1,256,5376]{1,2,0:T(8,128)(2,1)} async-done(((bf16[1,256,672]{1,2,0:T(8,128)(2,1)}), bf16[1,256,5376]{1,2,0:T(8,128)(2,1)}) %all-gather.6.cloned.1.call-update) | async-done | bytes 2752528 | tf_op jit(solution)/shard_map/all_gather | solution.py:187
  108.2 4.6 %copy.14.cot_ref = bf16[256,5376]{1,0:T(8,128)(2,1)} copy(bf16[256,5376]{0,1:T(8,128)(2,1)} %bitcast.22) | data formatting | bytes 5505024 | tf_op jit(solution)/shard_map/all_gather | solution.py:187
  112.7 3.4 %collective-permute-start.9 = (bf16[256,256]{1,0:T(8,128)(2,1)S(1)}, bf16[256,256]{1,0:T(8,128)(2,1)S(1)}, u32[]{:S(2)}, u32[]{:S(2)}) collective-permute-start(bf16[256,256]{1,0:T(8,128)(2,1)S(1)} %slice.45), channel_id=1, source_target_pairs={{0,32},{16,48},{32,64},{48,80},{64,96},{80,112},{96,128},{112,144}... | collective-permute-start | bytes 393224 | tf_op jit(solution)/shard_map/ppermute | solution.py:45
  116.1 1.5 collective-permute-start.10
  117.6 3.6 %slice.44.wo_ref = bf16[5376,256]{1,0:T(8,128)(2,1)} slice(bf16[5376,768]{1,0:T(8,128)(2,1)} %all-gather.4.cloned.1.call-done), slice={[0:5376], [512:768]} | slice | bytes 5505024 | tf_op jit(solution)/shard_map/slice | solution.py:197
  121.2 0.0 collective-permute-done.7
  121.2 0.0 collective-permute-done.8
  121.2 0.0 collective-permute-done.9
  121.3 0.7 constant_dynamic-update-slice_fusion
  121.9 0.8 copy-done.1
  122.8 9.7 %shard_map.110 = (bf16[256,256]{1,0:T(8,128)(2,1)}, bf16[256,256]{1,0:T(8,128)(2,1)}, f32[256,256]{1,0:T(8,128)}, f32[256,256]{1,0:T(8,128)}, f32[256,256]{1,0:T...) custom-call(bf16[256,256]{1,0:T(8,128)(2,1)} %get-tuple-element.26.q_ref, bf16[256,5376]{1,0:T(8,128)(2,1)} %copy.14.cot_ref, ...), custom_call_target="tpu_custom_call" | custom-call | tf_op jit(solution)/shard_map/pallas_call | solution.py:108
  132.5 1.3 collective-permute-start.14
  133.8 1.3 collective-permute-start.13
  135.1 1.3 collective-permute-start.12
  136.4 1.3 collective-permute-start.11
  137.7 9.0 %shard_map.111.base_ref = bf16[5376,768]{1,0:T(8,128)(2,1)} custom-call(bf16[5376,256]{1,0:T(8,128)(2,1)} %bitcast.20, bf16[5376,256]{1,0:T(8,128)(2,1)} %bitcast.23, bf16[256,256]{1,0:T(8,128)(2,1)} %get-tuple-element.12.gq_ref, bf16[256,256]{1,0:T(8,128)(2,1)} %get-tuple-element.18.attn_ref), custom_call_target="tpu_custom_call" | custom-call | tf_op jit(solution)/shard_map/pallas_call | solution.py:137
  146.6 0.0 collective-permute-done.14
  146.7 0.0 collective-permute-done.13
  146.7 0.3 collective-permute-done.12
  146.9 0.0 collective-permute-done.11
  146.9 0.7 add_convert_fusion.gkv_ref
  147.7 6.3 %shard_map.112 = bf16[5376,768]{1,0:T(8,128)(2,1)} custom-call(bf16[5376,256]{1,0:T(8,128)(2,1)} %bitcast.21, bf16[256,256]{1,0:T(8,128)(2,1)} %add_convert_fusion.gkv_ref, bf16[5376,768]{1,0:T(8,128)(2,1)} %shard_map.111.base_ref), custom_call_target="tpu_custom_call", output_to_operand_aliasing={{}: (2, {})} | custom-call | tf_op jit(solution)/shard_map/pallas_call | solution.py:150
  154.0 0.0 reduce-scatter.2.cloned.1.call-update
  154.0 0.9 copy-done.2
  154.9 0.1 copy-done.6
  155.0 4.2 %convolution_convert_fusion = bf16[256,5376]{1,0:T(8,128)(2,1)S(1)} fusion(bf16[5376,768]{1,0:T(8,128)(2,1)} %all-gather.4.cloned.1.call-done, bf16[256,256]{1,0:T(8,128)(2,1)S(1)} %copy-done.2, bf16[256,256]{1,0:T(8,128)(2,1)S(1)} %copy-done.6), kind=kOutput, calls=%fused_computation | convolution fusion | flops 1411186688 | bytes 8519680 | tf_op jit(solution)/shard_map/dot_general | solution.py:165
  159.2 2.8 %copy.15 = bf16[256,5376]{0,1:T(8,128)(2,1)} copy(bf16[256,5376]{1,0:T(8,128)(2,1)S(1)} %convolution_convert_fusion) | data formatting | bytes 5505024 | tf_op jit(solution)/shard_map/convert_element_type | solution.py:205
  162.0 73.5 %all_to_all.5 = bf16[256,16,336]{0,2,1:T(8,128)(2,1)S(1)} all-to-all(bf16[256,16,336]{0,2,1:T(8,128)(2,1)} %bitcast.24), channel_id=1, replica_groups=mesh['ylo'=2,'x'=4,'core'=2,'z'=8,'yhi'=2] {'z','yhi'}, dimensions={1} | all-to-all | bytes 5505024 | tf_op jit(solution)/shard_map/all_to_all | solution.py:208
  235.5 1.1 reduce_sum.12
  236.6 22.0 %reduce-scatter.2.cloned.1.call-done = bf16[336,768]{1,0:T(8,128)(2,1)} async-done(((bf16[5376,768]{1,0:T(8,128)(2,1)}), bf16[336,768]{1,0:T(8,128)(2,1)}) %reduce-scatter.2.cloned.1.call-update) | async-done | bytes 516112 | tf_op jit(solution)/shard_map/reduce_scatter | solution.py:211
  258.6 1.8 slice_bitcast_fusion.1
  260.3 1.6 fusion.11
  (26 shorter events, 0.2 us)
Async XLA Ops:
  7.2 58.2 %all-gather.4.cloned.1.call-start = ((), (), s32[]{:S(2)}) async-start(), calls=%async_computation.2 | async-start | bytes 8773632 | tf_op jit(solution)/shard_map/all_gather | solution.py:189
  9.2 98.9 %all-gather.6.cloned.1.call-start = ((), (), s32[]{:S(2)}) async-start(), calls=%async_computation.4 | async-start | bytes 3096576 | tf_op jit(solution)/shard_map/all_gather | solution.py:187
  22.3 24.1 %copy-start.7 = (s32[2,9]{1,0:T(2,128)S(1)}, s32[2,9]{1,0:T(2,128)}, u32[]{:S(2)}) copy-start(s32[2,9]{1,0:T(2,128)} %param.13) | copy-start | bytes 220
  23.1 235.5 %reduce-scatter.2.cloned.1.call-start = ((), (), s32[]{:S(2)}) async-start(), calls=%async_computation.3 | async-start | bytes 8773632 | tf_op jit(solution)/shard_map/reduce_scatter | solution.py:211
  23.2 10.2 %collective-permute-start.3 = (bf16[256,672]{0,1:T(8,128)(2,1)S(1)}, bf16[256,672]{0,1:T(8,128)(2,1)S(1)}, u32[]{:S(2)}, u32[]{:S(2)}) collective-permute-start(bf16[256,672]{0,1:T(8,128)(2,1)S(1)} %get-tuple-element.20), channel_id=1, source_target_pairs={{0,2},{2,4},{4,6},{6,8},{8,10},{10,12},{12,14},{14,0},{1,3},{3,5},... | collective-permute-start | bytes 1032200 | tf_op jit(solution)/shard_map/ppermute | solution.py:28
  24.3 9.1 %collective-permute-start = (bf16[256,672]{0,1:T(8,128)(2,1)S(1)}, bf16[256,672]{0,1:T(8,128)(2,1)}, u32[]{:S(2)}, u32[]{:S(2)}) collective-permute-start(bf16[256,672]{0,1:T(8,128)(2,1)S(1)} %get-tuple-element.20), channel_id=1, source_target_pairs={{0,14},{2,0},{4,2},{6,4},{8,6},{10,8},{12,10},{14,12},{1,15},{3,1}... | collective-permute-start | bytes 1032200 | tf_op jit(solution)/shard_map/ppermute | solution.py:30
  33.4 9.4 %copy-start.3 = (bf16[256,672]{0,1:T(8,128)(2,1)}, bf16[256,672]{0,1:T(8,128)(2,1)S(1)}, u32[]{:S(2)}) copy-start(bf16[256,672]{0,1:T(8,128)(2,1)S(1)} %collective-permute-done.3) | copy-start | bytes 1032196
  33.4 9.4 %collective-permute-start.4 = (bf16[256,672]{0,1:T(8,128)(2,1)S(1)}, bf16[256,672]{0,1:T(8,128)(2,1)}, u32[]{:S(2)}, u32[]{:S(2)}) collective-permute-start(bf16[256,672]{0,1:T(8,128)(2,1)S(1)} %collective-permute-done.3), channel_id=1, source_target_pairs={{0,2},{2,4},{4,6},{6,8},{8,10},{10,12},{12,14},{14,0},{1,3},{3,5},... | collective-permute-start | bytes 1032200 | tf_op jit(solution)/shard_map/ppermute | solution.py:28
  33.4 9.6 %collective-permute-start.1 = (bf16[256,672]{0,1:T(8,128)(2,1)}, bf16[256,672]{0,1:T(8,128)(2,1)}, u32[]{:S(2)}, u32[]{:S(2)}) collective-permute-start(bf16[256,672]{0,1:T(8,128)(2,1)} %collective-permute-done), channel_id=1, source_target_pairs={{0,14},{2,0},{4,2},{6,4},{8,6},{10,8},{12,10},{14,12},{1,15},{3,1}... | collective-permute-start | bytes 1032200 | tf_op jit(solution)/shard_map/ppermute | solution.py:30
  42.8 8.8 %collective-permute-start.5 = (bf16[256,672]{0,1:T(8,128)(2,1)}, bf16[256,672]{0,1:T(8,128)(2,1)}, u32[]{:S(2)}, u32[]{:S(2)}) collective-permute-start(bf16[256,672]{0,1:T(8,128)(2,1)} %collective-permute-done.4), channel_id=1, source_target_pairs={{0,2},{2,4},{4,6},{6,8},{8,10},{10,12},{12,14},{14,0},{1,3},{3,5},... | collective-permute-start | bytes 1032200 | tf_op jit(solution)/shard_map/ppermute | solution.py:28
  43.0 19.3 %copy-start.4 = (bf16[256,672]{0,1:T(8,128)(2,1)S(1)}, bf16[256,672]{0,1:T(8,128)(2,1)}, u32[]{:S(2)}) copy-start(bf16[256,672]{0,1:T(8,128)(2,1)} %copy-done.3) | copy-start | bytes 1032196
  43.0 10.6 %collective-permute-start.2 = (bf16[256,672]{0,1:T(8,128)(2,1)}, bf16[256,672]{0,1:T(8,128)(2,1)S(1)}, u32[]{:S(2)}, u32[]{:S(2)}) collective-permute-start(bf16[256,672]{0,1:T(8,128)(2,1)} %collective-permute-done.1), channel_id=1, source_target_pairs={{0,14},{2,0},{4,2},{6,4},{8,6},{10,8},{12,10},{14,12},{1,15},{3,1}... | collective-permute-start | bytes 1032200 | tf_op jit(solution)/shard_map/ppermute | solution.py:30
  51.6 8.7 %collective-permute-start.6 = (bf16[256,672]{0,1:T(8,128)(2,1)}, bf16[256,672]{0,1:T(8,128)(2,1)S(1)}, u32[]{:S(2)}, u32[]{:S(2)}) collective-permute-start(bf16[256,672]{0,1:T(8,128)(2,1)} %collective-permute-done.5), channel_id=1, source_target_pairs={{0,2},{2,4},{4,6},{6,8},{8,10},{10,12},{12,14},{14,0},{1,3},{3,5},... | collective-permute-start | bytes 1032200 | tf_op jit(solution)/shard_map/ppermute | solution.py:28
  62.4 7.1 %copy-start = (bf16[256,5376]{0,1:T(8,128)(2,1)}, bf16[256,5376]{0,1:T(8,128)(2,1)S(1)}, u32[]{:S(2)}) copy-start(bf16[256,5376]{0,1:T(8,128)(2,1)S(1)} %constant_dynamic-update-slice_fusion.5) | copy-start | bytes 8257540
  69.5 51.6 %collective-permute-start.7 = (bf16[256,256]{1,0:T(8,128)(2,1)S(1)}, bf16[256,256]{1,0:T(8,128)(2,1)S(1)}, u32[]{:S(2)}, u32[]{:S(2)}) collective-permute-start(bf16[256,256]{1,0:T(8,128)(2,1)S(1)} %slice.45), channel_id=1, source_target_pairs={{0,64},{16,80},{32,96},{48,112},{64,128},{80,144},{96,160},{112,17... | collective-permute-start | bytes 393224 | tf_op jit(solution)/shard_map/ppermute | solution.py:45
  74.1 47.1 %collective-permute-start.8 = (bf16[256,256]{1,0:T(8,128)(2,1)S(1)}, bf16[256,256]{1,0:T(8,128)(2,1)S(1)}, u32[]{:S(2)}, u32[]{:S(2)}) collective-permute-start(bf16[256,256]{1,0:T(8,128)(2,1)S(1)} %slice.45), channel_id=1, source_target_pairs={{0,48},{16,64},{32,80},{48,96},{64,112},{80,128},{96,144},{112,160... | collective-permute-start | bytes 393224 | tf_op jit(solution)/shard_map/ppermute | solution.py:45
  112.7 8.5 %collective-permute-start.9 = (bf16[256,256]{1,0:T(8,128)(2,1)S(1)}, bf16[256,256]{1,0:T(8,128)(2,1)S(1)}, u32[]{:S(2)}, u32[]{:S(2)}) collective-permute-start(bf16[256,256]{1,0:T(8,128)(2,1)S(1)} %slice.45), channel_id=1, source_target_pairs={{0,32},{16,48},{32,64},{48,80},{64,96},{80,112},{96,128},{112,144}... | collective-permute-start | bytes 393224 | tf_op jit(solution)/shard_map/ppermute | solution.py:45
  116.1 5.1 %collective-permute-start.10 = (bf16[256,256]{1,0:T(8,128)(2,1)S(1)}, bf16[256,256]{1,0:T(8,128)(2,1)S(1)}, u32[]{:S(2)}, u32[]{:S(2)}) collective-permute-start(bf16[256,256]{1,0:T(8,128)(2,1)S(1)} %slice.45), channel_id=1, source_target_pairs={{0,16},{16,32},{32,48},{48,64},{64,80},{80,96},{96,112},{112,128},... | collective-permute-start | bytes 393224 | tf_op jit(solution)/shard_map/ppermute | solution.py:45
  121.9 0.8 copy-start.1
  132.5 14.2 %collective-permute-start.14 = (f32[256,256]{1,0:T(8,128)}, f32[256,256]{1,0:T(8,128)S(1)}, u32[]{:S(2)}, u32[]{:S(2)}) collective-permute-start(f32[256,256]{1,0:T(8,128)} %get-tuple-element.17), channel_id=1, source_target_pairs={{64,0},{80,16},{96,32},{112,48},{128,64},{144,80},{160,96},{176,11... | collective-permute-start | bytes 786440 | tf_op jit(solution)/shard_map/ppermute | solution.py:45
  133.8 12.9 %collective-permute-start.13 = (f32[256,256]{1,0:T(8,128)}, f32[256,256]{1,0:T(8,128)S(1)}, u32[]{:S(2)}, u32[]{:S(2)}) collective-permute-start(f32[256,256]{1,0:T(8,128)} %get-tuple-element.16), channel_id=1, source_target_pairs={{48,0},{64,16},{80,32},{96,48},{112,64},{128,80},{144,96},{160,112... | collective-permute-start | bytes 786440 | tf_op jit(solution)/shard_map/ppermute | solution.py:45
  135.1 11.9 %collective-permute-start.12 = (f32[256,256]{1,0:T(8,128)}, f32[256,256]{1,0:T(8,128)S(1)}, u32[]{:S(2)}, u32[]{:S(2)}) collective-permute-start(f32[256,256]{1,0:T(8,128)} %get-tuple-element.15), channel_id=1, source_target_pairs={{32,0},{48,16},{64,32},{80,48},{96,64},{112,80},{128,96},{144,112}... | collective-permute-start | bytes 786440 | tf_op jit(solution)/shard_map/ppermute | solution.py:45
  136.4 10.6 %collective-permute-start.11 = (f32[256,256]{1,0:T(8,128)}, f32[256,256]{1,0:T(8,128)S(1)}, u32[]{:S(2)}, u32[]{:S(2)}) collective-permute-start(f32[256,256]{1,0:T(8,128)} %get-tuple-element.14), channel_id=1, source_target_pairs={{16,0},{32,16},{48,32},{64,48},{80,64},{96,80},{112,96},{128,112},... | collective-permute-start | bytes 786440 | tf_op jit(solution)/shard_map/ppermute | solution.py:45
  137.7 9.3 %copy-start.5 = (f32[256,256]{1,0:T(8,128)S(1)}, f32[256,256]{1,0:T(8,128)}, u32[]{:S(2)}) copy-start(f32[256,256]{1,0:T(8,128)} %get-tuple-element.13) | copy-start | bytes 786436
  154.0 0.9 copy-start.2
  154.0 1.0 copy-start.6
Sparse Core Ops, SparseCore 0:
  9.8 55.4 all-gather.3
  67.1 40.9 all-gather.5
  154.2 104.3 reduce-scatter.1

commit v12 on v10

--- a/solution.py
+++ b/solution.py
@@ -129,7 +129,7 @@
     out_ref[...] = _nn(tok_ref[...], gkv_ref[...]).astype(out_ref.dtype)
 
 
-def weight_terms(tokens_t, cot_t, grad_q, grad_kv, attn, block=768):
+def weight_terms(tokens_t, cot_t, grad_q, grad_kv, attn, block=1344):
     feats, rows = tokens_t.shape
     n_q, n_kv, n_attn = grad_q.shape[1], grad_kv.shape[1], attn.shape[1]
     width = n_q + n_kv + n_attn

time: 254 us -> 252 us (level)
  Pallas kernels: 21.9 us -> 18.4 us
  transfers between devices with their start and end apart: 18 -> 18, of which waited for: 7 -> 8; matrix products, arithmetic and copies ran while one was open for 9% -> 9% of each run, Pallas kernels for 4% -> 3%
where the time goes in v12:
time: 252 us; the launch traced here: 251 us
  blocking collectives  85 us (34%)
  waiting for transfers between devices  73.3 us (29%)
  starting transfers between devices  28.7 us (11%)
  Pallas kernels  18.4 us (7%)
  local copies, waits for them, and re-layouts  14.6 us (6%)
  between operations  14 us (6%)
  matrix products  12.5 us (5%)
  other arithmetic  4.85 us (2%)
    all_to_all x1, blocking collectives, shards(): lax.all_to_all(token_term.reshape(tok_rows, n_tp, cols), TP, 1, 1, tiled=...  73.1 us
    all_gather x1, waiting for transfers between devices, shards(): full_cot = lax.all_gather(pair[1], 'z', axis=1, tiled=True)  25 us
    ppermute x4, waiting for transfers between devices, ring_gather(): lax.ppermute(right[-1], axis, [(i, (i + 1) % size) for i in range(size)])  24.3 us
    reduce_scatter x1, waiting for transfers between devices, shards(): lax.psum_scatter(weight_parts, SEQ, scatter_dimension=0, tiled=True)  19.3 us
    ppermute x8, starting transfers between devices, from_behind(): return lax.ppermute(block, axis, route)  18.7 us
    all_gather x1, blocking collectives, shards(): pair = lax.all_gather(pair, 'yhi', axis=2, tiled=True)  12 us
    ppermute x3, starting transfers between devices, ring_gather(): lax.ppermute(left[-1], axis, [(i, (i - 1) % size) for i in range(size)])  8.75 us
    pallas_call x1, Pallas kernels, weight_terms(): pl.pallas_call(weight_terms_kernel, grid=(feats // block,), in_specs=[pl....  7.05 us
  transfers between devices with their start and end apart: 18, of which 8 were waited for; matrix products, arithmetic and copies ran while one was open for 9% of the time, Pallas kernels for 3%

profile of v12, /device:TPU:128, one launch (start us, length us, event | category | flops | bytes accessed | tf_op | source)
XLA Modules:
  0.0 251.3 jit_solution(14803180775049961343)
XLA Ops:
  7.2 0.0 all-gather.4.cloned.1.call-start
  7.2 2.0 pad_maximum_fusion
  9.2 0.0 all-gather.4.cloned.1.call-update
  9.2 0.0 all-gather.6.cloned.1.call-start
  9.3 1.0 pad_maximum_fusion.1
  10.3 12.0 %all_gather.9 = bf16[2,256,672]{1,2,0:T(8,128)(2,1)S(1)} all-gather(bf16[2,256,336]{1,2,0:T(8,128)(2,1)S(1)} %pad_maximum_fusion.1), channel_id=1, replica_groups=mesh['ylo'=2,'x'=4,'core'=2,'z'=8,'yhi'=2] {'yhi'}, dimensions={2}, use_global_device_ids=true | all-gather | bytes 1032192 | tf_op jit(solution)/shard_map/all_gather | solution.py:184
  22.3 0.8 fusion.18
  23.1 0.0 all-gather.6.cloned.1.call-update
  23.1 0.0 reduce-scatter.2.cloned.1.call-start
  23.1 1.1 collective-permute-start.3
  24.2 2.2 collective-permute-start
  26.5 7.0 %collective-permute-done.3 = bf16[256,672]{0,1:T(8,128)(2,1)} collective-permute-done((bf16[256,672]{0,1:T(8,128)(2,1)S(1)}, bf16[256,672]{0,1:T(8,128)(2,1)}, u32[]{:S(2)}, u32[]{:S(2)}) %collective-permute-start.3) | collective-permute-done | bytes 344096 | tf_op jit(solution)/shard_map/ppermute | solution.py:28
  33.5 0.0 collective-permute-start.4
  33.5 0.0 collective-permute-done
  33.5 3.2 %collective-permute-start.1 = (bf16[256,672]{0,1:T(8,128)(2,1)}, bf16[256,672]{0,1:T(8,128)(2,1)}, u32[]{:S(2)}, u32[]{:S(2)}) collective-permute-start(bf16[256,672]{0,1:T(8,128)(2,1)} %collective-permute-done), channel_id=1, source_target_pairs={{0,14},{2,0},{4,2},{6,4},{8,6},{10,8},{12,10},{14,12},{1,15},{3,1}... | collective-permute-start | bytes 1032200 | tf_op jit(solution)/shard_map/ppermute | solution.py:30
  36.7 0.2 broadcast_in_dim.6
  36.9 6.1 %collective-permute-done.4 = bf16[256,672]{0,1:T(8,128)(2,1)} collective-permute-done((bf16[256,672]{0,1:T(8,128)(2,1)}, bf16[256,672]{0,1:T(8,128)(2,1)}, u32[]{:S(2)}, u32[]{:S(2)}) %collective-permute-start.4) | collective-permute-done | bytes 344096 | tf_op jit(solution)/shard_map/ppermute | solution.py:28
  43.1 0.0 collective-permute-start.5
  43.1 0.0 collective-permute-done.1
  43.1 3.3 %collective-permute-start.2 = (bf16[256,672]{0,1:T(8,128)(2,1)}, bf16[256,672]{0,1:T(8,128)(2,1)S(1)}, u32[]{:S(2)}, u32[]{:S(2)}) collective-permute-start(bf16[256,672]{0,1:T(8,128)(2,1)} %collective-permute-done.1), channel_id=1, source_target_pairs={{0,14},{2,0},{4,2},{6,4},{8,6},{10,8},{12,10},{14,12},{1,15},{3,1}... | collective-permute-start | bytes 1032200 | tf_op jit(solution)/shard_map/ppermute | solution.py:30
  46.4 0.1 broadcast_bitcast_fusion
  46.5 0.6 copy.16
  47.1 4.7 %collective-permute-done.5 = bf16[256,672]{0,1:T(8,128)(2,1)S(1)} collective-permute-done((bf16[256,672]{0,1:T(8,128)(2,1)}, bf16[256,672]{0,1:T(8,128)(2,1)S(1)}, u32[]{:S(2)}, u32[]{:S(2)}) %collective-permute-start.5) | collective-permute-done | bytes 344096 | tf_op jit(solution)/shard_map/ppermute | solution.py:28
  51.8 0.0 collective-permute-start.6
  51.8 1.0 constant_dynamic-update-slice_fusion.11
  52.9 1.0 constant_dynamic-update-slice_fusion.10
  53.9 0.0 collective-permute-done.2
  53.9 6.4 %collective-permute-done.6 = bf16[256,672]{0,1:T(8,128)(2,1)S(1)} collective-permute-done((bf16[256,672]{0,1:T(8,128)(2,1)S(1)}, bf16[256,672]{0,1:T(8,128)(2,1)S(1)}, u32[]{:S(2)}, u32[]{:S(2)}) %collective-permute-start.6) | collective-permute-done | bytes 344096 | tf_op jit(solution)/shard_map/ppermute | solution.py:28
  60.4 1.0 constant_dynamic-update-slice_fusion.6
  61.4 1.0 constant_dynamic-update-slice_fusion.5
  62.4 2.9 %all-gather.4.cloned.1.call-done = bf16[5376,768]{1,0:T(8,128)(2,1)} async-done(((bf16[336,768]{1,0:T(8,128)(2,1)}), bf16[5376,768]{1,0:T(8,128)(2,1)}) %all-gather.4.cloned.1.call-update) | async-done | bytes 8257552 | tf_op jit(solution)/shard_map/all_gather | solution.py:188
  65.3 4.2 %fusion.6 = bf16[256,512]{1,0:T(8,128)(2,1)S(1)} fusion(bf16[256,5376]{0,1:T(8,128)(2,1)S(1)} %constant_dynamic-update-slice_fusion.5, bf16[5376,768]{1,0:T(8,128)(2,1)} %all-gather.4.cloned.1.call-done), kind=kOutput, calls=%fused_computation.7 | convolution fusion | flops 1409417216 | bytes 8519680 | tf_op jit(solution)/shard_map/dot_general | solution.py:193
  69.5 4.5 %collective-permute-start.7 = (bf16[256,256]{1,0:T(8,128)(2,1)S(1)}, bf16[256,256]{1,0:T(8,128)(2,1)S(1)}, u32[]{:S(2)}, u32[]{:S(2)}) collective-permute-start(bf16[256,256]{1,0:T(8,128)(2,1)S(1)} %slice.45), channel_id=1, source_target_pairs={{0,64},{16,80},{32,96},{48,112},{64,128},{80,144},{96,160},{112,17... | collective-permute-start | bytes 393224 | tf_op jit(solution)/shard_map/ppermute | solution.py:45
  74.1 2.3 collective-permute-start.8
  76.4 2.8 %collective-permute-start.9 = (bf16[256,256]{1,0:T(8,128)(2,1)S(1)}, bf16[256,256]{1,0:T(8,128)(2,1)S(1)}, u32[]{:S(2)}, u32[]{:S(2)}) collective-permute-start(bf16[256,256]{1,0:T(8,128)(2,1)S(1)} %slice.45), channel_id=1, source_target_pairs={{0,32},{16,48},{32,64},{48,80},{64,96},{80,112},{96,128},{112,144}... | collective-permute-start | bytes 393224 | tf_op jit(solution)/shard_map/ppermute | solution.py:45
  79.3 3.9 %collective-permute-start.10 = (bf16[256,256]{1,0:T(8,128)(2,1)S(1)}, bf16[256,256]{1,0:T(8,128)(2,1)S(1)}, u32[]{:S(2)}, u32[]{:S(2)}) collective-permute-start(bf16[256,256]{1,0:T(8,128)(2,1)S(1)} %slice.45), channel_id=1, source_target_pairs={{0,16},{16,32},{32,48},{48,64},{64,80},{80,96},{96,112},{112,128},... | collective-permute-start | bytes 393224 | tf_op jit(solution)/shard_map/ppermute | solution.py:45
  83.1 25.0 %all-gather.6.cloned.1.call-done = bf16[1,256,5376]{1,2,0:T(8,128)(2,1)} async-done(((bf16[1,256,672]{1,2,0:T(8,128)(2,1)}), bf16[1,256,5376]{1,2,0:T(8,128)(2,1)}) %all-gather.6.cloned.1.call-update) | async-done | bytes 2752528 | tf_op jit(solution)/shard_map/all_gather | solution.py:186
  108.2 4.2 %fusion.9.d_ref = bf16[256,256]{1,0:T(8,128)(2,1)} fusion(bf16[5376,768]{1,0:T(8,128)(2,1)} %all-gather.4.cloned.1.call-done, bf16[1,256,5376]{1,2,0:T(8,128)(2,1)} %all-gather.6.cloned.1.call-done), kind=kOutput, calls=%fused_computation.8 | convolution fusion | flops 704708608 | bytes 5636096 | tf_op jit(solution)/shard_map/dot_general | solution.py:190
  112.3 0.0 collective-permute-done.7
  112.4 0.0 collective-permute-done.8
  112.4 0.0 collective-permute-done.9
  112.4 0.0 collective-permute-done.10
  112.4 0.7 constant_dynamic-update-slice_fusion
  113.1 0.9 copy-done.1
  114.0 6.6 %shard_map.110 = (bf16[256,256]{1,0:T(8,128)(2,1)}, bf16[256,256]{1,0:T(8,128)(2,1)}, f32[256,256]{1,0:T(8,128)}, f32[256,256]{1,0:T(8,128)}, f32[256,256]{1,0:T...) custom-call(bf16[256,256]{1,0:T(8,128)(2,1)} %get-tuple-element.26.q_ref, bf16[256,256]{1,0:T(8,128)(2,1)} %fusion.9.d_ref, ...), custom_call_target="tpu_custom_call" | custom-call | tf_op jit(solution)/shard_map/pallas_call | solution.py:107
  120.6 1.3 collective-permute-start.14
  121.9 1.3 collective-permute-start.13
  123.2 1.3 collective-permute-start.12
  124.5 1.3 collective-permute-start.11
  125.8 7.0 %shard_map.111.base_ref = bf16[5376,768]{1,0:T(8,128)(2,1)} custom-call(bf16[5376,256]{1,0:T(8,128)(2,1)} %bitcast.24, bf16[5376,256]{1,0:T(8,128)(2,1)} %bitcast.27, bf16[256,256]{1,0:T(8,128)(2,1)} %get-tuple-element.12.gq_ref, bf16[256,256]{1,0:T(8,128)(2,1)} %get-tuple-element.18.attn_ref), custom_call_target="tpu_custom_call" | custom-call | tf_op jit(solution)/shard_map/pallas_call | solution.py:136
  132.9 1.6 collective-permute-done.12
  134.5 0.0 collective-permute-done.11
  134.5 0.7 add_convert_fusion.gkv_ref
  135.2 4.8 %shard_map.112 = bf16[5376,768]{1,0:T(8,128)(2,1)} custom-call(bf16[5376,256]{1,0:T(8,128)(2,1)} %bitcast.25, bf16[256,256]{1,0:T(8,128)(2,1)} %add_convert_fusion.gkv_ref, bf16[5376,768]{1,0:T(8,128)(2,1)} %shard_map.111.base_ref), custom_call_target="tpu_custom_call", output_to_operand_aliasing={{}: (2, {})} | custom-call | tf_op jit(solution)/shard_map/pallas_call | solution.py:149
  140.0 0.0 reduce-scatter.2.cloned.1.call-update
  140.0 0.9 copy-done.2
  140.9 0.1 copy-done.4
  141.0 4.2 %convolution_convert_fusion = bf16[256,5376]{1,0:T(8,128)(2,1)S(1)} fusion(bf16[5376,768]{1,0:T(8,128)(2,1)} %all-gather.4.cloned.1.call-done, bf16[256,256]{1,0:T(8,128)(2,1)S(1)} %copy-done.2, bf16[256,256]{1,0:T(8,128)(2,1)S(1)} %copy-done.4), kind=kOutput, calls=%fused_computation | convolution fusion | flops 1411186688 | bytes 8519680 | tf_op jit(solution)/shard_map/dot_general | solution.py:164
  145.2 2.8 %copy.13 = bf16[256,5376]{0,1:T(8,128)(2,1)} copy(bf16[256,5376]{1,0:T(8,128)(2,1)S(1)} %convolution_convert_fusion) | data formatting | bytes 5505024 | tf_op jit(solution)/shard_map/convert_element_type | solution.py:207
  148.0 73.1 %all_to_all.5 = bf16[256,16,336]{0,2,1:T(8,128)(2,1)S(1)} all-to-all(bf16[256,16,336]{0,2,1:T(8,128)(2,1)} %bitcast.26), channel_id=1, replica_groups=mesh['ylo'=2,'x'=4,'core'=2,'z'=8,'yhi'=2] {'z','yhi'}, dimensions={1} | all-to-all | bytes 5505024 | tf_op jit(solution)/shard_map/all_to_all | solution.py:210
  221.0 1.1 reduce_sum.12
  222.1 19.3 %reduce-scatter.2.cloned.1.call-done = bf16[336,768]{1,0:T(8,128)(2,1)} async-done(((bf16[5376,768]{1,0:T(8,128)(2,1)}), bf16[336,768]{1,0:T(8,128)(2,1)}) %reduce-scatter.2.cloned.1.call-update) | async-done | bytes 516112 | tf_op jit(solution)/shard_map/reduce_scatter | solution.py:213
  241.4 1.8 slice_bitcast_fusion.1
  243.2 1.6 fusion.19
  (21 shorter events, 0.2 us)
Async XLA Ops:
  7.2 58.2 %all-gather.4.cloned.1.call-start = ((), (), s32[]{:S(2)}) async-start(), calls=%async_computation.2 | async-start | bytes 8773632 | tf_op jit(solution)/shard_map/all_gather | solution.py:188
  9.2 98.9 %all-gather.6.cloned.1.call-start = ((), (), s32[]{:S(2)}) async-start(), calls=%async_computation.4 | async-start | bytes 3096576 | tf_op jit(solution)/shard_map/all_gather | solution.py:186
  22.3 20.8 %copy-start.5 = (s32[2,9]{1,0:T(2,128)S(1)}, s32[2,9]{1,0:T(2,128)}, u32[]{:S(2)}) copy-start(s32[2,9]{1,0:T(2,128)} %param.13) | copy-start | bytes 220
  23.1 218.3 %reduce-scatter.2.cloned.1.call-start = ((), (), s32[]{:S(2)}) async-start(), calls=%async_computation.3 | async-start | bytes 8773632 | tf_op jit(solution)/shard_map/reduce_scatter | solution.py:213
  23.1 10.3 %collective-permute-start.3 = (bf16[256,672]{0,1:T(8,128)(2,1)S(1)}, bf16[256,672]{0,1:T(8,128)(2,1)}, u32[]{:S(2)}, u32[]{:S(2)}) collective-permute-start(bf16[256,672]{0,1:T(8,128)(2,1)S(1)} %get-tuple-element.20), channel_id=1, source_target_pairs={{0,2},{2,4},{4,6},{6,8},{8,10},{10,12},{12,14},{14,0},{1,3},{3,5},... | collective-permute-start | bytes 1032200 | tf_op jit(solution)/shard_map/ppermute | solution.py:28
  24.2 9.2 %collective-permute-start = (bf16[256,672]{0,1:T(8,128)(2,1)S(1)}, bf16[256,672]{0,1:T(8,128)(2,1)}, u32[]{:S(2)}, u32[]{:S(2)}) collective-permute-start(bf16[256,672]{0,1:T(8,128)(2,1)S(1)} %get-tuple-element.20), channel_id=1, source_target_pairs={{0,14},{2,0},{4,2},{6,4},{8,6},{10,8},{12,10},{14,12},{1,15},{3,1}... | collective-permute-start | bytes 1032200 | tf_op jit(solution)/shard_map/ppermute | solution.py:30
  33.5 9.6 %collective-permute-start.4 = (bf16[256,672]{0,1:T(8,128)(2,1)}, bf16[256,672]{0,1:T(8,128)(2,1)}, u32[]{:S(2)}, u32[]{:S(2)}) collective-permute-start(bf16[256,672]{0,1:T(8,128)(2,1)} %collective-permute-done.3), channel_id=1, source_target_pairs={{0,2},{2,4},{4,6},{6,8},{8,10},{10,12},{12,14},{14,0},{1,3},{3,5},... | collective-permute-start | bytes 1032200 | tf_op jit(solution)/shard_map/ppermute | solution.py:28
  33.5 9.6 %collective-permute-start.1 = (bf16[256,672]{0,1:T(8,128)(2,1)}, bf16[256,672]{0,1:T(8,128)(2,1)}, u32[]{:S(2)}, u32[]{:S(2)}) collective-permute-start(bf16[256,672]{0,1:T(8,128)(2,1)} %collective-permute-done), channel_id=1, source_target_pairs={{0,14},{2,0},{4,2},{6,4},{8,6},{10,8},{12,10},{14,12},{1,15},{3,1}... | collective-permute-start | bytes 1032200 | tf_op jit(solution)/shard_map/ppermute | solution.py:30
  43.1 8.8 %collective-permute-start.5 = (bf16[256,672]{0,1:T(8,128)(2,1)}, bf16[256,672]{0,1:T(8,128)(2,1)S(1)}, u32[]{:S(2)}, u32[]{:S(2)}) collective-permute-start(bf16[256,672]{0,1:T(8,128)(2,1)} %collective-permute-done.4), channel_id=1, source_target_pairs={{0,2},{2,4},{4,6},{6,8},{8,10},{10,12},{12,14},{14,0},{1,3},{3,5},... | collective-permute-start | bytes 1032200 | tf_op jit(solution)/shard_map/ppermute | solution.py:28
  43.1 10.8 %collective-permute-start.2 = (bf16[256,672]{0,1:T(8,128)(2,1)}, bf16[256,672]{0,1:T(8,128)(2,1)S(1)}, u32[]{:S(2)}, u32[]{:S(2)}) collective-permute-start(bf16[256,672]{0,1:T(8,128)(2,1)} %collective-permute-done.1), channel_id=1, source_target_pairs={{0,14},{2,0},{4,2},{6,4},{8,6},{10,8},{12,10},{14,12},{1,15},{3,1}... | collective-permute-start | bytes 1032200 | tf_op jit(solution)/shard_map/ppermute | solution.py:30
  51.8 8.5 %collective-permute-start.6 = (bf16[256,672]{0,1:T(8,128)(2,1)S(1)}, bf16[256,672]{0,1:T(8,128)(2,1)S(1)}, u32[]{:S(2)}, u32[]{:S(2)}) collective-permute-start(bf16[256,672]{0,1:T(8,128)(2,1)S(1)} %collective-permute-done.5), channel_id=1, source_target_pairs={{0,2},{2,4},{4,6},{6,8},{8,10},{10,12},{12,14},{14,0},{1,3},{3,5},... | collective-permute-start | bytes 1032200 | tf_op jit(solution)/shard_map/ppermute | solution.py:28
  62.4 7.1 %copy-start = (bf16[256,5376]{0,1:T(8,128)(2,1)}, bf16[256,5376]{0,1:T(8,128)(2,1)S(1)}, u32[]{:S(2)}) copy-start(bf16[256,5376]{0,1:T(8,128)(2,1)S(1)} %constant_dynamic-update-slice_fusion.5) | copy-start | bytes 8257540
  69.5 42.8 %collective-permute-start.7 = (bf16[256,256]{1,0:T(8,128)(2,1)S(1)}, bf16[256,256]{1,0:T(8,128)(2,1)S(1)}, u32[]{:S(2)}, u32[]{:S(2)}) collective-permute-start(bf16[256,256]{1,0:T(8,128)(2,1)S(1)} %slice.45), channel_id=1, source_target_pairs={{0,64},{16,80},{32,96},{48,112},{64,128},{80,144},{96,160},{112,17... | collective-permute-start | bytes 393224 | tf_op jit(solution)/shard_map/ppermute | solution.py:45
  74.1 38.3 %collective-permute-start.8 = (bf16[256,256]{1,0:T(8,128)(2,1)S(1)}, bf16[256,256]{1,0:T(8,128)(2,1)S(1)}, u32[]{:S(2)}, u32[]{:S(2)}) collective-permute-start(bf16[256,256]{1,0:T(8,128)(2,1)S(1)} %slice.45), channel_id=1, source_target_pairs={{0,48},{16,64},{32,80},{48,96},{64,112},{80,128},{96,144},{112,160... | collective-permute-start | bytes 393224 | tf_op jit(solution)/shard_map/ppermute | solution.py:45
  76.4 36.0 %collective-permute-start.9 = (bf16[256,256]{1,0:T(8,128)(2,1)S(1)}, bf16[256,256]{1,0:T(8,128)(2,1)S(1)}, u32[]{:S(2)}, u32[]{:S(2)}) collective-permute-start(bf16[256,256]{1,0:T(8,128)(2,1)S(1)} %slice.45), channel_id=1, source_target_pairs={{0,32},{16,48},{32,64},{48,80},{64,96},{80,112},{96,128},{112,144}... | collective-permute-start | bytes 393224 | tf_op jit(solution)/shard_map/ppermute | solution.py:45
  79.3 33.2 %collective-permute-start.10 = (bf16[256,256]{1,0:T(8,128)(2,1)S(1)}, bf16[256,256]{1,0:T(8,128)(2,1)S(1)}, u32[]{:S(2)}, u32[]{:S(2)}) collective-permute-start(bf16[256,256]{1,0:T(8,128)(2,1)S(1)} %slice.45), channel_id=1, source_target_pairs={{0,16},{16,32},{32,48},{48,64},{64,80},{80,96},{96,112},{112,128},... | collective-permute-start | bytes 393224 | tf_op jit(solution)/shard_map/ppermute | solution.py:45
  113.1 0.9 copy-start.1
  120.6 12.2 %collective-permute-start.14 = (f32[256,256]{1,0:T(8,128)}, f32[256,256]{1,0:T(8,128)S(1)}, u32[]{:S(2)}, u32[]{:S(2)}) collective-permute-start(f32[256,256]{1,0:T(8,128)} %get-tuple-element.17), channel_id=1, source_target_pairs={{64,0},{80,16},{96,32},{112,48},{128,64},{144,80},{160,96},{176,11... | collective-permute-start | bytes 786440 | tf_op jit(solution)/shard_map/ppermute | solution.py:45
  121.9 11.0 %collective-permute-start.13 = (f32[256,256]{1,0:T(8,128)}, f32[256,256]{1,0:T(8,128)S(1)}, u32[]{:S(2)}, u32[]{:S(2)}) collective-permute-start(f32[256,256]{1,0:T(8,128)} %get-tuple-element.16), channel_id=1, source_target_pairs={{48,0},{64,16},{80,32},{96,48},{112,64},{128,80},{144,96},{160,112... | collective-permute-start | bytes 786440 | tf_op jit(solution)/shard_map/ppermute | solution.py:45
  123.2 11.3 %collective-permute-start.12 = (f32[256,256]{1,0:T(8,128)}, f32[256,256]{1,0:T(8,128)S(1)}, u32[]{:S(2)}, u32[]{:S(2)}) collective-permute-start(f32[256,256]{1,0:T(8,128)} %get-tuple-element.15), channel_id=1, source_target_pairs={{32,0},{48,16},{64,32},{80,48},{96,64},{112,80},{128,96},{144,112}... | collective-permute-start | bytes 786440 | tf_op jit(solution)/shard_map/ppermute | solution.py:45
  124.5 10.0 %collective-permute-start.11 = (f32[256,256]{1,0:T(8,128)}, f32[256,256]{1,0:T(8,128)S(1)}, u32[]{:S(2)}, u32[]{:S(2)}) collective-permute-start(f32[256,256]{1,0:T(8,128)} %get-tuple-element.14), channel_id=1, source_target_pairs={{16,0},{32,16},{48,32},{64,48},{80,64},{96,80},{112,96},{128,112},... | collective-permute-start | bytes 786440 | tf_op jit(solution)/shard_map/ppermute | solution.py:45
  125.8 8.7 %copy-start.3 = (f32[256,256]{1,0:T(8,128)S(1)}, f32[256,256]{1,0:T(8,128)}, u32[]{:S(2)}) copy-start(f32[256,256]{1,0:T(8,128)} %get-tuple-element.13) | copy-start | bytes 786436
  140.0 0.9 copy-start.2
  140.0 1.0 copy-start.4
Sparse Core Ops, SparseCore 0:
  9.8 55.4 all-gather.3
  67.1 40.9 all-gather.5
  140.1 101.2 reduce-scatter.1
